TPU v7x, 128 devices: a whole 4x4x4 slice. The times are simulated.
128 devices in a mesh: phase: 8 (over y_hi, z), row: 16 (over x, y_lo, core).
Axes of the slice: x: 4, y: 4 (y_hi: 2, y_lo: 2; y = y_hi * 2 + y_lo), z: 4, core: 2. Of those that a mesh axis runs over, the one named last changes fastest.
Arguments:
- frames: float32 [2, 64, 256, 256], P(None, 'phase', 'row'), may hold values from -50 to 50
- auxiliary: float32 [2, 64, 256, 256], P(None, 'phase', 'row'), may hold values from -6 to 6
- scaled_dual: float32 [2, 64, 256, 256], P(None, 'phase', 'row'), may hold values from -3 to 3
- coil_maps: float32 [16, 2, 256, 256], P(None, None, 'row'), may hold values from -5 to 5
- measured: float32 [16, 2, 64, 256, 256], P(None, None, 'phase', 'row'), may hold values from -6 to 6
- sampling: int32 [64, 256], P('phase'), may hold values 0 or 1
Outputs:
- new_frames: float32 [2, 64, 256, 256], P(None, 'phase', 'row')
- new_aux: float32 [2, 64, 256, 256], P(None, 'phase', 'row')
- new_dual: float32 [2, 64, 256, 256], P(None, 'phase', 'row')
- residual_norms: float32 [2], replicated
All inputs are finite; a program needn't handle non-finite values. No bound on the sum of `sampling` on one device may be relied on, other than what follows from the above.
Results may differ from a plain program's by a relative error of at most 0.003.
Values sent between devices are 32-bit elements; how exact they have to be, the bound alone decides.
No kernel may reach another device: no remote copies, remote signals or barrier semaphores. Data moves between devices by JAX's collectives and lax.ppermute only.
A program may use at most 256 MiB of HBM per device.

v0:
```python
import math

import jax
import jax.numpy as jnp
from jax import lax
from jax.sharding import PartitionSpec as P

CG_STEPS = 2


EXACT = lax.Precision.HIGHEST
PENALTY = 0.5
DAMPING = 0.1
THRESHOLD = 1.0


def padded_2(value, sides, width):
    for axis, dim in sides:
        count, length = (lax.axis_size(axis), value.shape[dim])
        up = [(i, (i + 1) % count) for i in range(count)]
        down = [(j, i) for i, j in up]
        last = lax.slice_in_dim(value, length - width, length, axis=dim)
        initial = lax.slice_in_dim(value, 0, width, axis=dim)
        before = lax.ppermute(last, axis, up)
        after = lax.ppermute(initial, axis, down)
        value = jnp.concatenate([before, value, after], axis=dim)
    return value


def from_behind(value, axis, steps):
    count = lax.axis_size(axis)
    pairs = [(source, (source + steps) % count) for source in range(count)]
    return lax.ppermute(value, axis, pairs)


def tables(count):
    indices = jnp.arange(count, dtype=jnp.int32)
    angles = (indices[:, None] * indices[None, :] % count).astype(jnp.float32) * (
        2.0 * math.pi / count
    )
    return (jnp.cos(angles) / math.sqrt(count), jnp.sin(angles) / math.sqrt(count))


def coil_images(maps, values):
    maps_real = maps[:, 0, None]
    maps_imag = maps[:, 1, None]
    return (
        maps_real * values[0] - maps_imag * values[1],
        maps_real * values[1] + maps_imag * values[0],
    )


def coil_combine(maps, real_part, imag_part):
    maps_real = maps[:, 0, None]
    maps_imag = maps[:, 1, None]
    total_real = jnp.sum(maps_real * real_part + maps_imag * imag_part, 0)
    total_imag = jnp.sum(maps_real * imag_part - maps_imag * real_part, 0)
    return jnp.stack([total_real, total_imag], 0)


def second_diff(values):
    padded = padded_2(values, (("phase", 1),), 1)
    return 2.0 * values - padded[:, 2:] - padded[:, :-2]


def residual_energy(residual):
    return lax.psum(jnp.sum(residual * residual), ("phase", "row"))


def conjugate(estimate, rhs, gram_fn):

    def apply_normal(values):
        return gram_fn(values) + PENALTY * second_diff(values) + DAMPING * values

    residual = rhs - apply_normal(estimate)
    direction = residual
    energy = residual_energy(residual)
    for iteration in range(CG_STEPS):
        image_dir = apply_normal(direction)
        curvature = lax.psum(jnp.sum(direction * image_dir), ("phase", "row"))
        step_size = energy / curvature
        estimate = estimate + step_size * direction
        residual = residual - step_size * image_dir
        if iteration + 1 < CG_STEPS:
            fresh = residual_energy(residual)
            direction = residual + fresh / energy * direction
            energy = fresh
    return estimate


def local(frames, auxiliary, scaled_dual, coil_maps, measured, sampling):
    groups = lax.axis_size("row")
    coil_count = coil_maps.shape[0]
    phases = frames.shape[1]
    row_count = frames.shape[2]
    col_count = frames.shape[3]
    row_total = row_count * groups
    narrow = col_count // groups
    cosine, sine_table = tables(row_total)
    weight = sampling.astype(jnp.float32)[:, None, :]

    def apply_table(values, table):
        return jnp.dot(values, table, precision=EXACT)

    def forward(real_part, imag_part):
        return (
            apply_table(real_part, cosine) + apply_table(imag_part, sine_table),
            apply_table(imag_part, cosine) - apply_table(real_part, sine_table),
        )

    def inverse(real_part, imag_part):
        return (
            apply_table(real_part, cosine) - apply_table(imag_part, sine_table),
            apply_table(imag_part, cosine) + apply_table(real_part, sine_table),
        )

    def filtered(real_part, imag_part):
        spec_real, spec_imag = forward(real_part, imag_part)
        return inverse(spec_real * weight, spec_imag * weight)

    def to_columns_layout(values):
        reshaped = values.reshape(values.shape[:-2] + (row_count, groups, narrow))
        return jnp.moveaxis(reshaped, -3, -1)

    difference = auxiliary - scaled_dual
    previous = from_behind(difference[:, -1:], "phase", 1)
    earlier = jnp.concatenate([previous, difference[:, :-1]], 1)
    rhs_penalty = PENALTY * (earlier - difference)
    moved = (
        lax.all_to_all(
            to_columns_layout(frames.reshape(2 * phases, row_count, col_count)),
            "row",
            split_axis=1,
            concat_axis=3,
            tiled=True,
        ),
        lax.all_to_all(
            to_columns_layout(rhs_penalty.reshape(2 * phases, row_count, col_count)),
            "row",
            split_axis=1,
            concat_axis=3,
            tiled=True,
        ),
        lax.all_to_all(
            to_columns_layout(coil_maps.reshape(2 * coil_count, row_count, col_count)),
            "row",
            split_axis=1,
            concat_axis=3,
            tiled=True,
        ),
        lax.all_to_all(
            to_columns_layout(measured.reshape(coil_count * 2 * phases, row_count, col_count)),
            "row",
            split_axis=1,
            concat_axis=3,
            tiled=True,
        ),
    )
    frames_cols = moved[0].reshape(2, phases, narrow, row_total)
    penalty_cols = moved[1].reshape(2, phases, narrow, row_total)
    maps_cols = moved[2].reshape(coil_count, 2, narrow, row_total)
    measured_cols = moved[3].reshape(coil_count, 2, phases, narrow, row_total)

    def gram_columns(values):
        real_part, imag_part = coil_images(maps_cols, values)
        back_real, back_imag = filtered(real_part, imag_part)
        return coil_combine(maps_cols, back_real, back_imag)

    back_real, back_imag = inverse(measured_cols[:, 0] * weight, measured_cols[:, 1] * weight)
    rhs = coil_combine(maps_cols, back_real, back_imag) + penalty_cols
    solved = conjugate(frames_cols, rhs, gram_columns)
    values = solved.reshape(2 * phases, narrow, row_total)
    reshaped = values.reshape(values.shape[:-2] + (narrow, groups, row_count))
    returned = lax.all_to_all(
        jnp.moveaxis(reshaped, -3, -1), "row", split_axis=1, concat_axis=3, tiled=True
    )
    estimate = returned.reshape(2, phases, row_count, col_count)
    following = from_behind(estimate[:, :1], "phase", -1)
    advanced = jnp.concatenate([estimate[:, 1:], following], 1)
    shifted = advanced - estimate + scaled_dual
    magnitude = jnp.sqrt(shifted[0] * shifted[0] + shifted[1] * shifted[1])
    factor = jnp.maximum(magnitude - THRESHOLD, 0.0) / jnp.maximum(magnitude, THRESHOLD)
    new_aux = shifted * factor[None]
    new_dual = shifted - new_aux
    primal_gap = new_dual - scaled_dual
    dual_gap = new_aux - auxiliary
    primal_sum, dual_sum = lax.psum(
        (jnp.sum(primal_gap * primal_gap), jnp.sum(dual_gap * dual_gap)), ("phase", "row")
    )
    residual_norms = jnp.stack([jnp.sqrt(primal_sum), PENALTY * jnp.sqrt(dual_sum)])
    return (estimate, new_aux, new_dual, residual_norms)


def solution(mesh):
    in_specs = (
        P(None, "phase", "row", None),
        P(None, "phase", "row", None),
        P(None, "phase", "row", None),
        P(None, None, "row", None),
        P(None, None, "phase", "row", None),
        P("phase", None),
    )
    out_specs = (
        P(None, "phase", "row", None),
        P(None, "phase", "row", None),
        P(None, "phase", "row", None),
        P(),
    )
    return jax.shard_map(local, mesh=mesh, in_specs=in_specs, out_specs=out_specs, check_vma=False)
```

profile of v0, /device:TPU:1, one launch (start us, length us, event | category | flops | bytes accessed | tf_op | source)
XLA Modules:
  0.0 575.1 jit_solution(8731979419725957966)
XLA Ops:
  1.7 2.5 collective-permute-start
  4.2 2.9 reshape_reshape.15
  7.1 1.9 copy.26
  10.5 6.3 %all-to-all-start = ((f32[16,1,4096]{2,1,0:T(1,128)}), f32[16,1,4096]{2,1,0:T(1,128)S(1)}, u32[]{:S(2)}, u32[]{:S(2)}) async-start(f32[16,1,4096]{2,1,0:T(1,128)} %reshape.40), calls=%async_computation | async-start | bytes 524288 | tf_op jit(solution)/shard_map/all_to_all | solution.py:130
  17.5 2.0 copy.45
  19.5 3.0 reshape.42
  24.2 4.1 all-to-all-start.3
  28.3 2.6 reshape_reshape.16
  30.9 4.0 copy.28
  36.7 6.3 %all-to-all-start.1 = ((f32[16,1,8192]{2,1,0:T(1,128)}), f32[16,1,8192]{2,1,0:T(1,128)S(1)}, u32[]{:S(2)}, u32[]{:S(2)}) async-start(f32[16,1,8192]{2,1,0:T(1,128)} %reshape.44), calls=%async_computation.1 | async-start | bytes 1048576 | tf_op jit(solution)/shard_map/all_to_all | solution.py:144
  43.1 19.4 %reshape_reshape.17 = f32[256,16,16,16]{3,2,1,0:T(8,128)} reshape(f32[16,2,8,16,256]{4,3,2,1,0:T(8,128)} %param.10) | data formatting | bytes 8388608 | tf_op jit(solution)/shard_map/reshape;reshape | solution.py:122
  62.5 21.3 %copy.30 = f32[256,16,16,16]{0,3,2,1:T(8,128)} copy(f32[256,16,16,16]{2,1,3,0:T(8,128)} %bitcast.200) | data formatting | bytes 8388608 | tf_op jit(solution)/shard_map/transpose | solution.py:123
  85.6 2.1 reshape.41
  88.5 5.7 all-to-all-start.2
  94.2 1.8 bitcast_bitcast_fusion.3
  96.0 2.6 copy.27
  98.6 2.4 reshape.33
  102.9 4.2 collective-permute-start.1
  111.9 2.2 copy.35
  115.1 1.9 reduce.2
  117.0 2.0 reshape.45
  119.1 1.8 bitcast_bitcast_fusion.1
  120.9 4.4 copy.29
  125.3 3.7 reshape.34
  129.0 2.9 fusion.10
  131.9 2.9 fusion.11
  134.8 3.0 subtract_multiply_fusion.2
  137.8 4.1 fusion.129
  141.9 3.3 add_multiply_fusion.2
  145.3 2.8 fusion.132
  148.1 4.1 convolution_subtract_fusion.2
  152.2 26.4 %copy.31 = f32[256,1,16,16,16]{4,3,2,0,1:T(8,128)} copy(f32[256,1,16,16,16]{0,4,2,3,1:T(8,128)} %bitcast.9) | data formatting | bytes 8388608 | tf_op jit(solution)/shard_map/all_to_all | solution.py:151
  178.6 23.6 %reshape.35 = f32[16,2,8,16,256]{4,3,2,1,0:T(8,128)} reshape(f32[256,1,16,16,16]{4,3,2,0,1:T(8,128)} %copy.31) | data formatting | bytes 8388608 | tf_op jit(solution)/shard_map/reshape | solution.py:162
  202.3 4.6 fusion.14
  206.9 2.9 fusion.16
  209.8 2.9 fusion.25
  212.7 3.0 fusion.22
  215.7 4.3 add_reduce_fusion.2
  220.9 2.9 fusion.7
  223.9 2.9 fusion.6
  226.7 5.1 collective-permute-start.3
  232.3 3.0 add_multiply_fusion.1
  235.3 2.9 fusion.126
  238.2 3.0 subtract_multiply_fusion.1
  241.1 2.9 fusion.123
  244.0 3.1 convolution_subtract_fusion.1
  247.1 3.4 add_reduce_fusion.1
  251.3 67.4 %all-reduce.1 = (f32[]{:T(128)}, f32[]{:T(128)}) all-reduce(f32[]{:T(128)} %get-tuple-element.15, f32[]{:T(128)} %get-tuple-element.14), channel_id=1, replica_groups=mesh['phase'=8,'row'=16] {'phase','row'}, use_global_device_ids=true, to_apply=%region_5.6 | all-reduce | flops 2 | bytes 16 | tf_op jit(solution)/shard_map/psum | solution.py:67
  320.7 62.7 %psum.44 = f32[]{:T(128)} all-reduce(f32[]{:T(128)} %multiply_reduce_fusion.2), channel_id=1, replica_groups=mesh['phase'=8,'row'=16] {'phase','row'}, use_global_device_ids=true, to_apply=%region_11.12 | all-reduce | flops 1 | bytes 8 | tf_op jit(solution)/shard_map/psum | solution.py:67
  384.9 2.9 fusion.3
  387.9 2.9 fusion.2
  390.8 2.8 collective-permute-start.5
  394.0 3.0 add_multiply_fusion
  397.0 2.8 fusion.120
  399.8 3.1 subtract_multiply_fusion
  402.9 2.8 fusion.117
  405.7 3.1 convolution_subtract_fusion
  408.8 3.4 add_reduce_fusion
  412.9 66.4 %psum.45 = f32[]{:T(128)} all-reduce(f32[]{:T(128)} %fusion.88), channel_id=1, replica_groups=mesh['phase'=8,'row'=16] {'phase','row'}, use_global_device_ids=true, to_apply=%region_15.16 | all-reduce | flops 1 | bytes 8 | tf_op jit(solution)/shard_map/psum | solution.py:80
  481.5 1.9 copy.38
  483.4 2.4 reshape.46
  485.8 11.3 %all_to_all.75 = f32[16,1,4096]{2,1,0:T(1,128)S(1)} all-to-all(f32[16,1,4096]{2,1,0:T(1,128)S(1)} %reshape.46), channel_id=1, replica_groups=mesh['phase'=8,'row'=16] {'row'}, dimensions={0} | all-to-all | bytes 524288 | tf_op jit(solution)/shard_map/all_to_all | solution.py:174
  501.4 2.3 collective-permute-start.7
  506.9 66.1 %all-reduce = (f32[]{:T(128)}, f32[]{:T(128)}) all-reduce(f32[]{:T(128)} %multiply_reduce_fusion, f32[]{:T(128)} %get-tuple-element.20), channel_id=1, replica_groups=mesh['phase'=8,'row'=16] {'phase','row'}, use_global_device_ids=true, to_apply=%region_19.20 | all-reduce | flops 2 | bytes 16 | tf_op jit(solution)/shard_map/psum | solution.py:187
  (85 shorter events, 29.7 us)
Async XLA Ops:
  1.7 15.1 %collective-permute-start = (f32[2,1,16,256]{3,2,1,0:T(8,128)S(1)}, f32[2,1,16,256]{3,2,1,0:T(8,128)S(1)}, u32[]{:S(2)}, u32[]{:S(2)}) collective-permute-start(f32[2,1,16,256]{3,2,1,0:T(8,128)S(1)} %slice.144), channel_id=1, source_target_pairs={{0,16},{16,32},{32,48},{48,64},{64,80},{80,96},{96,112},{112,0},{1... | collective-permute-start | bytes 98312 | tf_op jit(solution)/shard_map/ppermute | solution.py:33
  10.5 13.7 %all-to-all-start = ((f32[16,1,4096]{2,1,0:T(1,128)}), f32[16,1,4096]{2,1,0:T(1,128)S(1)}, u32[]{:S(2)}, u32[]{:S(2)}) async-start(f32[16,1,4096]{2,1,0:T(1,128)} %reshape.40), calls=%async_computation | async-start | bytes 524288 | tf_op jit(solution)/shard_map/all_to_all | solution.py:130
  19.5 8.8 %copy-start.11 = (f32[16,2,16,256]{3,2,1,0:T(8,128)S(1)}, f32[16,2,16,256]{3,2,1,0:T(8,128)}, u32[]{:S(2)}) copy-start(f32[16,2,16,256]{3,2,1,0:T(8,128)} %param.9) | copy-start | bytes 1572868
  24.2 12.5 %all-to-all-start.3 = ((f32[16,1,4096]{2,1,0:T(1,128)}), f32[16,1,4096]{2,1,0:T(1,128)S(1)}, u32[]{:S(2)}, u32[]{:S(2)}) async-start(f32[16,1,4096]{2,1,0:T(1,128)} %reshape.42), calls=%async_computation.3 | async-start | bytes 524288 | tf_op jit(solution)/shard_map/all_to_all | solution.py:137
  35.0 8.1 %copy-start.12 = (s32[8,256]{1,0:T(8,128)S(1)}, s32[8,256]{1,0:T(8,128)}, u32[]{:S(2)}) copy-start(s32[8,256]{1,0:T(8,128)} %param.11) | copy-start | bytes 24580
  36.7 25.8 %copy-start.8 = (f32[16,1,4096]{2,1,0:T(1,128)}, f32[16,1,4096]{2,1,0:T(1,128)S(1)}, u32[]{:S(2)}) copy-start(f32[16,1,4096]{2,1,0:T(1,128)S(1)} %all-to-all-done.3) | copy-start | bytes 786436
  36.7 51.0 %all-to-all-start.1 = ((f32[16,1,8192]{2,1,0:T(1,128)}), f32[16,1,8192]{2,1,0:T(1,128)S(1)}, u32[]{:S(2)}, u32[]{:S(2)}) async-start(f32[16,1,8192]{2,1,0:T(1,128)} %reshape.44), calls=%async_computation.1 | async-start | bytes 1048576 | tf_op jit(solution)/shard_map/all_to_all | solution.py:144
  87.7 0.8 copy-start.5
  88.5 63.7 %all-to-all-start.2 = ((f32[256,16,16,16]{0,3,2,1:T(8,128)}), f32[256,16,16,16]{0,3,2,1:T(8,128)}, u32[]{:S(2)}, u32[]{:S(2)}) async-start(f32[256,16,16,16]{0,3,2,1:T(8,128)} %copy.30), calls=%async_computation.2 | async-start | bytes 8388608 | tf_op jit(solution)/shard_map/all_to_all | solution.py:151
  101.8 6.5 %copy-start.9 = (f32[16,1,4096]{2,1,0:T(1,128)S(1)}, f32[16,1,4096]{2,1,0:T(1,128)}, u32[]{:S(2)}) copy-start(f32[16,1,4096]{2,1,0:T(1,128)} %copy-done.8) | copy-start | bytes 786436
  102.9 117.1 %collective-permute-start.1 = (f32[2,1,16,256]{3,2,1,0:T(8,128)}, f32[2,1,16,256]{3,2,1,0:T(8,128)}, u32[]{:S(2)}, u32[]{:S(2)}) collective-permute-start(f32[2,1,16,256]{3,2,1,0:T(8,128)} %get-tuple-element.35), channel_id=1, source_target_pairs={{16,0},{32,16},{48,32},{64,48},{80,64},{96,80},{112,96},{0,112},{1... | collective-permute-start | bytes 98312 | tf_op jit(solution)/shard_map/ppermute | solution.py:25
  107.1 112.9 %collective-permute-start.2 = (f32[2,1,16,256]{3,2,1,0:T(8,128)}, f32[2,1,16,256]{3,2,1,0:T(8,128)}, u32[]{:S(2)}, u32[]{:S(2)}) collective-permute-start(f32[2,1,16,256]{3,2,1,0:T(8,128)} %get-tuple-element.36), channel_id=1, source_target_pairs={{0,16},{16,32},{32,48},{48,64},{64,80},{80,96},{96,112},{112,0},{1... | collective-permute-start | bytes 98312 | tf_op jit(solution)/shard_map/ppermute | solution.py:24
  114.1 1.0 copy-start.6
  202.3 4.6 copy-start
  212.7 3.0 copy-start.1
  212.7 3.0 copy-start.2
  226.7 23.8 %collective-permute-start.3 = (f32[2,1,16,256]{3,2,1,0:T(8,128)S(1)}, f32[2,1,16,256]{3,2,1,0:T(8,128)S(1)}, u32[]{:S(2)}, u32[]{:S(2)}) collective-permute-start(f32[2,1,16,256]{3,2,1,0:T(8,128)S(1)} %get-tuple-element.33), channel_id=1, source_target_pairs={{16,0},{32,16},{48,32},{64,48},{80,64},{96,80},{112,96},{0,112},{1... | collective-permute-start | bytes 98312 | tf_op jit(solution)/shard_map/ppermute | solution.py:25
  231.9 18.6 %collective-permute-start.4 = (f32[2,1,16,256]{3,2,1,0:T(8,128)S(1)}, f32[2,1,16,256]{3,2,1,0:T(8,128)S(1)}, u32[]{:S(2)}, u32[]{:S(2)}) collective-permute-start(f32[2,1,16,256]{3,2,1,0:T(8,128)S(1)} %get-tuple-element.34), channel_id=1, source_target_pairs={{0,16},{16,32},{32,48},{48,64},{64,80},{80,96},{96,112},{112,0},{1... | collective-permute-start | bytes 98312 | tf_op jit(solution)/shard_map/ppermute | solution.py:24
  390.8 21.4 %collective-permute-start.5 = (f32[2,1,16,256]{3,2,1,0:T(8,128)S(1)}, f32[2,1,16,256]{3,2,1,0:T(8,128)S(1)}, u32[]{:S(2)}, u32[]{:S(2)}) collective-permute-start(f32[2,1,16,256]{3,2,1,0:T(8,128)S(1)} %get-tuple-element.29), channel_id=1, source_target_pairs={{16,0},{32,16},{48,32},{64,48},{80,64},{96,80},{112,96},{0,112},{1... | collective-permute-start | bytes 98312 | tf_op jit(solution)/shard_map/ppermute | solution.py:25
  393.6 18.7 %collective-permute-start.6 = (f32[2,1,16,256]{3,2,1,0:T(8,128)S(1)}, f32[2,1,16,256]{3,2,1,0:T(8,128)S(1)}, u32[]{:S(2)}, u32[]{:S(2)}) collective-permute-start(f32[2,1,16,256]{3,2,1,0:T(8,128)S(1)} %get-tuple-element.30), channel_id=1, source_target_pairs={{0,16},{16,32},{32,48},{48,64},{64,80},{80,96},{96,112},{112,0},{1... | collective-permute-start | bytes 98312 | tf_op jit(solution)/shard_map/ppermute | solution.py:24
  500.4 4.3 copy-start.4
  501.4 73.5 %copy-start.3 = (f32[2,8,16,256]{3,2,1,0:T(8,128)}, f32[2,8,16,256]{3,2,1,0:T(8,128)S(1)}, u32[]{:S(2)}) copy-start(f32[2,8,16,256]{3,2,1,0:T(8,128)S(1)} %reshape.37) | copy-start | bytes 786436
  501.4 4.8 copy-start.7
  501.4 3.3 collective-permute-start.7
  506.2 68.7 %copy-start.10 = (f32[2,8,16,256]{3,2,1,0:T(8,128)}, f32[2,8,16,256]{3,2,1,0:T(8,128)S(1)}, u32[]{:S(2)}) copy-start(f32[2,8,16,256]{3,2,1,0:T(8,128)S(1)} %get-tuple-element.22) | copy-start | bytes 786436
where the time goes:
time: 583 us; the launch traced here: 575 us
  blocking collectives  274 us (47%)
  local copies, waits for them, and re-layouts  150 us (26%)
  matrix products  88.7 us (15%)
  starting transfers between devices  40.4 us (7%)
  other arithmetic  12.8 us (2%)
  between operations  6.86 us (1%)
    psum x2, blocking collectives, residual_energy(): return lax.psum(jnp.sum(residual * residual), ('phase', 'row'))  130 us
    dot_general x28, matrix products, apply_table(): return jnp.dot(values, table, precision=EXACT)  88.7 us
    psum x1, blocking collectives, conjugate(): curvature = lax.psum(jnp.sum(direction * image_dir), ('phase', 'row'))  66.4 us
    psum x1, blocking collectives, local(): lax.psum((jnp.sum(primal_gap * primal_gap), jnp.sum(dual_gap * dual_gap))...  66.1 us
    transpose x4, local copies, waits for them, and re-layouts, to_columns_layout(): return jnp.moveaxis(reshaped, -3, -1)  29.3 us
    all_to_all x1, local copies, waits for them, and re-layouts, local(): lax.all_to_all(to_columns_layout(measured.reshape(coil_count * 2 * phases...  26.4 us
    another operation x4, local copies, waits for them, and re-layouts, to_columns_layout(): reshaped = values.reshape(values.shape[:-2] + (row_count, groups, narrow))  25.6 us
    reshape x1, local copies, waits for them, and re-layouts, local(): measured_cols = moved[3].reshape(coil_count, 2, phases, narrow, row_total)  23.6 us
  transfers between devices with their start and end apart: 12, of which 2 were waited for; matrix products, arithmetic and copies ran while one was open for 39% of the time, Pallas kernels for 0%

commit v1 on v0

v1 whole, which is shorter than its diff:
```python
import functools
import math

import jax
import jax.numpy as jnp
import numpy as np
from jax import lax
from jax.experimental import pallas as pl
from jax.experimental.pallas import tpu as pltpu
from jax.sharding import PartitionSpec as P

PENALTY = 0.5
DAMPING = 0.1
THRESHOLD = 1.0

COILS = 16
PHASES = 8
ROWS = 16
SIZE = 256
LANES = 128
GROUP = 16
ROW_SHARDS = 16
PHASE_SHARDS = 8
ALL = ROW_SHARDS * PHASE_SHARDS

F32 = jnp.float32
BF16 = jnp.bfloat16


def lane_bit(rows, bit):
    lane = lax.broadcasted_iota(jnp.int32, (rows, LANES), 1)
    return (lane & (GROUP << bit)) != 0


def lane_group(rows):
    return lax.broadcasted_iota(jnp.int32, (rows, LANES), 1) // GROUP


def roll(value, groups):
    groups %= 8
    if groups == 0:
        return value
    return pltpu.roll(value, groups * GROUP, 1)


def gather_coils(halves):
    rows = halves[0][0].shape[0]
    lane = lax.broadcasted_iota(jnp.int32, (rows, LANES), 1)
    turned = []
    for c, (low, high) in enumerate(halves):
        if c >= 8:
            low, high = high, low
        shift = c % 8
        if shift:
            low, high = roll(low, shift), roll(high, shift)
            wrapped = lane < shift * GROUP
            low, high = jnp.where(wrapped, high, low), jnp.where(wrapped, low, high)
        turned.append((low, high))
    for bit in range(3):
        mask = lane_bit(rows, bit)
        turned = [
            tuple(jnp.where(mask, turned[(i + (1 << bit)) % 16][h], turned[i][h]) for h in range(2))
            for i in range(16)
        ]
    turned = [(turned[i][0], turned[(i + 8) % 16][1]) for i in range(16)]
    return [turned[(-j) % 16] for j in range(16)]


def transpose_groups(values):
    rows = values[0].shape[0]
    turned = [roll(value, a) for a, value in enumerate(values)]
    for bit in range(3):
        mask = lane_bit(rows, bit)
        turned = [jnp.where(mask, turned[(i + (1 << bit)) % 8], turned[i]) for i in range(8)]
    return [roll(turned[(-b) % 8], -b) for b in range(8)]


def pick_groups(values):
    rows = values[0].shape[0]
    for bit in range(3):
        mask = lane_bit(rows, bit)
        values = [jnp.where(mask, values[i + 1], values[i]) for i in range(0, len(values), 2)]
    return values[0]


def sum_groups(value):
    value = value + pltpu.roll(value, 4 * GROUP, 1)
    value = value + pltpu.roll(value, 2 * GROUP, 1)
    return value + pltpu.roll(value, GROUP, 1)


def spread_group(value, group):
    return sum_groups(jnp.where(lane_group(value.shape[0]) == group, value, 0.0))


def split(value):
    high = value.astype(BF16)
    return high, (value - high.astype(F32)).astype(BF16)


def dot(a, b):
    return jnp.dot(a, b, preferred_element_type=F32)


def dot3(table, value):
    return dot(table[0], value[0]) + (dot(table[0], value[1]) + dot(table[1], value[0]))


def wide(value):
    return jnp.concatenate([value, value], 1)


def combine(maps_real, maps_imag, real, imag):
    out_real = maps_real * real + maps_imag * imag
    out_imag = maps_real * imag - maps_imag * real
    return (
        sum_groups(out_real[:, :LANES] + out_real[:, LANES:]),
        sum_groups(out_imag[:, :LANES] + out_imag[:, LANES:]),
    )


def coil_images(maps_real, maps_imag, real, imag):
    real, imag = wide(real), wide(imag)
    return maps_real * real - maps_imag * imag, maps_real * imag + maps_imag * real


def pack_measured_kernel(in_ref, out_ref):
    for row in range(0, in_ref.shape[2], 8):
        halves = [
            (in_ref[c, 0, row : row + 8, :LANES], in_ref[c, 0, row : row + 8, LANES:])
            for c in range(COILS)
        ]
        for j, (low, high) in enumerate(gather_coils(halves)):
            out_ref[j, row : row + 8, :LANES] = low
            out_ref[j, row : row + 8, LANES:] = high


def pack_measured(measured, part):
    lines = measured.shape[2]
    step = 32
    return pl.pallas_call(
        pack_measured_kernel,
        grid=(lines // step,),
        in_specs=[pl.BlockSpec((COILS, 1, step, SIZE), lambda i: (0, part, i, 0))],
        out_specs=pl.BlockSpec((ROW_SHARDS, step, SIZE), lambda i: (0, i, 0)),
        out_shape=jax.ShapeDtypeStruct((ROW_SHARDS, lines, SIZE), F32),
        name=f"pack_measured_{part}",
    )(measured)


def pack_image_kernel(maps_ref, frames_ref, aux_ref, dual_ref, before_ref, after_ref, out_ref):
    for part in range(2):
        for row in range(0, ROWS, 8):
            at = slice(row, row + 8)
            halves = [
                (maps_ref[c, part, at, :LANES], maps_ref[c, part, at, LANES:]) for c in range(COILS)
            ]
            for j, (low, high) in enumerate(gather_coils(halves)):
                out_ref[j, part, at, :LANES] = low
                out_ref[j, part, at, LANES:] = high
            for half in range(2):
                cols = slice(half * LANES, (half + 1) * LANES)
                frames = [frames_ref[part, t, at, cols] for t in range(PHASES)]
                following = frames[1:] + [after_ref[part, 0, at, cols]]
                gap = [
                    aux_ref[part, t, at, cols] - dual_ref[part, t, at, cols] - following[t] + frames[t]
                    for t in range(PHASES)
                ]
                gap_before = [before_ref[part, 0, at, cols] - frames[0]] + gap[:-1]
                local = [
                    PENALTY * (gap_before[t] - gap[t]) - DAMPING * frames[t] for t in range(PHASES)
                ]
                to = slice(part * LANES, (part + 1) * LANES)
                for which, values in ((2, frames), (3, local)):
                    for jj, value in enumerate(transpose_groups(values)):
                        out_ref[half * 8 + jj, which, at, to] = value


def gram_table_kernel(weight_ref, tables_ref, out_ref):
    weight = weight_ref[0]
    cos_high, cos_low, sin_high, sin_low = (tables_ref[i] for i in range(4))

    def scaled(table):
        return (table.astype(F32) * weight).astype(BF16)

    cos_w = scaled(cos_high), scaled(cos_low)
    sin_w = scaled(sin_high), scaled(sin_low)
    cos, sin = (cos_high, cos_low), (sin_high, sin_low)
    real = dot3(cos_w, cos) + dot3(sin_w, sin)
    imag = dot3(sin_w, cos) - dot3(cos_w, sin)
    out_ref[0, 0], out_ref[0, 2] = split(real)
    out_ref[0, 1], out_ref[0, 3] = split(imag)


def gram_tables(weight, tables):
    return pl.pallas_call(
        gram_table_kernel,
        grid=(PHASES,),
        in_specs=[
            pl.BlockSpec((1, 1, SIZE), lambda t: (t, 0, 0)),
            pl.BlockSpec((4, SIZE, SIZE), lambda t: (0, 0, 0)),
        ],
        out_specs=pl.BlockSpec((1, 4, SIZE, SIZE), lambda t: (t, 0, 0, 0)),
        out_shape=jax.ShapeDtypeStruct((PHASES, 4, SIZE, SIZE), BF16),
        name="gram_tables",
    )(weight, tables)


def maps_of(image_ref):
    return image_ref[:, 0].reshape(SIZE, SIZE), image_ref[:, 1].reshape(SIZE, SIZE)


def gram(gram_ref, maps, real, imag):
    real, imag = (split(v) for v in coil_images(*maps, real, imag))
    table_real = gram_ref[0, 0], gram_ref[0, 2]
    table_imag = gram_ref[0, 1], gram_ref[0, 3]
    back_real = dot3(table_real, real) - dot3(table_imag, imag)
    back_imag = dot3(table_real, imag) + dot3(table_imag, real)
    return combine(*maps, back_real, back_imag)


def start_kernel(gram_ref, image_ref, out_ref):
    t = pl.program_id(0)
    frames = image_ref[:, 2].reshape(SIZE, SIZE)
    local = image_ref[:, 3].reshape(SIZE, SIZE)
    real, imag = spread_group(frames[:, :LANES], t), spread_group(frames[:, LANES:], t)
    gram_real, gram_imag = gram(gram_ref, maps_of(image_ref), real, imag)
    out_ref[0, 0] = spread_group(local[:, :LANES], t) - gram_real
    out_ref[1, 0] = spread_group(local[:, LANES:], t) - gram_imag


GRAM_SPEC = pl.BlockSpec((1, 4, SIZE, SIZE), lambda t: (t, 0, 0, 0))
IMAGE_SPEC = pl.BlockSpec((ROW_SHARDS, 4, ROWS, SIZE), lambda t: (0, 0, 0, 0))
MAPS_SPEC = pl.BlockSpec((ROW_SHARDS, 2, ROWS, SIZE), lambda t: (0, 0, 0, 0))
VECTOR_SPEC = pl.BlockSpec((2, 1, SIZE, LANES), lambda t: (0, t, 0, 0))
VECTOR = jax.ShapeDtypeStruct((2, PHASES, SIZE, LANES), F32)


def start(grams, image):
    return pl.pallas_call(
        start_kernel,
        grid=(PHASES,),
        in_specs=[GRAM_SPEC, IMAGE_SPEC],
        out_specs=VECTOR_SPEC,
        out_shape=VECTOR,
        name="start",
    )(grams, image)


def adjoint_kernel(part, weight_ref, tables_ref, image_ref, lines_ref, in_ref, out_ref):
    weight = weight_ref[0]
    lines = split(lines_ref[...].reshape(SIZE, SIZE))

    def scaled(i):
        return (tables_ref[i].astype(F32) * weight).astype(BF16)

    by_cos = dot3((scaled(0), scaled(1)), lines)
    by_sin = dot3((scaled(2), scaled(3)), lines)
    maps = maps_of(image_ref)
    if part == 0:
        real, imag = combine(*maps, by_cos, by_sin)
    else:
        real, imag = combine(*maps, -by_sin, by_cos)
    out_ref[0, 0] = in_ref[0, 0] + real
    out_ref[1, 0] = in_ref[1, 0] + imag


def adjoint(part, weight, tables, image, lines, so_far):
    return pl.pallas_call(
        functools.partial(adjoint_kernel, part),
        grid=(PHASES,),
        in_specs=[
            pl.BlockSpec((1, 1, SIZE), lambda t: (t, 0, 0)),
            pl.BlockSpec((4, SIZE, SIZE), lambda t: (0, 0, 0)),
            MAPS_SPEC,
            pl.BlockSpec((ROW_SHARDS, ROWS, SIZE), lambda t: (0, t, 0)),
            VECTOR_SPEC,
        ],
        out_specs=VECTOR_SPEC,
        out_shape=VECTOR,
        name=f"adjoint_{part}",
    )(weight, tables, image, lines, so_far)


def gram_kernel(gram_ref, image_ref, in_ref, out_ref):
    real, imag = gram(gram_ref, maps_of(image_ref), in_ref[0, 0], in_ref[1, 0])
    out_ref[0, 0] = real
    out_ref[1, 0] = imag


def gram_apply(grams, image, vector):
    return pl.pallas_call(
        gram_kernel,
        grid=(PHASES,),
        in_specs=[GRAM_SPEC, MAPS_SPEC, VECTOR_SPEC],
        out_specs=VECTOR_SPEC,
        out_shape=VECTOR,
        name="gram_apply",
    )(grams, image, vector)


def fold(value):
    return jnp.sum(value.reshape(-1, 8, LANES), 0)


def normal_kernel(first_ref, gram_ref, before_ref, after_ref, image_ref, edge_ref, back_ref, sums_ref):
    @pl.when(pl.program_id(0) == 0)
    def _():
        sums_ref[...] = jnp.zeros_like(sums_ref)

    rows = first_ref.shape[2]
    rr = rw = ww = dd = 0.0
    for part in range(2):
        values = [first_ref[part, t] for t in range(PHASES)]
        around = [before_ref[part]] + values + [after_ref[part]]
        images = [
            gram_ref[part, t]
            + PENALTY * ((around[t + 1] - around[t]) - (around[t + 2] - around[t + 1]))
            + DAMPING * values[t]
            for t in range(PHASES)
        ]
        for t in range(PHASES):
            image_ref[part, t] = images[t]
            rr += fold(values[t] * values[t])
            rw += fold(values[t] * images[t])
            ww += fold(images[t] * images[t])
            if t:
                step = images[t] - images[t - 1]
                dd += fold(step * step)
        edge_ref[part] = images[0]
        for which, vectors in ((0, values), (1, images)):
            back = pick_groups(vectors)
            for j in range(rows // ROWS):
                back_ref[j, 2 * which + part] = back[j * ROWS : (j + 1) * ROWS]
    for i, value in enumerate((rr, rw, ww, dd)):
        sums_ref[i] += value


def normal(first, grams_first, before, after):
    rows = 64
    whole = pl.BlockSpec((2, PHASES, rows, LANES), lambda i: (0, 0, i, 0))
    edge = pl.BlockSpec((2, rows, LANES), lambda i: (0, i, 0))
    return pl.pallas_call(
        normal_kernel,
        grid=(SIZE // rows,),
        in_specs=[whole, whole, edge, edge],
        out_specs=[
            whole,
            edge,
            pl.BlockSpec((rows // ROWS, 4, ROWS, LANES), lambda i: (i, 0, 0, 0)),
            pl.BlockSpec((4, 8, LANES), lambda i: (0, 0, 0)),
        ],
        out_shape=[
            VECTOR,
            jax.ShapeDtypeStruct((2, SIZE, LANES), F32),
            jax.ShapeDtypeStruct((ROW_SHARDS, 4, ROWS, LANES), F32),
            jax.ShapeDtypeStruct((4, 8, LANES), F32),
        ],
        name="normal",
    )(first, grams_first, before, after)


def curvature_kernel(gram_ref, image_ref, in_ref, out_ref):
    @pl.when(pl.program_id(0) == 0)
    def _():
        out_ref[...] = jnp.zeros_like(out_ref)

    real, imag = coil_images(*maps_of(image_ref), in_ref[0, 0], in_ref[1, 0])
    real_high, imag_high = real.astype(BF16), imag.astype(BF16)
    table_real, table_imag = gram_ref[0, 0], gram_ref[0, 1]
    back_real = dot(table_real, real_high) - dot(table_imag, imag_high)
    back_imag = dot(table_real, imag_high) + dot(table_imag, real_high)
    total = real * back_real + imag * back_imag
    out_ref[...] += fold(total[:, :LANES]) + fold(total[:, LANES:])


def curvature(grams, image, vector):
    return pl.pallas_call(
        curvature_kernel,
        grid=(PHASES,),
        in_specs=[pl.BlockSpec((1, 2, SIZE, SIZE), lambda t: (t, 0, 0, 0)), MAPS_SPEC, VECTOR_SPEC],
        out_specs=pl.BlockSpec((8, LANES), lambda t: (0, 0)),
        out_shape=jax.ShapeDtypeStruct((8, LANES), F32),
        name="curvature",
    )(grams, image, vector)


def lane_row(values):
    lane = lax.broadcasted_iota(jnp.int32, (1, LANES), 1)
    row = jnp.zeros((1, LANES), F32)
    for i, value in enumerate(values):
        row = jnp.where(lane == i, value, row)
    return row


def whole_sum(value):
    return jnp.sum(jnp.sum(value, 0, keepdims=True), 1, keepdims=True)


def share_kernel(sums_ref, curve_ref, last_ref, after_ref, out_ref):
    rr, rw, ww, dd = (whole_sum(sums_ref[i]) * 0.125 for i in range(4))
    edge = 0.0
    for part in range(2):
        step = after_ref[part] - last_ref[part, 0]
        edge = edge + fold(step * step)
    dd = dd + whole_sum(edge) * 0.125
    curve = whole_sum(curve_ref[...]) + PENALTY * dd + DAMPING * ww
    row = lane_row((rr, rw, ww, curve))
    out_ref[...] = jnp.broadcast_to(row[None], out_ref.shape)


def share(sums, curve, vector, after):
    return pl.pallas_call(
        share_kernel,
        grid=(1,),
        in_specs=[
            pl.BlockSpec((4, 8, LANES), lambda i: (0, 0, 0)),
            pl.BlockSpec((8, LANES), lambda i: (0, 0)),
            pl.BlockSpec((2, 1, SIZE, LANES), lambda i: (0, PHASES - 1, 0, 0)),
            pl.BlockSpec((2, SIZE, LANES), lambda i: (0, 0, 0)),
        ],
        out_specs=pl.BlockSpec((ALL, 1, LANES), lambda i: (0, 0, 0)),
        out_shape=jax.ShapeDtypeStruct((ALL, 1, LANES), F32),
        name="share",
    )(sums, curve, vector, after)


def unpack_kernel(in_ref, out_ref, edge_ref):
    for which in range(4):
        for row in range(0, ROWS, 8):
            at = slice(row, row + 8)
            for half in range(2):
                values = [in_ref[half * 8 + jj, which, at] for jj in range(8)]
                cols = slice(half * LANES, (half + 1) * LANES)
                for t, value in enumerate(transpose_groups(values)):
                    out_ref[which, t, at, cols] = value
                    if t == 0:
                        edge_ref[which, at, cols] = value


def unpack(back):
    return pl.pallas_call(
        unpack_kernel,
        out_shape=[
            jax.ShapeDtypeStruct((4, PHASES, ROWS, SIZE), F32),
            jax.ShapeDtypeStruct((4, ROWS, SIZE), F32),
        ],
        name="unpack",
    )(back)


def finish_kernel(
    shared_ref, frames_ref, aux_ref, dual_ref, steps_ref, edge_ref, after_ref,
    x_ref, new_aux_ref, new_dual_ref, out_ref,
):
    row = jnp.sum(shared_ref[...], 0)
    rr, rw, ww, curve = (row[:, i : i + 1] for i in range(4))
    alpha = rr / rw
    fresh = rr - 2.0 * alpha * rw + alpha * alpha * ww
    beta = fresh / rr
    gamma = 1.0 + beta
    bend = gamma * gamma * rw - 2.0 * gamma * alpha * ww + alpha * alpha * curve
    second = fresh / bend
    by_first = alpha + second * gamma
    by_image = -second * alpha
    primal = dual_sum = 0.0
    for row in range(0, ROWS, 8):
        at = slice(row, row + 8)
        parts = []
        for part in range(2):
            values = [
                frames_ref[part, t, at]
                + by_first * steps_ref[part, t, at]
                + by_image * steps_ref[2 + part, t, at]
                for t in range(PHASES)
            ]
            for t in range(PHASES):
                x_ref[part, t, at] = values[t]
            after = (
                after_ref[part, 0, at]
                + by_first * edge_ref[part, at]
                + by_image * edge_ref[2 + part, at]
            )
            parts.append(values + [after])
        for t in range(PHASES):
            dual = [dual_ref[part, t, at] for part in range(2)]
            shifted = [parts[part][t + 1] - parts[part][t] + dual[part] for part in range(2)]
            magnitude = jnp.sqrt(shifted[0] * shifted[0] + shifted[1] * shifted[1])
            factor = jnp.maximum(magnitude - THRESHOLD, 0.0) / jnp.maximum(magnitude, THRESHOLD)
            for part in range(2):
                new_aux = shifted[part] * factor
                new_dual = shifted[part] - new_aux
                new_aux_ref[part, t, at] = new_aux
                new_dual_ref[part, t, at] = new_dual
                gap = new_dual - dual[part]
                primal += gap * gap
                gap = new_aux - aux_ref[part, t, at]
                dual_sum += gap * gap
    sums = lane_row((whole_sum(primal), whole_sum(dual_sum)))
    out_ref[...] = jnp.broadcast_to(sums[None], out_ref.shape)


def finish(shared, frames, auxiliary, scaled_dual, steps, edge, after):
    image = jax.ShapeDtypeStruct((2, PHASES, ROWS, SIZE), F32)
    return pl.pallas_call(
        finish_kernel,
        out_shape=[image, image, image, jax.ShapeDtypeStruct((ALL, 1, LANES), F32)],
        name="finish",
    )(shared, frames, auxiliary, scaled_dual, steps, edge, after)


def norms_kernel(in_ref, out_ref):
    root = jnp.sqrt(jnp.sum(in_ref[...], 0))
    lane = lax.broadcasted_iota(jnp.int32, (1, LANES), 1)
    out_ref[...] = jnp.where(lane == 1, PENALTY, 1.0) * root


def norms(shared):
    return pl.pallas_call(
        norms_kernel, out_shape=jax.ShapeDtypeStruct((1, LANES), F32), name="norms"
    )(shared)


def tables():
    index = np.arange(SIZE)
    angle = (index[:, None] * index[None, :] % SIZE) * (2.0 * math.pi / SIZE)
    out = []
    for table in (np.cos(angle), np.sin(angle)):
        table = (table / math.sqrt(SIZE)).astype(np.float32)
        high = table.astype(BF16)
        out += [high, (table - high.astype(np.float32)).astype(BF16)]
    return np.stack(out)


def shift(value, steps):
    pairs = [(i, (i + steps) % PHASE_SHARDS) for i in range(PHASE_SHARDS)]
    return lax.ppermute(value, "phase", pairs)


def exchange(value, axes):
    return lax.all_to_all(value, axes, 0, 0, tiled=True)


def local(frames, auxiliary, scaled_dual, coil_maps, measured, sampling):
    table = jnp.asarray(tables())
    weight = sampling.astype(F32)[:, None, :]
    lines = measured.reshape(COILS, 2, PHASES * ROWS, SIZE)

    last = slice(PHASES - 1, PHASES)
    before = shift(auxiliary[:, last] - scaled_dual[:, last] + frames[:, last], 1)
    after = shift(frames[:, :1], -1)
    packed_real = exchange(pack_measured(lines, 0), "row")
    packed_image = pl.pallas_call(
        pack_image_kernel,
        out_shape=jax.ShapeDtypeStruct((ROW_SHARDS, 4, ROWS, SIZE), F32),
        name="pack_image",
    )(coil_maps, frames, auxiliary, scaled_dual, before, after)
    image = exchange(packed_image, "row")
    packed_imag = exchange(pack_measured(lines, 1), "row")

    grams = gram_tables(weight, table)
    residual = start(grams, image)
    residual = adjoint(0, weight, table, image, packed_real, residual)
    residual = adjoint(1, weight, table, image, packed_imag, residual)

    residual_before = shift(residual[:, PHASES - 1], 1)
    residual_after = shift(residual[:, 0], -1)
    grams_residual = gram_apply(grams, image, residual)
    product, product_first, back, sums = normal(
        residual, grams_residual, residual_before, residual_after
    )
    product_after = shift(product_first, -1)
    steps, steps_first = unpack(exchange(back, "row"))
    steps_after = shift(steps_first, -1)
    curve = curvature(grams, image, product)
    shared = exchange(share(sums, curve, product, product_after), ("phase", "row"))
    new_frames, new_aux, new_dual, gaps = finish(
        shared, frames, auxiliary, scaled_dual, steps, steps_after, after
    )
    residual_norms = norms(exchange(gaps, ("phase", "row")))[0, :2]
    return new_frames, new_aux, new_dual, residual_norms


def solution(mesh):
    image = P(None, "phase", "row", None)
    in_specs = (
        image,
        image,
        image,
        P(None, None, "row", None),
        P(None, None, "phase", "row", None),
        P("phase", None),
    )
    return jax.shard_map(
        local, mesh=mesh, in_specs=in_specs, out_specs=(image, image, image, P()), check_vma=False
    )
```

time: 583 us -> 206 us (0.35); the launches traced: 575 us -> 204 us
  blocking collectives: 274 us -> 30.7 us
  local copies, waits for them, and re-layouts: 150 us -> 7.02 us
  matrix products: 88.7 us -> 0 us
  Pallas kernels: 0 us -> 77.9 us
  waiting for transfers between devices: 2.66 us -> 49.1 us
  other arithmetic: 12.8 us -> 0.83 us
  between operations: 6.86 us -> 0.7 us
    psum x4 -> x0, blocking collectives: 263 us -> none  [the longest x2 130 us: residual_energy(): return lax.psum(jnp.sum(residual * residual), ('phase', 'row'))]
    dot_general x28 -> x0, matrix products: 88.7 us -> none  [apply_table(): return jnp.dot(values, table, precision=EXACT)]
    pallas_call x0 -> x14, Pallas kernels: none -> 77.9 us  [the longest x2 17.5 us: adjoint(): pl.pallas_call(functools.partial(adjoint_kernel, part), grid=(PHASES,), i...]
    all_to_all x10 -> x0, local copies, waits for them, and re-layouts: 42.6 us -> none  [the longest x1 26.4 us: local(): lax.all_to_all(to_columns_layout(measured.reshape(coil_count * 2 * phases...]
    all_to_all x4, waiting for transfers between devices: 1.64 us -> 42.7 us  [exchange(): return lax.all_to_all(value, axes, 0, 0, tiled=True)]
    reshape x5 -> x0, local copies, waits for them, and re-layouts: 31.7 us -> none  [the longest x1 23.6 us: local(): measured_cols = moved[3].reshape(coil_count, 2, phases, narrow, row_total)]
    transpose x5 -> x0, local copies, waits for them, and re-layouts: 31.2 us -> none  [the longest x4 29.3 us: to_columns_layout(): return jnp.moveaxis(reshaped, -3, -1)]
    another operation x5 -> x0, local copies, waits for them, and re-layouts: 26.2 us -> none  [the longest x4 25.6 us: to_columns_layout(): reshaped = values.reshape(values.shape[:-2] + (row_count, groups, narrow))]
  transfers between devices with their start and end apart: 12 -> 10, of which waited for: 2 -> 5; matrix products, arithmetic and copies ran while one was open for 39% -> 0% of each run, Pallas kernels for 0% -> 28%
where the time goes in v1:
time: 206 us; the launch traced here: 204 us
  Pallas kernels  77.9 us (38%)
  waiting for transfers between devices  49.1 us (24%)
  starting transfers between devices  38 us (18%)
  blocking collectives  30.7 us (15%)
  local copies, waits for them, and re-layouts  7.02 us (3%)
    all_to_all x4, waiting for transfers between devices, exchange(): return lax.all_to_all(value, axes, 0, 0, tiled=True)  42.7 us
    all_to_all x2, blocking collectives, exchange(): return lax.all_to_all(value, axes, 0, 0, tiled=True)  30.7 us
    all_to_all x4, starting transfers between devices, exchange(): return lax.all_to_all(value, axes, 0, 0, tiled=True)  22.7 us
    pallas_call x2, Pallas kernels, adjoint(): pl.pallas_call(functools.partial(adjoint_kernel, part), grid=(PHASES,), i...  17.5 us
    ppermute x6, starting transfers between devices, shift(): return lax.ppermute(value, 'phase', pairs)  15.3 us
    pallas_call x1, Pallas kernels, start(): pl.pallas_call(start_kernel, grid=(PHASES,), in_specs=[GRAM_SPEC, IMAGE_S...  10.9 us
    pallas_call x1, Pallas kernels, gram_apply(): pl.pallas_call(gram_kernel, grid=(PHASES,), in_specs=[GRAM_SPEC, MAPS_SPE...  10 us
    pallas_call x2, Pallas kernels, pack_measured(): pl.pallas_call(pack_measured_kernel, grid=(lines // step,), in_specs=[pl....  8.36 us
  transfers between devices with their start and end apart: 10, of which 5 were waited for; matrix products, arithmetic and copies ran while one was open for 0% of the time, Pallas kernels for 28%

profile of v1, /device:TPU:1, one launch (start us, length us, event | category | flops | bytes accessed | tf_op | source)
XLA Modules:
  0.0 204.2 jit_solution(977692420437744988)
XLA Ops:
  0.6 0.8 fusion
  1.5 7.3 %collective-permute-start.1 = (f32[2,1,16,256]{3,2,1,0:T(8,128)S(1)}, f32[2,1,16,256]{3,2,1,0:T(8,128)S(1)}, u32[]{:S(2)}, u32[]{:S(2)}) collective-permute-start(f32[2,1,16,256]{3,2,1,0:T(8,128)S(1)} %get-tuple-element.26), channel_id=1, source_target_pairs={{0,112},{16,0},{32,16},{48,32},{64,48},{80,64},{96,80},{112,96},{1... | collective-permute-start | bytes 98312 | tf_op jit(solution)/shard_map/ppermute | solution.py:537
  8.7 0.0 collective-permute-start
  8.7 1.0 collective-permute-done.1.after_ref
  9.8 0.0 copy-start.6
  9.8 5.4 %collective-permute-done.before_ref = f32[2,1,16,256]{3,2,1,0:T(8,128)S(1)} collective-permute-done((f32[2,1,16,256]{3,2,1,0:T(8,128)S(1)}, f32[2,1,16,256]{3,2,1,0:T(8,128)S(1)}, u32[]{:S(2)}, u32[]{:S(2)}) %collective-permute-start) | collective-permute-done | bytes 32800 | tf_op jit(solution)/shard_map/ppermute | solution.py:537
  15.1 0.0 copy-done.6
  15.1 0.0 copy-start.8
  15.1 0.6 copy-done.8
  15.7 3.4 %pack_image.1 = f32[16,4,16,256]{3,2,1,0:T(8,128)} custom-call(f32[16,2,16,256]{3,2,1,0:T(8,128)} %maps_ref.1, f32[2,8,16,256]{3,2,1,0:T(8,128)} %frames_ref.3, f32[2,8,16,256]{3,2,1,0:T(8,128)} %aux_ref.3, f32[2,8,16,256]{3,2,1,0:T(8,128)} %dual_ref.3, f32[2,1,16,256]{3,2,1,0:T(8,128)} %copy-done.8, f32[2,1,16,256]{3,2,1,0:T(8,128)} %copy-done.6), custom_call_target="tpu_custom_call" | custom-call | tf_op jit(solution)/shard_map/pack_image/pallas_call | solution.py:553
  19.1 6.5 %all-to-all-start = ((f32[16,4,16,256]{3,2,1,0:T(8,128)}), f32[16,4,16,256]{3,2,1,0:T(8,128)S(1)}, u32[]{:S(2)}, u32[]{:S(2)}) async-start(f32[16,4,16,256]{3,2,1,0:T(8,128)} %pack_image.1), calls=%async_computation | async-start | bytes 2097152 | tf_op jit(solution)/shard_map/all_to_all | solution.py:541
  25.6 4.2 %pack_measured_0.1 = f32[16,128,256]{2,1,0:T(8,128)} custom-call(f32[16,2,128,256]{3,2,1,0:T(8,128)} %bitcast.11), custom_call_target="tpu_custom_call" | custom-call | tf_op jit(solution)/shard_map/pack_measured_0/pallas_call | solution.py:141
  29.8 11.5 %all-to-all-done.image_ref = f32[16,4,16,256]{3,2,1,0:T(8,128)S(1)} async-done(((f32[16,4,16,256]{3,2,1,0:T(8,128)}), f32[16,4,16,256]{3,2,1,0:T(8,128)S(1)}, u32[]{:S(2)}, u32[]{:S(2)}) %all-to-all-start) | async-done | bytes 1048608 | tf_op jit(solution)/shard_map/all_to_all | solution.py:541
  41.4 0.0 copy-start
  41.4 4.4 %all-to-all-start.2 = ((f32[16,128,256]{2,1,0:T(8,128)}), f32[16,128,256]{2,1,0:T(8,128)S(1)}, u32[]{:S(2)}, u32[]{:S(2)}) async-start(f32[16,128,256]{2,1,0:T(8,128)} %pack_measured_0.1), calls=%async_computation.2 | async-start | bytes 4194304 | tf_op jit(solution)/shard_map/all_to_all | solution.py:541
  45.7 4.2 %pack_measured_1.1 = f32[16,128,256]{2,1,0:T(8,128)} custom-call(f32[16,2,128,256]{3,2,1,0:T(8,128)} %bitcast.12), custom_call_target="tpu_custom_call" | custom-call | tf_op jit(solution)/shard_map/pack_measured_1/pallas_call | solution.py:141
  49.9 0.0 copy-done
  49.9 0.0 copy-start.9
  49.9 22.8 %all-to-all-done.2.lines_ref = f32[16,128,256]{2,1,0:T(8,128)S(1)} async-done(((f32[16,128,256]{2,1,0:T(8,128)}), f32[16,128,256]{2,1,0:T(8,128)S(1)}, u32[]{:S(2)}, u32[]{:S(2)}) %all-to-all-start.2) | async-done | bytes 2097184 | tf_op jit(solution)/shard_map/all_to_all | solution.py:541
  72.8 0.0 copy-start.1
  72.8 5.5 %all-to-all-start.1 = ((f32[16,128,256]{2,1,0:T(8,128)}), f32[16,128,256]{2,1,0:T(8,128)}, u32[]{:S(2)}, u32[]{:S(2)}) async-start(f32[16,128,256]{2,1,0:T(8,128)} %pack_measured_1.1), calls=%async_computation.1 | async-start | bytes 4194304 | tf_op jit(solution)/shard_map/all_to_all | solution.py:541
  78.3 0.0 copy-done.9
  78.3 0.0 copy-done.1
  78.3 0.6 broadcast_in_dim.3.weight_ref
  78.9 7.4 %gram_tables.1.gram_ref = bf16[8,4,256,256]{3,2,1,0:T(8,128)(2,1)} custom-call(f32[8,1,256]{2,1,0:T(1,128)} %broadcast_in_dim.3.weight_ref, bf16[4,256,256]{2,1,0:T(8,128)(2,1)} %constant.2.clone.tables_ref), custom_call_target="tpu_custom_call" | custom-call | tf_op jit(solution)/shard_map/gram_tables/pallas_call | solution.py:196
  86.3 10.9 %start.1.in_ref = f32[2,8,256,128]{3,2,1,0:T(8,128)} custom-call(bf16[8,4,256,256]{3,2,1,0:T(8,128)(2,1)} %gram_tables.1.gram_ref, f32[16,4,16,256]{3,2,1,0:T(8,128)} %copy-done), custom_call_target="tpu_custom_call" | custom-call | tf_op jit(solution)/shard_map/start/pallas_call | solution.py:240
  97.2 8.7 %adjoint_0.1.in_ref = f32[2,8,256,128]{3,2,1,0:T(8,128)} custom-call(f32[8,1,256]{2,1,0:T(1,128)} %broadcast_in_dim.3.weight_ref, bf16[4,256,256]{2,1,0:T(8,128)(2,1)} %constant.2.clone.tables_ref, f32[16,4,16,256]{3,2,1,0:T(8,128)} %copy-done, f32[16,128,256]{2,1,0:T(8,128)} %copy-done.1, f32[2,8,256,128]{3,2,1,0:T(8,128)} %start.1.in_ref), custom_call_target="tpu_custom_call" | custom-call | tf_op jit(solution)/shard_map/adjoint_0/pallas_call | solution.py:269
  105.9 0.0 all-to-all-done.1.lines_ref
  106.0 8.8 %adjoint_1.1.in_ref.first_ref = f32[2,8,256,128]{3,2,1,0:T(8,128)} custom-call(f32[8,1,256]{2,1,0:T(1,128)} %broadcast_in_dim.3.weight_ref, bf16[4,256,256]{2,1,0:T(8,128)(2,1)} %constant.2.clone.tables_ref, f32[16,4,16,256]{3,2,1,0:T(8,128)} %copy-done, f32[16,128,256]{2,1,0:T(8,128)} %all-to-all-done.1.lines_ref, f32[2,8,256,128]{3,2,1,0:T(8,128)} %adjoint_0.1.in_ref), custom_call_target="tpu_custom_call" | custom-call | tf_op jit(solution)/shard_map/adjoint_1/pallas_call | solution.py:269
  114.7 1.1 slice_bitcast_fusion
  115.8 0.1 collective-permute-start.2
  115.9 5.1 %collective-permute-start.3 = (f32[2,256,128]{2,1,0:T(8,128)S(1)}, f32[2,256,128]{2,1,0:T(8,128)S(1)}, u32[]{:S(2)}, u32[]{:S(2)}) collective-permute-start(f32[2,256,128]{2,1,0:T(8,128)S(1)} %get-tuple-element.24), channel_id=1, source_target_pairs={{0,112},{16,0},{32,16},{48,32},{64,48},{80,64},{96,80},{112,96},{1... | collective-permute-start | bytes 786440 | tf_op jit(solution)/shard_map/ppermute | solution.py:537
  120.9 10.0 %gram_apply.1.gram_ref = f32[2,8,256,128]{3,2,1,0:T(8,128)} custom-call(bf16[8,4,256,256]{3,2,1,0:T(8,128)(2,1)} %gram_tables.1.gram_ref, f32[16,4,16,256]{3,2,1,0:T(8,128)} %copy-done, f32[2,8,256,128]{3,2,1,0:T(8,128)} %adjoint_1.1.in_ref.first_ref), custom_call_target="tpu_custom_call" | custom-call | tf_op jit(solution)/shard_map/gram_apply/pallas_call | solution.py:292
  131.0 0.0 collective-permute-done.2.before_ref
  131.0 0.0 copy-start.4
  131.0 0.0 collective-permute-done.3.after_ref
  131.0 0.7 copy-done.4
  131.7 0.0 copy-start.5
  131.7 0.7 copy-done.5
  132.4 4.8 %normal.1 = (f32[2,8,256,128]{3,2,1,0:T(8,128)}, f32[2,256,128]{2,1,0:T(8,128)}, f32[16,4,16,128]{3,2,1,0:T(8,128)}, f32[4,8,128]{2,1,0:T(8,128)}) custom-call(f32[2,8,256,128]{3,2,1,0:T(8,128)} %adjoint_1.1.in_ref.first_ref, f32[2,8,256,128]{3,2,1,0:T(8,128)} %gram_apply.1.gram_ref, f32[2,256,128]{2,1,0:T(8,128)} %copy-done.4, f32[2,256,128]{2,1,0:T(8,128)} %copy-done.5), custom_call_target="tpu_custom_call" | custom-call | tf_op jit(solution)/shard_map/normal/pallas_call | solution.py:343
  137.2 6.3 %all-to-all-start.4 = ((f32[16,4,16,128]{3,2,1,0:T(8,128)}), f32[16,4,16,128]{3,2,1,0:T(8,128)S(1)}, u32[]{:S(2)}, u32[]{:S(2)}) async-start(f32[16,4,16,128]{3,2,1,0:T(8,128)} %get-tuple-element.17), calls=%async_computation.4 | async-start | bytes 1048576 | tf_op jit(solution)/shard_map/all_to_all | solution.py:541
  143.5 1.3 collective-permute-start.4
  144.8 8.3 %all-to-all-done.4.in_ref = f32[16,4,16,128]{3,2,1,0:T(8,128)S(1)} async-done(((f32[16,4,16,128]{3,2,1,0:T(8,128)}), f32[16,4,16,128]{3,2,1,0:T(8,128)S(1)}, u32[]{:S(2)}, u32[]{:S(2)}) %all-to-all-start.4) | async-done | bytes 524320 | tf_op jit(solution)/shard_map/all_to_all | solution.py:541
  153.2 0.0 copy-start.2
  153.2 0.8 copy-done.2
  154.0 2.6 %unpack.1 = (f32[4,8,16,256]{3,2,1,0:T(8,128)}, f32[4,16,256]{2,1,0:T(8,128)}) custom-call(f32[16,4,16,128]{3,2,1,0:T(8,128)} %copy-done.2), custom_call_target="tpu_custom_call" | custom-call | tf_op jit(solution)/shard_map/unpack/pallas_call | solution.py:442
  156.6 1.6 collective-permute-start.5
  158.2 6.8 %curvature.1.curve_ref = f32[8,128]{1,0:T(8,128)} custom-call(bf16[8,4,256,256]{3,2,1,0:T(8,128)(2,1)} %gram_tables.1.gram_ref, f32[16,4,16,256]{3,2,1,0:T(8,128)} %copy-done, f32[2,8,256,128]{3,2,1,0:T(8,128)} %get-tuple-element.15.in_ref.last_ref), custom_call_target="tpu_custom_call" | custom-call | tf_op jit(solution)/shard_map/curvature/pallas_call | solution.py:378
  165.0 0.0 collective-permute-done.4.after_ref
  165.0 0.0 copy-start.3
  165.0 0.7 copy-done.3
  165.7 1.8 share.1
  167.6 15.4 %all_to_all.30.shared_ref = f32[128,1,128]{2,1,0:T(1,128)} all-to-all(f32[128,1,128]{2,1,0:T(1,128)} %share.1), channel_id=1, replica_groups=mesh['phase'=8,'row'=16] {'phase','row'}, dimensions={0} | all-to-all | bytes 131072 | tf_op jit(solution)/shard_map/all_to_all | solution.py:541
  183.0 0.0 collective-permute-done.5.edge_ref
  183.0 0.0 copy-start.7
  183.0 0.6 copy-done.7
  183.6 2.6 %finish.1 = (f32[2,8,16,256]{3,2,1,0:T(8,128)}, f32[2,8,16,256]{3,2,1,0:T(8,128)}, f32[2,8,16,256]{3,2,1,0:T(8,128)}, f32[128,1,128]{2,1,0:T(1,128)}) custom-call(f32[128,1,128]{2,1,0:T(1,128)} %all_to_all.30.shared_ref, f32[2,8,16,256]{3,2,1,0:T(8,128)} %frames_ref.3, f32[2,8,16,256]{3,2,1,0:T(8,128)} %aux_ref.3, f32[2,8,16,256]{3,2,1,0:T(8,128)} %dual_ref.3, ...), custom_call_target="tpu_custom_call" | custom-call | tf_op jit(solution)/shard_map/finish/pallas_call | solution.py:505
  186.2 15.3 %all_to_all.31.in_ref = f32[128,1,128]{2,1,0:T(1,128)} all-to-all(f32[128,1,128]{2,1,0:T(1,128)} %get-tuple-element.23), channel_id=1, replica_groups=mesh['phase'=8,'row'=16] {'phase','row'}, dimensions={0} | all-to-all | bytes 131072 | tf_op jit(solution)/shard_map/all_to_all | solution.py:541
  201.4 1.6 norms.1
  203.0 1.2 slice_bitcast_fusion.2
  (1 shorter events, 0.0 us)
Async XLA Ops:
  1.5 8.3 %collective-permute-start.1 = (f32[2,1,16,256]{3,2,1,0:T(8,128)S(1)}, f32[2,1,16,256]{3,2,1,0:T(8,128)S(1)}, u32[]{:S(2)}, u32[]{:S(2)}) collective-permute-start(f32[2,1,16,256]{3,2,1,0:T(8,128)S(1)} %get-tuple-element.26), channel_id=1, source_target_pairs={{0,112},{16,0},{32,16},{48,32},{64,48},{80,64},{96,80},{112,96},{1... | collective-permute-start | bytes 98312 | tf_op jit(solution)/shard_map/ppermute | solution.py:537
  8.7 6.4 %collective-permute-start = (f32[2,1,16,256]{3,2,1,0:T(8,128)S(1)}, f32[2,1,16,256]{3,2,1,0:T(8,128)S(1)}, u32[]{:S(2)}, u32[]{:S(2)}) collective-permute-start(f32[2,1,16,256]{3,2,1,0:T(8,128)S(1)} %get-tuple-element.27), channel_id=1, source_target_pairs={{0,16},{16,32},{32,48},{48,64},{64,80},{80,96},{96,112},{112,0},{1... | collective-permute-start | bytes 98312 | tf_op jit(solution)/shard_map/ppermute | solution.py:537
  9.8 5.4 %copy-start.6 = (f32[2,1,16,256]{3,2,1,0:T(8,128)}, f32[2,1,16,256]{3,2,1,0:T(8,128)S(1)}, u32[]{:S(2)}) copy-start(f32[2,1,16,256]{3,2,1,0:T(8,128)S(1)} %collective-permute-done.1.after_ref) | copy-start | bytes 98308
  15.1 0.6 copy-start.8
  19.1 22.2 %all-to-all-start = ((f32[16,4,16,256]{3,2,1,0:T(8,128)}), f32[16,4,16,256]{3,2,1,0:T(8,128)S(1)}, u32[]{:S(2)}, u32[]{:S(2)}) async-start(f32[16,4,16,256]{3,2,1,0:T(8,128)} %pack_image.1), calls=%async_computation | async-start | bytes 2097152 | tf_op jit(solution)/shard_map/all_to_all | solution.py:541
  41.4 8.6 %copy-start = (f32[16,4,16,256]{3,2,1,0:T(8,128)}, f32[16,4,16,256]{3,2,1,0:T(8,128)S(1)}, u32[]{:S(2)}) copy-start(f32[16,4,16,256]{3,2,1,0:T(8,128)S(1)} %all-to-all-done.image_ref) | copy-start | bytes 3145732
  41.4 31.4 %all-to-all-start.2 = ((f32[16,128,256]{2,1,0:T(8,128)}), f32[16,128,256]{2,1,0:T(8,128)S(1)}, u32[]{:S(2)}, u32[]{:S(2)}) async-start(f32[16,128,256]{2,1,0:T(8,128)} %pack_measured_0.1), calls=%async_computation.2 | async-start | bytes 4194304 | tf_op jit(solution)/shard_map/all_to_all | solution.py:541
  49.9 28.4 %copy-start.9 = (s32[8,256]{1,0:T(8,128)S(1)}, s32[8,256]{1,0:T(8,128)}, u32[]{:S(2)}) copy-start(s32[8,256]{1,0:T(8,128)} %param.12) | copy-start | bytes 24580
  72.8 5.5 %copy-start.1 = (f32[16,128,256]{2,1,0:T(8,128)}, f32[16,128,256]{2,1,0:T(8,128)S(1)}, u32[]{:S(2)}) copy-start(f32[16,128,256]{2,1,0:T(8,128)S(1)} %all-to-all-done.2.lines_ref) | copy-start | bytes 6291460
  72.8 33.2 %all-to-all-start.1 = ((f32[16,128,256]{2,1,0:T(8,128)}), f32[16,128,256]{2,1,0:T(8,128)}, u32[]{:S(2)}, u32[]{:S(2)}) async-start(f32[16,128,256]{2,1,0:T(8,128)} %pack_measured_1.1), calls=%async_computation.1 | async-start | bytes 4194304 | tf_op jit(solution)/shard_map/all_to_all | solution.py:541
  115.8 15.2 %collective-permute-start.2 = (f32[2,256,128]{2,1,0:T(8,128)S(1)}, f32[2,256,128]{2,1,0:T(8,128)S(1)}, u32[]{:S(2)}, u32[]{:S(2)}) collective-permute-start(f32[2,256,128]{2,1,0:T(8,128)S(1)} %get-tuple-element.25), channel_id=1, source_target_pairs={{0,16},{16,32},{32,48},{48,64},{64,80},{80,96},{96,112},{112,0},{1... | collective-permute-start | bytes 786440 | tf_op jit(solution)/shard_map/ppermute | solution.py:537
  115.9 15.1 %collective-permute-start.3 = (f32[2,256,128]{2,1,0:T(8,128)S(1)}, f32[2,256,128]{2,1,0:T(8,128)S(1)}, u32[]{:S(2)}, u32[]{:S(2)}) collective-permute-start(f32[2,256,128]{2,1,0:T(8,128)S(1)} %get-tuple-element.24), channel_id=1, source_target_pairs={{0,112},{16,0},{32,16},{48,32},{64,48},{80,64},{96,80},{112,96},{1... | collective-permute-start | bytes 786440 | tf_op jit(solution)/shard_map/ppermute | solution.py:537
  131.0 0.7 copy-start.4
  131.7 0.7 copy-start.5
  137.2 15.9 %all-to-all-start.4 = ((f32[16,4,16,128]{3,2,1,0:T(8,128)}), f32[16,4,16,128]{3,2,1,0:T(8,128)S(1)}, u32[]{:S(2)}, u32[]{:S(2)}) async-start(f32[16,4,16,128]{3,2,1,0:T(8,128)} %get-tuple-element.17), calls=%async_computation.4 | async-start | bytes 1048576 | tf_op jit(solution)/shard_map/all_to_all | solution.py:541
  143.5 21.5 %collective-permute-start.4 = (f32[2,256,128]{2,1,0:T(8,128)}, f32[2,256,128]{2,1,0:T(8,128)S(1)}, u32[]{:S(2)}, u32[]{:S(2)}) collective-permute-start(f32[2,256,128]{2,1,0:T(8,128)} %get-tuple-element.16), channel_id=1, source_target_pairs={{0,112},{16,0},{32,16},{48,32},{64,48},{80,64},{96,80},{112,96},{1... | collective-permute-start | bytes 786440 | tf_op jit(solution)/shard_map/ppermute | solution.py:537
  153.2 0.8 copy-start.2
  156.6 26.4 %collective-permute-start.5 = (f32[4,16,256]{2,1,0:T(8,128)}, f32[4,16,256]{2,1,0:T(8,128)S(1)}, u32[]{:S(2)}, u32[]{:S(2)}) collective-permute-start(f32[4,16,256]{2,1,0:T(8,128)} %get-tuple-element.19), channel_id=1, source_target_pairs={{0,112},{16,0},{32,16},{48,32},{64,48},{80,64},{96,80},{112,96},{1... | collective-permute-start | bytes 196616 | tf_op jit(solution)/shard_map/ppermute | solution.py:537
  165.0 0.7 copy-start.3
  183.0 0.6 copy-start.7

commit v2 on v1

v2 whole, which is shorter than its diff:
```python
import functools
import math

import jax
import jax.numpy as jnp
import numpy as np
from jax import lax
from jax.experimental import pallas as pl
from jax.experimental.pallas import tpu as pltpu
from jax.sharding import PartitionSpec as P

PENALTY = 0.5
DAMPING = 0.1
THRESHOLD = 1.0

COILS = 16
PHASES = 8
ROWS = 16
SIZE = 256
LANES = 128
GROUP = 16
FOLD = 32
LINES = PHASES * ROWS
MAIN = 88
EXTRA = LINES - MAIN
IMAGE = 4 * ROWS
ROW_SHARDS = 16
PHASE_SHARDS = 8
ALL = ROW_SHARDS * PHASE_SHARDS

F32 = jnp.float32
BF16 = jnp.bfloat16


def lane_bit(rows, bit):
    lane = lax.broadcasted_iota(jnp.int32, (rows, LANES), 1)
    return (lane & (GROUP << bit)) != 0


def lane_group(rows):
    return lax.broadcasted_iota(jnp.int32, (rows, LANES), 1) // GROUP


def roll(value, groups):
    groups %= 8
    if groups == 0:
        return value
    return pltpu.roll(value, groups * GROUP, 1)


def gather_coils(halves):
    rows = halves[0][0].shape[0]
    lane = lax.broadcasted_iota(jnp.int32, (rows, LANES), 1)
    turned = []
    for c, (low, high) in enumerate(halves):
        if c >= 8:
            low, high = high, low
        shift = c % 8
        if shift:
            low, high = roll(low, shift), roll(high, shift)
            wrapped = lane < shift * GROUP
            low, high = jnp.where(wrapped, high, low), jnp.where(wrapped, low, high)
        turned.append((low, high))
    for bit in range(3):
        mask = lane_bit(rows, bit)
        turned = [
            tuple(jnp.where(mask, turned[(i + (1 << bit)) % 16][h], turned[i][h]) for h in range(2))
            for i in range(16)
        ]
    turned = [(turned[i][0], turned[(i + 8) % 16][1]) for i in range(16)]
    return [turned[(-j) % 16] for j in range(16)]


def transpose_groups(values):
    rows = values[0].shape[0]
    turned = [roll(value, a) for a, value in enumerate(values)]
    for bit in range(3):
        mask = lane_bit(rows, bit)
        turned = [jnp.where(mask, turned[(i + (1 << bit)) % 8], turned[i]) for i in range(8)]
    return [roll(turned[(-b) % 8], -b) for b in range(8)]


def spread_half(value, half):
    rows = value.shape[0]
    turned = pltpu.roll(value, 4 * GROUP, 1)
    low = ~lane_bit(rows, 2)
    values = [jnp.where(low == (half == 0), value, turned)]
    for bit in (1, 0):
        low = ~lane_bit(rows, bit)
        spread = []
        for value in values:
            turned = pltpu.roll(value, GROUP << bit, 1)
            spread += [jnp.where(low, value, turned), jnp.where(low, turned, value)]
        values = spread
    return values


def sum_four(values):
    rows = values[0].shape[0]
    for bit in range(2):
        low = ~lane_bit(rows, bit)
        values = [
            jnp.where(low, a, b) + pltpu.roll(jnp.where(low, b, a), GROUP << bit, 1)
            for a, b in zip(values[::2], values[1::2])
        ]
    return values[0] + pltpu.roll(values[0], 4 * GROUP, 1)


def fold_phase(value, phase):
    group = lane_group(FOLD)
    out = None
    for i in range(8):
        piece = roll(value[i * FOLD : (i + 1) * FOLD], i - phase)
        out = piece if out is None else jnp.where(group == i, piece, out)
    return out


def unfold_phase(value, phase, i):
    return roll(value, phase - i)


def split(value):
    high = value.astype(BF16)
    return high, (value - high.astype(F32)).astype(BF16)


def dot(a, b):
    return jnp.dot(a, b, preferred_element_type=F32)


def dot3(table, value):
    return dot(table[0], value[0]) + (dot(table[0], value[1]) + dot(table[1], value[0]))


def wide(value):
    return jnp.concatenate([value, value], 1)


def images_of(maps_ref, at, real, imag):
    maps_real, maps_imag = maps_at(maps_ref, at)
    real, imag = wide(real), wide(imag)
    return maps_real * real - maps_imag * imag, maps_real * imag + maps_imag * real


def maps_at(maps_ref, at):
    return maps_ref[0, at], maps_ref[1, at]


def combine(maps_real, maps_imag, real, imag):
    out_real = maps_real * real + maps_imag * imag
    out_imag = maps_real * imag - maps_imag * real
    return out_real[:, :LANES] + out_real[:, LANES:], out_imag[:, :LANES] + out_imag[:, LANES:]


def chunks(step):
    return [slice(row, row + step) for row in range(0, SIZE, step)]


def store_split(ref, which, at, value):
    ref[which, at], ref[which + 1, at] = split(value)


def expand(vector_ref, maps_ref, pieces):
    half = pl.program_id(0)
    for at in chunks(32):
        real = spread_half(vector_ref[0, at], half)
        imag = spread_half(vector_ref[1, at], half)
        for t in range(4):
            image_real, image_imag = images_of(maps_ref, at, real[t], imag[t])
            store_split(pieces[t], 0, at, image_real)
            store_split(pieces[t], 2, at, image_imag)


def reduce(maps_ref, backs, finish):
    for at in chunks(32):
        maps = maps_at(maps_ref, at)
        terms = [combine(*maps, backs[t][0, at], backs[t][1, at]) for t in range(4)]
        finish(at, sum_four([term[0] for term in terms]), sum_four([term[1] for term in terms]))


def gram_products(gram_ref, pieces, backs):
    for t in range(4):
        real_high, real_low, imag_high, imag_low = (pieces[t][i] for i in range(4))
        table_real, table_imag, low_real, low_imag = (gram_ref[t, i] for i in range(4))
        backs[t][0] = (
            dot(table_real, real_high) + dot(table_real, real_low) + dot(low_real, real_high)
        ) - (dot(table_imag, imag_high) + dot(table_imag, imag_low) + dot(low_imag, imag_high))
        backs[t][1] = (
            dot(table_real, imag_high) + dot(table_real, imag_low) + dot(low_real, imag_high)
        ) + (dot(table_imag, real_high) + dot(table_imag, real_low) + dot(low_imag, real_high))


def in_step(rows):
    return lane_bit(rows, 2) == (pl.program_id(0) == 1)


def split_three(value):
    high = value.astype(BF16)
    value = value - high.astype(F32)
    middle = value.astype(BF16)
    return high, middle, (value - middle.astype(F32)).astype(BF16)


def compact(weight_ref, in_ref, lines_ref, base):
    count = lines_ref.shape[1]
    weight = jnp.broadcast_to(weight_ref[...], (8, LINES))
    row = lax.broadcasted_iota(jnp.int32, (LINES, LINES), 0)
    col = lax.broadcasted_iota(jnp.int32, (LINES, LINES), 1)
    upto = jnp.where(row <= col, 1.0, 0.0).astype(BF16)
    number = dot(weight.astype(BF16), upto).astype(jnp.int32)
    number = jnp.broadcast_to(number[:1], (count, LINES))
    acquired = jnp.broadcast_to(weight_ref[...], (count, LINES)) > 0.5
    line = lax.broadcasted_iota(jnp.int32, (count, LINES), 0) + (base + 1)
    select = jnp.where((number == line) & acquired, 1.0, 0.0).astype(BF16)
    step = in_ref.shape[0]
    for c in range(step):
        high, middle, low = split_three(in_ref[c, 0])
        lines_ref[pl.program_id(0) * step + c] = (
            dot(select, high) + dot(select, middle) + dot(select, low)
        )


def pack_lines(lines_ref, out_ref, start):
    for row in range(0, lines_ref.shape[1], 8):
        at = slice(row, row + 8)
        to = slice(start + row, start + row + 8)
        halves = [(lines_ref[c, at, :LANES], lines_ref[c, at, LANES:]) for c in range(COILS)]
        for j, (low, high) in enumerate(gather_coils(halves)):
            out_ref[j, to, :LANES] = low
            out_ref[j, to, LANES:] = high


def pack_image(maps_ref, frames_ref, aux_ref, dual_ref, out_ref):
    for part in range(2):
        for row in range(0, ROWS, 8):
            at = slice(row, row + 8)
            halves = [
                (maps_ref[c, part, at, :LANES], maps_ref[c, part, at, LANES:]) for c in range(COILS)
            ]
            to = slice(part * ROWS + row, part * ROWS + row + 8)
            for j, (low, high) in enumerate(gather_coils(halves)):
                out_ref[j, to, :LANES] = low
                out_ref[j, to, LANES:] = high
            for half in range(2):
                cols = slice(half * LANES, (half + 1) * LANES)
                frames = [frames_ref[part, t, at, cols] for t in range(PHASES)]
                splits = [
                    aux_ref[part, t, at, cols] - dual_ref[part, t, at, cols] for t in range(PHASES)
                ]
                lanes = slice(part * LANES, (part + 1) * LANES)
                for which, values in ((2, frames), (3, splits)):
                    to = slice(which * ROWS + row, which * ROWS + row + 8)
                    for jj, value in enumerate(transpose_groups(values)):
                        out_ref[half * 8 + jj, to, lanes] = value


def pack_first_kernel(
    weight_ref, in_ref, maps_ref, frames_ref, aux_ref, dual_ref, out_ref, lines_ref
):
    compact(weight_ref, in_ref, lines_ref, 0)

    @pl.when(pl.program_id(0) == pl.num_programs(0) - 1)
    def _():
        pack_image(maps_ref, frames_ref, aux_ref, dual_ref, out_ref)
        pack_lines(lines_ref, out_ref, IMAGE)


def whole_spec(value):
    return pl.BlockSpec(value.shape, lambda *_: (0,) * value.ndim)


def pack_first(weight, measured, *images):
    step = 4
    return pl.pallas_call(
        pack_first_kernel,
        grid=(COILS // step,),
        in_specs=[
            whole_spec(weight),
            pl.BlockSpec((step, 1, LINES, SIZE), lambda i: (i, 0, 0, 0)),
            *(whole_spec(value) for value in images),
        ],
        out_specs=pl.BlockSpec((ROW_SHARDS, IMAGE + MAIN, SIZE), lambda i: (0, 0, 0)),
        out_shape=jax.ShapeDtypeStruct((ROW_SHARDS, IMAGE + MAIN, SIZE), F32),
        scratch_shapes=[pltpu.VMEM((COILS, MAIN, SIZE), F32)],
        compiler_params=params(),
        name="pack_first",
    )(weight, measured, *images)


def pack_more_kernel(base, weight_ref, in_ref, out_ref, lines_ref):
    compact(weight_ref, in_ref, lines_ref, base)

    @pl.when(pl.program_id(0) == pl.num_programs(0) - 1)
    def _():
        pack_lines(lines_ref, out_ref, 0)


def pack_more(weight, measured, part, base, count):
    step = 4
    return pl.pallas_call(
        functools.partial(pack_more_kernel, base),
        grid=(COILS // step,),
        in_specs=[
            whole_spec(weight),
            pl.BlockSpec((step, 1, LINES, SIZE), lambda i: (i, part, 0, 0)),
        ],
        out_specs=pl.BlockSpec((ROW_SHARDS, count, SIZE), lambda i: (0, 0, 0)),
        out_shape=jax.ShapeDtypeStruct((ROW_SHARDS, count, SIZE), F32),
        scratch_shapes=[pltpu.VMEM((COILS, count, SIZE), F32)],
        compiler_params=params(),
        name=f"pack_more_{part}_{base}",
    )(weight, measured)


def line_table_kernel(index_ref, tables_ref, out_ref):
    row = lax.broadcasted_iota(jnp.int32, (SIZE, SIZE), 0)
    select = jnp.where(row == index_ref[0], 1.0, 0.0).astype(BF16)
    for i in range(4):
        out_ref[0, i] = dot(tables_ref[i], select).astype(BF16)


def line_tables(index, tables):
    return pl.pallas_call(
        line_table_kernel,
        grid=(PHASES,),
        in_specs=[pl.BlockSpec((1, 1, SIZE), lambda t: (t, 0, 0)), whole_spec(tables)],
        out_specs=pl.BlockSpec((1, 4, SIZE, SIZE), lambda t: (t, 0, 0, 0)),
        out_shape=jax.ShapeDtypeStruct((PHASES, 4, SIZE, SIZE), BF16),
        name="line_tables",
    )(index, tables)


def receive_kernel(image_ref, maps_ref, frames_ref, splits_ref, first_ref, last_ref):
    for part in range(2):
        lanes = slice(part * LANES, (part + 1) * LANES)
        for block in range(ROW_SHARDS):
            at = slice(block * ROWS, (block + 1) * ROWS)
            maps_ref[part, at] = image_ref[block, part * ROWS : (part + 1) * ROWS]
            frames_ref[part, at] = image_ref[block, 2 * ROWS : 3 * ROWS, lanes]
            splits_ref[part, at] = image_ref[block, 3 * ROWS : 4 * ROWS, lanes]
        first_ref[part] = fold_phase(frames_ref[part], 0)
        last_ref[part] = fold_phase(frames_ref[part] + splits_ref[part], PHASES - 1)


def receive(image):
    return pl.pallas_call(
        receive_kernel,
        grid=(1,),
        in_specs=[IMAGE_SPEC],
        out_specs=[MAPS_SPEC, VECTOR_SPEC, VECTOR_SPEC, FOLDED_SPEC, FOLDED_SPEC],
        out_shape=[jax.ShapeDtypeStruct((2, SIZE, SIZE), F32), VECTOR, VECTOR, FOLDED, FOLDED],
        name="receive",
    )(image)


def gram_table_kernel(weight_ref, tables_ref, out_ref):
    weight = weight_ref[0]
    cos_high, cos_low, sin_high, sin_low = (tables_ref[i] for i in range(4))

    def scaled(table):
        return (table.astype(F32) * weight).astype(BF16)

    cos_w = scaled(cos_high), scaled(cos_low)
    sin_w = scaled(sin_high), scaled(sin_low)
    cos, sin = (cos_high, cos_low), (sin_high, sin_low)
    real = dot3(cos_w, cos) + dot3(sin_w, sin)
    imag = dot3(sin_w, cos) - dot3(cos_w, sin)
    out_ref[0, 0], out_ref[0, 2] = split(real)
    out_ref[0, 1], out_ref[0, 3] = split(imag)


def gram_tables(weight, tables):
    return pl.pallas_call(
        gram_table_kernel,
        grid=(PHASES,),
        in_specs=[
            pl.BlockSpec((1, 1, SIZE), lambda t: (t, 0, 0)),
            pl.BlockSpec((4, SIZE, SIZE), lambda t: (0, 0, 0)),
        ],
        out_specs=pl.BlockSpec((1, 4, SIZE, SIZE), lambda t: (t, 0, 0, 0)),
        out_shape=jax.ShapeDtypeStruct((PHASES, 4, SIZE, SIZE), BF16),
        name="gram_tables",
    )(weight, tables)


GRAM_SPEC = pl.BlockSpec((4, 4, SIZE, SIZE), lambda i, *_: (i, 0, 0, 0))
IMAGE_SPEC = pl.BlockSpec((ROW_SHARDS, IMAGE, SIZE), lambda *_: (0, 0, 0))
MAPS_SPEC = pl.BlockSpec((2, SIZE, SIZE), lambda *_: (0, 0, 0))
VECTOR_SPEC = pl.BlockSpec((2, SIZE, LANES), lambda *_: (0, 0, 0))
VECTOR = jax.ShapeDtypeStruct((2, SIZE, LANES), F32)
FOLDED_SPEC = pl.BlockSpec((2, FOLD, LANES), lambda *_: (0, 0, 0))
FOLDED = jax.ShapeDtypeStruct((2, FOLD, LANES), F32)
SUMS_SPEC = pl.BlockSpec((4, 8, LANES), lambda i: (0, 0, 0))
PIECES = [pltpu.VMEM((4, SIZE, SIZE), BF16)] * 4
BACKS = [pltpu.VMEM((2, SIZE, SIZE), F32)] * 4


def params():
    return pltpu.CompilerParams(vmem_limit_bytes=48 << 20)


def start_kernel(
    gram_ref, maps_ref, frames_ref, splits_ref, before_ref, after_ref, in_ref, out_ref, *scratch
):
    pieces, backs = scratch[:4], scratch[4:]

    @pl.when(pl.program_id(0) == 0)
    def _():
        group = lane_group(FOLD)
        for i in range(8):
            at = slice(i * FOLD, (i + 1) * FOLD)
            for part in range(2):
                frames, splits = frames_ref[part, at], splits_ref[part, at]
                ahead = jnp.where(
                    group == PHASES - 1,
                    unfold_phase(after_ref[part], PHASES - 1, i),
                    pltpu.roll(frames, LANES - GROUP, 1),
                )
                behind = jnp.where(
                    group == 0,
                    unfold_phase(before_ref[part], 0, i),
                    pltpu.roll(frames + splits, GROUP, 1),
                )
                gap = splits - (ahead - frames)
                gap_behind = behind - frames
                out_ref[part, at] = (
                    in_ref[part, at] + PENALTY * (gap_behind - gap) - DAMPING * frames
                )

    expand(frames_ref, maps_ref, pieces)
    gram_products(gram_ref, pieces, backs)

    def finish(at, real, imag):
        keep = in_step(at.stop - at.start)
        for part, value in enumerate((real, imag)):
            out_ref[part, at] -= jnp.where(keep, value, 0.0)

    reduce(maps_ref, backs, finish)


def start(grams, maps, frames, splits, before, after, so_far):
    return pl.pallas_call(
        start_kernel,
        grid=(2,),
        in_specs=[GRAM_SPEC, MAPS_SPEC] + [VECTOR_SPEC] * 2 + [FOLDED_SPEC] * 2 + [VECTOR_SPEC],
        out_specs=VECTOR_SPEC,
        out_shape=VECTOR,
        scratch_shapes=PIECES + BACKS,
        compiler_params=params(),
        name="start",
    )(grams, maps, frames, splits, before, after, so_far)


def adjoint_kernel(
    part, base, window_ref, tables_ref, maps_ref, lines_ref, in_ref, out_ref, first_ref, last_ref, *scratch
):
    pieces, backs = scratch[:4], scratch[4:]
    half = pl.program_id(0)
    count = lines_ref.shape[1] - base

    @pl.when(half == 0)
    def _():
        out_ref[...] = in_ref[...]

    for t in range(4):
        for block in range(ROW_SHARDS):
            at = slice(block * ROWS, (block + 1) * ROWS)
            start = window_ref[(half * 4 + t) * ROW_SHARDS + block]
            aligned = jnp.minimum(start // 8, (count - ROWS) // 8 - 1) * 8
            rows = lines_ref[block, pl.ds(pl.multiple_of(base + aligned, 8), ROWS + 8)]
            rows = pltpu.roll(rows, lax.rem(ROWS + 8 - (start - aligned), ROWS + 8), 0)
            store_split(pieces[t], 0, at, rows[:ROWS])
        high, low = pieces[t][0], pieces[t][1]
        cos, cos_low, sin, sin_low = (tables_ref[t, i] for i in range(4))
        by_cos = dot(cos, high) + dot(cos, low) + dot(cos_low, high)
        by_sin = dot(sin, high) + dot(sin, low) + dot(sin_low, high)
        backs[t][0], backs[t][1] = (by_cos, by_sin) if part == 0 else (-by_sin, by_cos)

    def finish(at, real, imag):
        keep = in_step(at.stop - at.start)
        for which, value in enumerate((real, imag)):
            out_ref[which, at] += jnp.where(keep, value, 0.0)

    reduce(maps_ref, backs, finish)

    @pl.when(half == 1)
    def _():
        for which in range(2):
            value = out_ref[which]
            first_ref[which] = fold_phase(value, 0)
            last_ref[which] = fold_phase(value, PHASES - 1)


def adjoint(part, base, window, tables, maps, lines, so_far):
    return pl.pallas_call(
        functools.partial(adjoint_kernel, part, base),
        grid_spec=pltpu.PrefetchScalarGridSpec(
            num_scalar_prefetch=1,
            grid=(2,),
            in_specs=[GRAM_SPEC, MAPS_SPEC, whole_spec(lines), VECTOR_SPEC],
            out_specs=[VECTOR_SPEC, FOLDED_SPEC, FOLDED_SPEC],
            scratch_shapes=PIECES + BACKS,
        ),
        out_shape=[VECTOR, FOLDED, FOLDED],
        compiler_params=params(),
        name=f"adjoint_{part}_{base}",
    )(window, tables, maps, lines, so_far)


def gram_kernel(gram_ref, maps_ref, in_ref, out_ref, *scratch):
    pieces, backs = scratch[:4], scratch[4:]
    expand(in_ref, maps_ref, pieces)
    gram_products(gram_ref, pieces, backs)

    @pl.when(pl.program_id(0) == 0)
    def _():
        out_ref[...] = jnp.zeros_like(out_ref)

    def finish(at, real, imag):
        keep = in_step(at.stop - at.start)
        for part, value in enumerate((real, imag)):
            out_ref[part, at] += jnp.where(keep, value, 0.0)

    reduce(maps_ref, backs, finish)


def gram_apply(grams, maps, vector):
    return pl.pallas_call(
        gram_kernel,
        grid=(2,),
        in_specs=[GRAM_SPEC, MAPS_SPEC, VECTOR_SPEC],
        out_specs=VECTOR_SPEC,
        out_shape=VECTOR,
        scratch_shapes=PIECES + BACKS,
        compiler_params=params(),
        name="gram_apply",
    )(grams, maps, vector)


def fold(value):
    return jnp.sum(value.reshape(-1, 8, LANES), 0)


def normal_kernel(
    first_ref, gram_ref, before_ref, after_ref, image_ref, first_edge_ref, last_edge_ref, sums_ref
):
    rr = rw = ww = dd = 0.0
    group = lane_group(FOLD)
    for part in range(2):
        for i in range(8):
            at = slice(i * FOLD, (i + 1) * FOLD)
            value = first_ref[part, at]
            behind = jnp.where(
                group == 0, unfold_phase(before_ref[part], 0, i), pltpu.roll(value, GROUP, 1)
            )
            ahead = jnp.where(
                group == PHASES - 1,
                unfold_phase(after_ref[part], PHASES - 1, i),
                pltpu.roll(value, LANES - GROUP, 1),
            )
            image = (
                gram_ref[part, at]
                + PENALTY * ((value - behind) - (ahead - value))
                + DAMPING * value
            )
            image_ref[part, at] = image
            rr += fold(value * value)
            rw += fold(value * image)
            ww += fold(image * image)
            step = pltpu.roll(image, LANES - GROUP, 1) - image
            dd += fold(jnp.where(group == PHASES - 1, 0.0, step * step))
        whole = image_ref[part]
        first_edge_ref[part] = fold_phase(whole, 0)
        last_edge_ref[part] = fold_phase(whole, PHASES - 1)
    for i, value in enumerate((rr, rw, ww, dd)):
        sums_ref[i] = value


def normal(first, grams_first, before, after):
    return pl.pallas_call(
        normal_kernel,
        out_shape=[
            VECTOR,
            FOLDED,
            FOLDED,
            jax.ShapeDtypeStruct((4, 8, LANES), F32),
        ],
        name="normal",
    )(first, grams_first, before, after)


def curvature_kernel(gram_ref, maps_ref, in_ref, out_ref, *scratch):
    pieces, backs = scratch[:4], scratch[4:]
    half = pl.program_id(0)

    @pl.when(half == 0)
    def _():
        out_ref[...] = jnp.zeros_like(out_ref)

    for at in chunks(32):
        real = spread_half(in_ref[0, at], half)
        imag = spread_half(in_ref[1, at], half)
        for t in range(4):
            for which, value in enumerate(images_of(maps_ref, at, real[t], imag[t])):
                pieces[t][which, at] = value.astype(BF16)
    for t in range(4):
        table_real, table_imag = gram_ref[t, 0], gram_ref[t, 1]
        real, imag = pieces[t][0], pieces[t][1]
        backs[t][0] = dot(table_real, real) - dot(table_imag, imag)
        backs[t][1] = dot(table_real, imag) + dot(table_imag, real)
    total = 0.0
    for at in chunks(32):
        for t in range(4):
            both = pieces[t][0, at].astype(F32) * backs[t][0, at] + pieces[t][1, at].astype(
                F32
            ) * backs[t][1, at]
            total += fold(both[:, :LANES] + both[:, LANES:])
    out_ref[...] += total


def curvature(grams, maps, vector):
    return pl.pallas_call(
        curvature_kernel,
        grid=(2,),
        in_specs=[pl.BlockSpec((4, 2, SIZE, SIZE), lambda i: (i, 0, 0, 0)), MAPS_SPEC, VECTOR_SPEC],
        out_specs=pl.BlockSpec((8, LANES), lambda i: (0, 0)),
        out_shape=jax.ShapeDtypeStruct((8, LANES), F32),
        scratch_shapes=[pltpu.VMEM((2, SIZE, SIZE), BF16)] * 4 + BACKS,
        compiler_params=params(),
        name="curvature",
    )(grams, maps, vector)


def lane_row(values):
    lane = lax.broadcasted_iota(jnp.int32, (1, LANES), 1)
    row = jnp.zeros((1, LANES), F32)
    for i, value in enumerate(values):
        row = jnp.where(lane == i, value, row)
    return row


def whole_sum(value):
    return jnp.sum(jnp.sum(value, 0, keepdims=True), 1, keepdims=True)


def share_kernel(sums_ref, curve_ref, last_ref, after_ref, out_ref):
    rr, rw, ww, dd = (whole_sum(sums_ref[i]) for i in range(4))
    edge = 0.0
    for part in range(2):
        step = after_ref[part] - last_ref[part]
        edge = edge + fold(step * step)
    curve = whole_sum(curve_ref[...]) + PENALTY * (dd + whole_sum(edge)) + DAMPING * ww
    row = lane_row((rr, rw, ww, curve))
    out_ref[...] = jnp.broadcast_to(row[None], out_ref.shape)


def share(sums, curve, last, after):
    return pl.pallas_call(
        share_kernel, out_shape=jax.ShapeDtypeStruct((ALL, 1, LANES), F32), name="share"
    )(sums, curve, last, after)


def solve_kernel(
    shared_ref, frames_ref, residual_ref, product_ref, frames_after_ref, residual_after_ref, product_after_ref, out_ref
):
    row = jnp.sum(shared_ref[...], 0)
    rr, rw, ww, curve = (row[:, i : i + 1] for i in range(4))
    alpha = rr / rw
    fresh = rr - 2.0 * alpha * rw + alpha * alpha * ww
    beta = fresh / rr
    gamma = 1.0 + beta
    bend = gamma * gamma * rw - 2.0 * gamma * alpha * ww + alpha * alpha * curve
    second = fresh / bend
    by_first = alpha + second * gamma
    by_image = -second * alpha
    group = lane_group(ROWS)
    for j in range(ROW_SHARDS):
        at = slice(j * ROWS, (j + 1) * ROWS)
        piece, half = j // 2, slice(j % 2 * ROWS, (j % 2 + 1) * ROWS)
        edge = []
        for part in range(2):
            out_ref[j, part] = (
                frames_ref[part, at]
                + by_first * residual_ref[part, at]
                + by_image * product_ref[part, at]
            )
            after = (
                frames_after_ref[part, half]
                + by_first * residual_after_ref[part, half]
                + by_image * product_after_ref[part, half]
            )
            edge.append(roll(after, part - piece))
        out_ref[j, 2] = jnp.where(group == 0, edge[0], edge[1])


def solve(shared, frames, residual, product, frames_after, residual_after, product_after):
    return pl.pallas_call(
        solve_kernel,
        out_shape=jax.ShapeDtypeStruct((ROW_SHARDS, 3, ROWS, LANES), F32),
        name="solve",
    )(shared, frames, residual, product, frames_after, residual_after, product_after)


def finish_kernel(in_ref, aux_ref, dual_ref, x_ref, new_aux_ref, new_dual_ref, out_ref):
    primal = dual_sum = 0.0
    group = lane_group(8)
    for row in range(0, ROWS, 8):
        at = slice(row, row + 8)
        for half in range(2):
            cols = slice(half * LANES, (half + 1) * LANES)
            parts = []
            for part in range(2):
                blocks = [in_ref[half * 8 + jj, part, at] for jj in range(8)]
                values = transpose_groups(blocks)
                after = None
                for jj in range(8):
                    piece = roll(in_ref[half * 8 + jj, 2, at], jj - part)
                    after = piece if after is None else jnp.where(group == jj, piece, after)
                for t in range(PHASES):
                    x_ref[part, t, at, cols] = values[t]
                parts.append(values + [after])
            for t in range(PHASES):
                dual = [dual_ref[part, t, at, cols] for part in range(2)]
                shifted = [parts[part][t + 1] - parts[part][t] + dual[part] for part in range(2)]
                magnitude = jnp.sqrt(shifted[0] * shifted[0] + shifted[1] * shifted[1])
                factor = jnp.maximum(magnitude - THRESHOLD, 0.0) / jnp.maximum(magnitude, THRESHOLD)
                for part in range(2):
                    new_aux = shifted[part] * factor
                    new_dual = shifted[part] - new_aux
                    new_aux_ref[part, t, at, cols] = new_aux
                    new_dual_ref[part, t, at, cols] = new_dual
                    gap = new_dual - dual[part]
                    primal += gap * gap
                    gap = new_aux - aux_ref[part, t, at, cols]
                    dual_sum += gap * gap
    sums = lane_row((whole_sum(primal), whole_sum(dual_sum)))
    out_ref[...] = jnp.broadcast_to(sums[None], out_ref.shape)


def finish(back, auxiliary, scaled_dual):
    image = jax.ShapeDtypeStruct((2, PHASES, ROWS, SIZE), F32)
    return pl.pallas_call(
        finish_kernel,
        out_shape=[image, image, image, jax.ShapeDtypeStruct((ALL, 1, LANES), F32)],
        name="finish",
    )(back, auxiliary, scaled_dual)


def tables():
    index = np.arange(SIZE)
    angle = (index[:, None] * index[None, :] % SIZE) * (2.0 * math.pi / SIZE)
    out = []
    for table in (np.cos(angle), np.sin(angle)):
        table = (table / math.sqrt(SIZE)).astype(np.float32)
        high = table.astype(BF16)
        out += [high, (table - high.astype(np.float32)).astype(BF16)]
    return np.stack(out)


def shift(value, steps):
    pairs = [(i, (i + steps) % PHASE_SHARDS) for i in range(PHASE_SHARDS)]
    return lax.ppermute(value, "phase", pairs)


def exchange(value, axes):
    return lax.all_to_all(value, axes, 0, 0, tiled=True)


def windows(number, acquired, base, count):
    before = number[:, :, :1] - acquired[:, :, :1] - base
    window = jnp.clip(before, 0, count - ROWS)
    place = lax.broadcasted_iota(jnp.int32, (1, 1, 1, ROWS), 3)
    match = (acquired > 0)[..., None] & (number[..., None] - (1 + base) == window[..., None] + place)
    match = match & (number[..., None] > base) & (number[..., None] <= base + count)
    k = lax.broadcasted_iota(jnp.int32, (1, ROW_SHARDS, ROWS, 1), 1) * ROWS
    k = k + lax.broadcasted_iota(jnp.int32, (1, ROW_SHARDS, ROWS, 1), 2)
    index = jnp.sum(jnp.where(match, k + 1, 0), 2) - 1
    return window.reshape(PHASES * ROW_SHARDS), index.reshape(PHASES, 1, SIZE)


def in_hbm(value):
    return pltpu.with_memory_space_constraint(value, pltpu.HBM)


def local(frames, auxiliary, scaled_dual, coil_maps, measured, sampling):
    table = jnp.asarray(tables())
    lines = measured.reshape(COILS, 2, LINES, SIZE)
    own = lax.dynamic_slice_in_dim(sampling, lax.axis_index("row") * ROWS, ROWS, 1)
    own = own.astype(F32).reshape(1, LINES)

    packed = pack_first(own, lines, *(in_hbm(v) for v in (coil_maps, frames, auxiliary, scaled_dual)))
    image = exchange(packed, "row")
    lines, own, late_sampling, packed = lax.optimization_barrier((lines, own, sampling, packed))
    packed = pack_more(own, lines, 1, 0, MAIN)
    late_sampling, packed = lax.optimization_barrier((late_sampling, packed))
    grams = in_hbm(gram_tables(late_sampling.astype(F32)[:, None, :], table))

    acquired = late_sampling.reshape(PHASES, ROW_SHARDS, ROWS)
    by_phase = jnp.sum(acquired, 2, keepdims=True)
    number = jnp.cumsum(acquired, 2) + jnp.cumsum(by_phase, 0) - by_phase
    overflow = jnp.max(number) > MAIN
    window, index = windows(number, acquired, 0, MAIN)
    line_table = in_hbm(line_tables(index, table))
    image, packed, grams, line_table, window, overflow = lax.optimization_barrier(
        (image, packed, grams, line_table, window, overflow)
    )
    lines_imag = in_hbm(exchange(packed, "row"))
    image = in_hbm(image)

    maps, frames_cols, splits, first, last = receive(image)
    frames_before, frames_after = shift(last, 1), shift(first, -1)
    residual, _, _ = adjoint(0, IMAGE, window, line_table, maps, image, jnp.zeros((2, SIZE, LANES), F32))
    residual = start(grams, maps, frames_cols, splits, frames_before, frames_after, residual)

    residual, first, last = adjoint(1, 0, window, line_table, maps, lines_imag, residual)

    def more(carry):
        residual = carry[1]
        window, index = windows(number, acquired, MAIN, EXTRA)
        line_table = line_tables(index, table)
        for part in range(2):
            extra = exchange(pack_more(own, lines, part, MAIN, EXTRA), "row")
            residual, first, last = adjoint(part, 0, window, line_table, maps, extra, residual)
        return jnp.array(False), residual, first, last

    _, residual, first, last = lax.while_loop(
        lambda carry: carry[0], more, (overflow, residual, first, last)
    )

    residual_before = shift(last, 1)
    residual_after = shift(first, -1)
    grams_residual = gram_apply(grams, maps, residual)
    product, first, last, sums = normal(residual, grams_residual, residual_before, residual_after)
    product_after = shift(first, -1)
    shared = share(sums, curvature(grams, maps, product), last, product_after)
    shared = exchange(shared, ("phase", "row"))
    back = solve(shared, frames_cols, residual, product, frames_after, residual_after, product_after)
    new_frames, new_aux, new_dual, gaps = finish(exchange(back, "row"), auxiliary, scaled_dual)
    gaps = jnp.sum(exchange(gaps, ("phase", "row"))[:, 0, :2], 0)
    residual_norms = jnp.sqrt(gaps) * jnp.array([1.0, PENALTY], F32)
    return new_frames, new_aux, new_dual, residual_norms


def solution(mesh):
    image = P(None, "phase", "row", None)
    in_specs = (
        image,
        image,
        image,
        P(None, None, "row", None),
        P(None, None, "phase", "row", None),
        P("phase", None),
    )
    return jax.shard_map(
        local, mesh=mesh, in_specs=in_specs, out_specs=(image, image, image, P()), check_vma=False
    )
```

time: 206 us -> 168 us (0.82)
  waiting for transfers between devices: 49.1 us -> 6.89 us
  blocking collectives: 30.7 us -> 52.8 us
  starting transfers between devices: 38 us -> 24.4 us
  Pallas kernels: 77.9 us -> 68.3 us
  other arithmetic: 0.83 us -> 5.68 us
    all_to_all x4 -> x2, waiting for transfers between devices: 42.7 us -> 6.88 us  [exchange(): return lax.all_to_all(value, axes, 0, 0, tiled=True)]
    all_to_all x2 -> x3, blocking collectives: 30.7 us -> 52.8 us  [exchange(): return lax.all_to_all(value, axes, 0, 0, tiled=True)]
    all_to_all x4 -> x2, starting transfers between devices: 22.7 us -> 13 us  [exchange(): return lax.all_to_all(value, axes, 0, 0, tiled=True)]
    pallas_call x12, Pallas kernels: 67.9 us -> 58.6 us  [the longest x2 13.2 us: adjoint(): pl.pallas_call(functools.partial(adjoint_kernel, part, base), grid_spec=p...]
    ppermute x6 -> x5, waiting for transfers between devices: 6.38 us -> 0.01 us  [shift(): return lax.ppermute(value, 'phase', pairs)]
    ppermute x6 -> x5, starting transfers between devices: 15.3 us -> 11.5 us  [shift(): return lax.ppermute(value, 'phase', pairs)]
    squeeze x2 -> x0, local copies, waits for them, and re-layouts: 2.25 us -> none  [the longest x1 1.19 us: local(): residual_norms = norms(exchange(gaps, ('phase', 'row')))[0, :2]]
    unnamed x20 -> x26, local copies, waits for them, and re-layouts: 4.16 us -> 5.75 us
  transfers between devices with their start and end apart: 10 -> 7, of which waited for: 5 -> 1; matrix products, arithmetic and copies ran while one was open for 0% -> 4% of each run, Pallas kernels for 28% -> 27%
where the time goes in v2:
time: 168 us; the launch traced here: 167 us
  Pallas kernels  68.3 us (41%)
  blocking collectives  52.8 us (31%)
  starting transfers between devices  24.4 us (15%)
  local copies, waits for them, and re-layouts  7.31 us (4%)
  waiting for transfers between devices  6.89 us (4%)
  other arithmetic  5.68 us (3%)
    all_to_all x3, blocking collectives, exchange(): return lax.all_to_all(value, axes, 0, 0, tiled=True)  52.8 us
    pallas_call x2, Pallas kernels, adjoint(): pl.pallas_call(functools.partial(adjoint_kernel, part, base), grid_spec=p...  13.2 us
    all_to_all x2, starting transfers between devices, exchange(): return lax.all_to_all(value, axes, 0, 0, tiled=True)  13 us
    ppermute x5, starting transfers between devices, shift(): return lax.ppermute(value, 'phase', pairs)  11.5 us
    pallas_call x1, Pallas kernels, gram_apply(): pl.pallas_call(gram_kernel, grid=(2,), in_specs=[GRAM_SPEC, MAPS_SPEC, VE...  7.69 us
    pallas_call x1, Pallas kernels, gram_tables(): pl.pallas_call(gram_table_kernel, grid=(PHASES,), in_specs=[pl.BlockSpec(...  7.37 us
    pallas_call x1, Pallas kernels, pack_first(): pl.pallas_call(pack_first_kernel, grid=(COILS // step,), in_specs=[whole_...  7.08 us
    pallas_call x1, Pallas kernels, start(): pl.pallas_call(start_kernel, grid=(2,), in_specs=[GRAM_SPEC, MAPS_SPEC] +...  7 us
  transfers between devices with their start and end apart: 7, of which 1 were waited for; matrix products, arithmetic and copies ran while one was open for 4% of the time, Pallas kernels for 27%

profile of v2, /device:TPU:1, one launch (start us, length us, event | category | flops | bytes accessed | tf_op | source)
XLA Modules:
  0.0 166.8 jit_solution(5915813835961633697)
XLA Ops:
  0.6 0.8 dynamic-slice_convert_fusion
  1.4 0.1 reshape.140.weight_ref
  1.5 7.1 %pack_first.1 = f32[16,152,256]{2,1,0:T(8,128)} custom-call(f32[1,128]{1,0:T(1,128)S(1)} %reshape.140.weight_ref, f32[16,2,128,256]{3,2,1,0:T(8,128)} %bitcast.in_ref, f32[16,2,16,256]{3,2,1,0:T(8,128)} %maps_ref.1, f32[2,8,16,256]{3,2,1,0:T(8,128)} %frames_ref.1, f32[2,8,16,256]{3,2,1,0:T(8,128)} %aux_ref.3, f32[2,8,16,256]{3,2,1,0:T(8,128)} %dual_ref.3), custom_call_target="tpu_custom_call" | custom-call | tf_op jit(solution)/shard_map/pack_first/pallas_call | solution.py:274
  8.6 0.0 copy-start.11
  8.6 6.9 %all-to-all-start.2 = ((f32[16,152,256]{2,1,0:T(8,128)}), f32[16,152,256]{2,1,0:T(8,128)S(1)}, u32[]{:S(2)}, u32[]{:S(2)}) async-start(f32[16,152,256]{2,1,0:T(8,128)} %pack_first.1), calls=%async_computation.2 | async-start | bytes 4980736 | tf_op jit(solution)/shard_map/all_to_all | solution.py:766
  15.5 5.0 %pack_more_1_0.1 = f32[16,88,256]{2,1,0:T(8,128)} custom-call(f32[1,128]{1,0:T(1,128)S(1)} %reshape.140.weight_ref, f32[16,2,128,256]{3,2,1,0:T(8,128)} %bitcast.in_ref), custom_call_target="tpu_custom_call" | custom-call | tf_op jit(solution)/shard_map/pack_more_1_0/pallas_call | solution.py:300
  20.5 0.0 copy-done.11
  20.5 0.1 reshape.142
  20.6 0.2 reduce_sum.36
  20.8 1.4 reduce_window_sum.22
  22.2 0.6 broadcast_in_dim.24.weight_ref
  22.8 0.7 fusion.2
  23.5 0.2 fusion.1
  23.8 0.1 reshape.143.window_ref
  23.8 0.1 add_add_fusion.1
  24.0 0.1 iota_add_fusion.1
  24.0 1.5 select_reduce_fusion.1
  25.6 0.7 sub.49.index_ref
  26.3 6.3 %line_tables.2.tables_ref = bf16[8,4,256,256]{3,2,1,0:T(8,128)(2,1)} custom-call(s32[8,1,256]{2,1,0:T(1,128)} %sub.49.index_ref, bf16[4,256,256]{2,1,0:T(8,128)(2,1)} %constant.64.clone.tables_ref), custom_call_target="tpu_custom_call" | custom-call | tf_op jit(solution)/shard_map/line_tables/pallas_call | solution.py:323
  32.5 7.4 %gram_tables.1.gram_ref = bf16[8,4,256,256]{3,2,1,0:T(8,128)(2,1)} custom-call(f32[8,1,256]{2,1,0:T(1,128)} %broadcast_in_dim.24.weight_ref, bf16[4,256,256]{2,1,0:T(8,128)(2,1)} %constant.64.clone.tables_ref), custom_call_target="tpu_custom_call" | custom-call | tf_op jit(solution)/shard_map/gram_tables/pallas_call | solution.py:373
  40.5 6.9 %all-to-all-done.2.image_ref.lines_ref = f32[16,152,256]{2,1,0:T(8,128)S(1)} async-done(((f32[16,152,256]{2,1,0:T(8,128)}), f32[16,152,256]{2,1,0:T(8,128)S(1)}, u32[]{:S(2)}, u32[]{:S(2)}) %all-to-all-start.2) | async-done | bytes 2490400 | tf_op jit(solution)/shard_map/all_to_all | solution.py:766
  47.4 1.5 copy-done.8
  48.9 6.0 %all-to-all-start.3 = ((f32[16,88,256]{2,1,0:T(8,128)}), f32[16,88,256]{2,1,0:T(8,128)}, u32[]{:S(2)}, u32[]{:S(2)}) async-start(f32[16,88,256]{2,1,0:T(8,128)} %pack_more_1_0.1), calls=%async_computation.3 | async-start | bytes 2883584 | tf_op jit(solution)/shard_map/all_to_all | solution.py:766
  55.0 2.1 %receive.1 = (f32[2,256,256]{2,1,0:T(8,128)S(1)}, f32[2,256,128]{2,1,0:T(8,128)}, f32[2,256,128]{2,1,0:T(8,128)}, f32[2,32,128]{2,1,0:T(8,128)}, f32[2,32,128]{2,1,0:T(8,128)}) custom-call(f32[16,152,256]{2,1,0:T(8,128)} %copy-done.8), custom_call_target="tpu_custom_call" | custom-call | tf_op jit(solution)/shard_map/receive/pallas_call | solution.py:346
  57.1 1.7 collective-permute-start
  58.7 4.5 %collective-permute-start.1 = (f32[2,32,128]{2,1,0:T(8,128)}, f32[2,32,128]{2,1,0:T(8,128)S(1)}, u32[]{:S(2)}, u32[]{:S(2)}) collective-permute-start(f32[2,32,128]{2,1,0:T(8,128)} %get-tuple-element.102), channel_id=1, source_target_pairs={{0,112},{16,0},{32,16},{48,32},{64,48},{80,64},{96,80},{112,96},{1... | collective-permute-start | bytes 98312 | tf_op jit(solution)/shard_map/ppermute | solution.py:762
  63.3 0.1 copy.29
  63.3 0.1 copy.28
  63.5 6.7 %adjoint_0_64.1 = (f32[2,256,128]{2,1,0:T(8,128)S(1)}, f32[2,32,128]{2,1,0:T(8,128)}, f32[2,32,128]{2,1,0:T(8,128)}) custom-call(s32[128]{0:T(128)S(1)} %reshape.143.window_ref, bf16[8,4,256,256]{3,2,1,0:T(8,128)(2,1)} %line_tables.2.tables_ref, f32[2,256,256]{2,1,0:T(8,128)S(1)} %get-tuple-element.222.maps_ref, f32[16,152,256]{2,1,0:T(8,128)} %copy-done.8, ...), custom_call_target="tpu_custom_call" | custom-call | tf_op jit(solution)/shard_map/adjoint_0_64/pallas_call | solution.py:495
  70.2 0.0 collective-permute-done.before_ref
  70.2 0.0 collective-permute-done.1.after_ref.frames_after_ref
  70.2 0.0 copy-start.6
  70.2 0.0 copy-done.3
  70.2 0.0 copy-done.5
  70.2 7.0 %start.1.in_ref = f32[2,256,128]{2,1,0:T(8,128)S(1)} custom-call(bf16[8,4,256,256]{3,2,1,0:T(8,128)(2,1)} %gram_tables.1.gram_ref, f32[2,256,256]{2,1,0:T(8,128)S(1)} %get-tuple-element.222.maps_ref, f32[2,256,128]{2,1,0:T(8,128)S(1)} %copy-done.3, f32[2,256,128]{2,1,0:T(8,128)S(1)} %copy-done.5, f32[2,32,128]{2,1,0:T(8,128)S(1)} %collective-permute-done.before_ref, ...), custom_call_target="tpu_custom_call" | custom-call | tf_op jit(solution)/shard_map/start/pallas_call | solution.py:442
  77.3 0.0 all-to-all-done.3.lines_ref
  77.3 6.5 %adjoint_1_0.2 = (f32[2,256,128]{2,1,0:T(8,128)S(1)}, f32[2,32,128]{2,1,0:T(8,128)}, f32[2,32,128]{2,1,0:T(8,128)}) custom-call(s32[128]{0:T(128)S(1)} %reshape.143.window_ref, bf16[8,4,256,256]{3,2,1,0:T(8,128)(2,1)} %line_tables.2.tables_ref, f32[2,256,256]{2,1,0:T(8,128)S(1)} %get-tuple-element.222.maps_ref, f32[16,88,256]{2,1,0:T(8,128)} %all-to-all-done.3.lines_ref, ...), custom_call_target="tpu_custom_call" | custom-call | tf_op jit(solution)/shard_map/adjoint_1_0/pallas_call | solution.py:495
  83.7 0.0 copy-done.6
  83.7 0.0 collective-permute-start.2
  83.7 5.1 %collective-permute-start.3 = (f32[2,32,128]{2,1,0:T(8,128)}, f32[2,32,128]{2,1,0:T(8,128)S(1)}, u32[]{:S(2)}, u32[]{:S(2)}) collective-permute-start(f32[2,32,128]{2,1,0:T(8,128)} %get-tuple-element.109), channel_id=1, source_target_pairs={{0,112},{16,0},{32,16},{48,32},{64,48},{80,64},{96,80},{112,96},{1... | collective-permute-start | bytes 98312 | tf_op jit(solution)/shard_map/ppermute | solution.py:762
  88.8 7.7 %gram_apply.1.gram_ref = f32[2,256,128]{2,1,0:T(8,128)S(1)} custom-call(bf16[8,4,256,256]{3,2,1,0:T(8,128)(2,1)} %gram_tables.1.gram_ref, f32[2,256,256]{2,1,0:T(8,128)S(1)} %get-tuple-element.245, f32[2,256,128]{2,1,0:T(8,128)S(1)} %get-tuple-element.107.in_ref.first_ref.residual_ref), custom_call_target="tpu_custom_call" | custom-call | tf_op jit(solution)/shard_map/gram_apply/pallas_call | solution.py:528
  96.5 0.0 copy-start.2
  96.5 0.7 copy-done.2
  97.2 0.0 collective-permute-done.2.before_ref
  97.2 0.0 collective-permute-done.3.after_ref.residual_after_ref
  97.2 0.6 copy-done.12
  97.8 0.6 copy-done.9
  98.4 2.9 %normal.1 = (f32[2,256,128]{2,1,0:T(8,128)}, f32[2,32,128]{2,1,0:T(8,128)}, f32[2,32,128]{2,1,0:T(8,128)}, f32[4,8,128]{2,1,0:T(8,128)}) custom-call(f32[2,256,128]{2,1,0:T(8,128)S(1)} %get-tuple-element.107.in_ref.first_ref.residual_ref, f32[2,256,128]{2,1,0:T(8,128)} %copy-done.2, f32[2,32,128]{2,1,0:T(8,128)} %copy-done.12, f32[2,32,128]{2,1,0:T(8,128)} %copy-done.9), custom_call_target="tpu_custom_call" | custom-call | tf_op jit(solution)/shard_map/normal/pallas_call | solution.py:580
  101.4 0.2 collective-permute-start.4
  101.6 0.9 copy-done.4
  102.5 3.6 %curvature.1.curve_ref = f32[8,128]{1,0:T(8,128)S(1)} custom-call(bf16[8,4,256,256]{3,2,1,0:T(8,128)(2,1)} %gram_tables.1.gram_ref, f32[2,256,256]{2,1,0:T(8,128)S(1)} %get-tuple-element.245, f32[2,256,128]{2,1,0:T(8,128)S(1)} %copy-done.4), custom_call_target="tpu_custom_call" | custom-call | tf_op jit(solution)/shard_map/curvature/pallas_call | solution.py:622
  106.1 0.0 copy-start.7
  106.1 0.6 copy-done.7
  106.7 0.0 collective-permute-done.4.after_ref.product_after_ref
  106.7 0.6 copy-done.10
  107.3 1.6 share.1
  108.8 25.3 %all_to_all.37.shared_ref = f32[128,1,128]{2,1,0:T(1,128)} all-to-all(f32[128,1,128]{2,1,0:T(1,128)} %share.1), channel_id=1, replica_groups=mesh['phase'=8,'row'=16] {'phase','row'}, dimensions={0} | all-to-all | bytes 131072 | tf_op jit(solution)/shard_map/all_to_all | solution.py:766
  134.1 2.2 %solve.1 = f32[16,3,16,128]{3,2,1,0:T(8,128)} custom-call(f32[128,1,128]{2,1,0:T(1,128)} %all_to_all.37.shared_ref, f32[2,256,128]{2,1,0:T(8,128)} %get-tuple-element.99.frames_ref, f32[2,256,128]{2,1,0:T(8,128)S(1)} %get-tuple-element.107.in_ref.first_ref.residual_ref, f32[2,256,128]{2,1,0:T(8,128)} %get-tuple-element.111.in_ref.product_ref, ...), custom_call_target="tpu_custom_call" | custom-call | tf_op jit(solution)/shard_map/solve/pallas_call | solution.py:697
  136.3 13.4 %all_to_all.38.in_ref = f32[16,3,16,128]{3,2,1,0:T(8,128)} all-to-all(f32[16,3,16,128]{3,2,1,0:T(8,128)} %solve.1), channel_id=1, replica_groups=mesh['phase'=8,'row'=16] {'row'}, dimensions={0} | all-to-all | bytes 786432 | tf_op jit(solution)/shard_map/all_to_all | solution.py:766
  149.7 2.3 %finish.1 = (f32[2,8,16,256]{3,2,1,0:T(8,128)}, f32[2,8,16,256]{3,2,1,0:T(8,128)}, f32[2,8,16,256]{3,2,1,0:T(8,128)}, f32[128,1,128]{2,1,0:T(1,128)}) custom-call(f32[16,3,16,128]{3,2,1,0:T(8,128)} %all_to_all.38.in_ref, f32[2,8,16,256]{3,2,1,0:T(8,128)} %aux_ref.3, f32[2,8,16,256]{3,2,1,0:T(8,128)} %dual_ref.3), custom_call_target="tpu_custom_call" | custom-call | tf_op jit(solution)/shard_map/finish/pallas_call | solution.py:742
  152.0 14.1 %all_to_all.39 = f32[128,1,128]{2,1,0:T(1,128)S(1)} all-to-all(f32[128,1,128]{2,1,0:T(1,128)} %get-tuple-element.117), channel_id=1, replica_groups=mesh['phase'=8,'row'=16] {'phase','row'}, dimensions={0} | all-to-all | bytes 131072 | tf_op jit(solution)/shard_map/all_to_all | solution.py:766
  166.1 0.2 slice_reduce_fusion
  166.3 0.0 copy-done.13
  166.3 0.5 sqrt_multiply_fusion
  (15 shorter events, 0.1 us)
Async XLA Ops:
  8.6 11.9 %copy-start.11 = (s32[8,256]{1,0:T(8,128)S(1)}, s32[8,256]{1,0:T(8,128)}, u32[]{:S(2)}) copy-start(s32[8,256]{1,0:T(8,128)} %param.15) | copy-start | bytes 24580
  8.6 38.8 %all-to-all-start.2 = ((f32[16,152,256]{2,1,0:T(8,128)}), f32[16,152,256]{2,1,0:T(8,128)S(1)}, u32[]{:S(2)}, u32[]{:S(2)}) async-start(f32[16,152,256]{2,1,0:T(8,128)} %pack_first.1), calls=%async_computation.2 | async-start | bytes 4980736 | tf_op jit(solution)/shard_map/all_to_all | solution.py:766
  47.4 1.5 copy-start.8
  48.9 28.3 %all-to-all-start.3 = ((f32[16,88,256]{2,1,0:T(8,128)}), f32[16,88,256]{2,1,0:T(8,128)}, u32[]{:S(2)}, u32[]{:S(2)}) async-start(f32[16,88,256]{2,1,0:T(8,128)} %pack_more_1_0.1), calls=%async_computation.3 | async-start | bytes 2883584 | tf_op jit(solution)/shard_map/all_to_all | solution.py:766
  57.1 13.2 %copy-start.3 = (f32[2,256,128]{2,1,0:T(8,128)S(1)}, f32[2,256,128]{2,1,0:T(8,128)}, u32[]{:S(2)}) copy-start(f32[2,256,128]{2,1,0:T(8,128)} %get-tuple-element.99.frames_ref) | copy-start | bytes 786436
  57.1 13.2 %copy-start.5 = (f32[2,256,128]{2,1,0:T(8,128)S(1)}, f32[2,256,128]{2,1,0:T(8,128)}, u32[]{:S(2)}) copy-start(f32[2,256,128]{2,1,0:T(8,128)} %get-tuple-element.100.splits_ref) | copy-start | bytes 786436
  57.1 13.1 %collective-permute-start = (f32[2,32,128]{2,1,0:T(8,128)}, f32[2,32,128]{2,1,0:T(8,128)S(1)}, u32[]{:S(2)}, u32[]{:S(2)}) collective-permute-start(f32[2,32,128]{2,1,0:T(8,128)} %get-tuple-element.101), channel_id=1, source_target_pairs={{0,16},{16,32},{32,48},{48,64},{64,80},{80,96},{96,112},{112,0},{1... | collective-permute-start | bytes 98312 | tf_op jit(solution)/shard_map/ppermute | solution.py:762
  58.7 11.5 %collective-permute-start.1 = (f32[2,32,128]{2,1,0:T(8,128)}, f32[2,32,128]{2,1,0:T(8,128)S(1)}, u32[]{:S(2)}, u32[]{:S(2)}) collective-permute-start(f32[2,32,128]{2,1,0:T(8,128)} %get-tuple-element.102), channel_id=1, source_target_pairs={{0,112},{16,0},{32,16},{48,32},{64,48},{80,64},{96,80},{112,96},{1... | collective-permute-start | bytes 98312 | tf_op jit(solution)/shard_map/ppermute | solution.py:762
  70.2 13.5 %copy-start.6 = (f32[2,32,128]{2,1,0:T(8,128)}, f32[2,32,128]{2,1,0:T(8,128)S(1)}, u32[]{:S(2)}) copy-start(f32[2,32,128]{2,1,0:T(8,128)S(1)} %collective-permute-done.1.after_ref.frames_after_ref) | copy-start | bytes 98308
  83.7 13.5 %collective-permute-start.2 = (f32[2,32,128]{2,1,0:T(8,128)}, f32[2,32,128]{2,1,0:T(8,128)S(1)}, u32[]{:S(2)}, u32[]{:S(2)}) collective-permute-start(f32[2,32,128]{2,1,0:T(8,128)} %get-tuple-element.108), channel_id=1, source_target_pairs={{0,16},{16,32},{32,48},{48,64},{64,80},{80,96},{96,112},{112,0},{1... | collective-permute-start | bytes 98312 | tf_op jit(solution)/shard_map/ppermute | solution.py:762
  83.7 13.5 %collective-permute-start.3 = (f32[2,32,128]{2,1,0:T(8,128)}, f32[2,32,128]{2,1,0:T(8,128)S(1)}, u32[]{:S(2)}, u32[]{:S(2)}) collective-permute-start(f32[2,32,128]{2,1,0:T(8,128)} %get-tuple-element.109), channel_id=1, source_target_pairs={{0,112},{16,0},{32,16},{48,32},{64,48},{80,64},{96,80},{112,96},{1... | collective-permute-start | bytes 98312 | tf_op jit(solution)/shard_map/ppermute | solution.py:762
  96.5 0.7 copy-start.2
  97.2 0.6 copy-start.12
  97.8 0.6 copy-start.9
  101.4 5.3 %collective-permute-start.4 = (f32[2,32,128]{2,1,0:T(8,128)}, f32[2,32,128]{2,1,0:T(8,128)S(1)}, u32[]{:S(2)}, u32[]{:S(2)}) collective-permute-start(f32[2,32,128]{2,1,0:T(8,128)} %get-tuple-element.113), channel_id=1, source_target_pairs={{0,112},{16,0},{32,16},{48,32},{64,48},{80,64},{96,80},{112,96},{1... | collective-permute-start | bytes 98312 | tf_op jit(solution)/shard_map/ppermute | solution.py:762
  101.6 0.9 copy-start.4
  102.5 63.8 %copy-start.13 = (f32[2]{0:T(128)S(1)}, f32[2]{0:T(128)}, u32[]{:S(2)}) copy-start(f32[2]{0:T(128)} %constant.65.clone) | copy-start | bytes 28
  106.1 0.6 copy-start.7
  106.7 0.6 copy-start.10

commit v3 on v2

--- a/solution.py
+++ b/solution.py
@@ -27,6 +27,8 @@
 ROW_SHARDS = 16
 PHASE_SHARDS = 8
 ALL = ROW_SHARDS * PHASE_SHARDS
+
+IN_VMEM = pl.BlockSpec(memory_space=pltpu.VMEM)
 
 F32 = jnp.float32
 BF16 = jnp.bfloat16
@@ -178,10 +180,10 @@
         finish(at, sum_four([term[0] for term in terms]), sum_four([term[1] for term in terms]))
 
 
-def gram_products(gram_ref, pieces, backs):
+def products(tables_ref, pieces, backs):
     for t in range(4):
         real_high, real_low, imag_high, imag_low = (pieces[t][i] for i in range(4))
-        table_real, table_imag, low_real, low_imag = (gram_ref[t, i] for i in range(4))
+        table_real, table_imag, low_real, low_imag = (tables_ref[t, i] for i in range(4))
         backs[t][0] = (
             dot(table_real, real_high) + dot(table_real, real_low) + dot(low_real, real_high)
         ) - (dot(table_imag, imag_high) + dot(table_imag, imag_low) + dot(low_imag, imag_high))
@@ -201,7 +203,7 @@
     return high, middle, (value - middle.astype(F32)).astype(BF16)
 
 
-def compact(weight_ref, in_ref, lines_ref, base):
+def compact(weight_ref, in_ref, lines_ref, base, at_step):
     count = lines_ref.shape[1]
     weight = jnp.broadcast_to(weight_ref[...], (8, LINES))
     row = lax.broadcasted_iota(jnp.int32, (LINES, LINES), 0)
@@ -215,108 +217,88 @@
     step = in_ref.shape[0]
     for c in range(step):
         high, middle, low = split_three(in_ref[c, 0])
-        lines_ref[pl.program_id(0) * step + c] = (
+        lines_ref[at_step * step + c] = (
             dot(select, high) + dot(select, middle) + dot(select, low)
         )
 
 
-def pack_lines(lines_ref, out_ref, start):
+def pack_lines(lines_ref, out_ref):
     for row in range(0, lines_ref.shape[1], 8):
         at = slice(row, row + 8)
-        to = slice(start + row, start + row + 8)
         halves = [(lines_ref[c, at, :LANES], lines_ref[c, at, LANES:]) for c in range(COILS)]
+        for j, (low, high) in enumerate(gather_coils(halves)):
+            out_ref[j, at, :LANES] = low
+            out_ref[j, at, LANES:] = high
+
+
+def pack_image_kernel(maps_ref, frames_ref, aux_ref, dual_ref, out_ref):
+    for part in range(2):
+        to = slice(part * 8, (part + 1) * 8)
+        halves = [(maps_ref[c, part, :, :LANES], maps_ref[c, part, :, LANES:]) for c in range(COILS)]
         for j, (low, high) in enumerate(gather_coils(halves)):
             out_ref[j, to, :LANES] = low
             out_ref[j, to, LANES:] = high
-
-
-def pack_image(maps_ref, frames_ref, aux_ref, dual_ref, out_ref):
-    for part in range(2):
-        for row in range(0, ROWS, 8):
-            at = slice(row, row + 8)
-            halves = [
-                (maps_ref[c, part, at, :LANES], maps_ref[c, part, at, LANES:]) for c in range(COILS)
-            ]
-            to = slice(part * ROWS + row, part * ROWS + row + 8)
-            for j, (low, high) in enumerate(gather_coils(halves)):
-                out_ref[j, to, :LANES] = low
-                out_ref[j, to, LANES:] = high
-            for half in range(2):
-                cols = slice(half * LANES, (half + 1) * LANES)
-                frames = [frames_ref[part, t, at, cols] for t in range(PHASES)]
-                splits = [
-                    aux_ref[part, t, at, cols] - dual_ref[part, t, at, cols] for t in range(PHASES)
-                ]
-                lanes = slice(part * LANES, (part + 1) * LANES)
-                for which, values in ((2, frames), (3, splits)):
-                    to = slice(which * ROWS + row, which * ROWS + row + 8)
-                    for jj, value in enumerate(transpose_groups(values)):
-                        out_ref[half * 8 + jj, to, lanes] = value
-
-
-def pack_first_kernel(
-    weight_ref, in_ref, maps_ref, frames_ref, aux_ref, dual_ref, out_ref, lines_ref
-):
-    compact(weight_ref, in_ref, lines_ref, 0)
-
-    @pl.when(pl.program_id(0) == pl.num_programs(0) - 1)
+        for half in range(2):
+            cols = slice(half * LANES, (half + 1) * LANES)
+            frames = [frames_ref[part, t, :, cols] for t in range(PHASES)]
+            splits = [aux_ref[part, t, :, cols] - dual_ref[part, t, :, cols] for t in range(PHASES)]
+            lanes = slice(part * LANES, (part + 1) * LANES)
+            for which, values in ((2, frames), (3, splits)):
+                to_rows = slice(which * 8, (which + 1) * 8)
+                for jj, value in enumerate(transpose_groups(values)):
+                    out_ref[half * 8 + jj, to_rows, lanes] = value
+
+
+def whole_spec(value):
+    return pl.BlockSpec(value.shape, lambda *_: (0,) * len(value.shape))
+
+
+def pack_image(coil_maps, *images):
+    rows = pl.BlockSpec((2, PHASES, 8, SIZE), lambda i: (0, 0, i, 0))
+    return pl.pallas_call(
+        pack_image_kernel,
+        grid=(ROWS // 8,),
+        in_specs=[pl.BlockSpec((COILS, 2, 8, SIZE), lambda i: (0, 0, i, 0))] + [rows] * 3,
+        out_specs=pl.BlockSpec((ROW_SHARDS, 32, SIZE), lambda i: (0, i, 0)),
+        out_shape=jax.ShapeDtypeStruct((ROW_SHARDS, IMAGE, SIZE), F32),
+        compiler_params=params(),
+        name="pack_image",
+    )(coil_maps, *images)
+
+
+PACK_STEPS = 4
+
+
+def pack_measured_kernel(base, weight_ref, in_ref, out_ref, lines_ref):
+    step = pl.program_id(1)
+    compact(weight_ref, in_ref, lines_ref, base, step)
+
+    @pl.when(step == PACK_STEPS - 1)
     def _():
-        pack_image(maps_ref, frames_ref, aux_ref, dual_ref, out_ref)
-        pack_lines(lines_ref, out_ref, IMAGE)
-
-
-def whole_spec(value):
-    return pl.BlockSpec(value.shape, lambda *_: (0,) * value.ndim)
-
-
-def pack_first(weight, measured, *images):
-    step = 4
-    return pl.pallas_call(
-        pack_first_kernel,
-        grid=(COILS // step,),
+        pack_lines(lines_ref, out_ref)
+
+
+def pack_measured(weight, measured, base, count):
+    return pl.pallas_call(
+        functools.partial(pack_measured_kernel, base),
+        grid=(2, PACK_STEPS),
         in_specs=[
             whole_spec(weight),
-            pl.BlockSpec((step, 1, LINES, SIZE), lambda i: (i, 0, 0, 0)),
-            *(whole_spec(value) for value in images),
+            pl.BlockSpec((COILS // PACK_STEPS, 1, LINES, SIZE), lambda part, i: (i, part, 0, 0)),
         ],
-        out_specs=pl.BlockSpec((ROW_SHARDS, IMAGE + MAIN, SIZE), lambda i: (0, 0, 0)),
-        out_shape=jax.ShapeDtypeStruct((ROW_SHARDS, IMAGE + MAIN, SIZE), F32),
-        scratch_shapes=[pltpu.VMEM((COILS, MAIN, SIZE), F32)],
-        compiler_params=params(),
-        name="pack_first",
-    )(weight, measured, *images)
-
-
-def pack_more_kernel(base, weight_ref, in_ref, out_ref, lines_ref):
-    compact(weight_ref, in_ref, lines_ref, base)
-
-    @pl.when(pl.program_id(0) == pl.num_programs(0) - 1)
-    def _():
-        pack_lines(lines_ref, out_ref, 0)
-
-
-def pack_more(weight, measured, part, base, count):
-    step = 4
-    return pl.pallas_call(
-        functools.partial(pack_more_kernel, base),
-        grid=(COILS // step,),
-        in_specs=[
-            whole_spec(weight),
-            pl.BlockSpec((step, 1, LINES, SIZE), lambda i: (i, part, 0, 0)),
-        ],
-        out_specs=pl.BlockSpec((ROW_SHARDS, count, SIZE), lambda i: (0, 0, 0)),
-        out_shape=jax.ShapeDtypeStruct((ROW_SHARDS, count, SIZE), F32),
+        out_specs=pl.BlockSpec((ROW_SHARDS, count, SIZE), lambda part, i: (0, part, 0)),
+        out_shape=jax.ShapeDtypeStruct((ROW_SHARDS, 2 * count, SIZE), F32),
         scratch_shapes=[pltpu.VMEM((COILS, count, SIZE), F32)],
         compiler_params=params(),
-        name=f"pack_more_{part}_{base}",
+        name=f"pack_measured_{base}",
     )(weight, measured)
 
 
 def line_table_kernel(index_ref, tables_ref, out_ref):
     row = lax.broadcasted_iota(jnp.int32, (SIZE, SIZE), 0)
     select = jnp.where(row == index_ref[0], 1.0, 0.0).astype(BF16)
-    for i in range(4):
-        out_ref[0, i] = dot(tables_ref[i], select).astype(BF16)
+    for i, table in enumerate((0, 2, 1, 3)):
+        out_ref[0, i] = dot(tables_ref[table], select).astype(BF16)
 
 
 def line_tables(index, tables):
@@ -326,6 +308,7 @@
         in_specs=[pl.BlockSpec((1, 1, SIZE), lambda t: (t, 0, 0)), whole_spec(tables)],
         out_specs=pl.BlockSpec((1, 4, SIZE, SIZE), lambda t: (t, 0, 0, 0)),
         out_shape=jax.ShapeDtypeStruct((PHASES, 4, SIZE, SIZE), BF16),
+        compiler_params=params(),
         name="line_tables",
     )(index, tables)
 
@@ -334,10 +317,15 @@
     for part in range(2):
         lanes = slice(part * LANES, (part + 1) * LANES)
         for block in range(ROW_SHARDS):
-            at = slice(block * ROWS, (block + 1) * ROWS)
-            maps_ref[part, at] = image_ref[block, part * ROWS : (part + 1) * ROWS]
-            frames_ref[part, at] = image_ref[block, 2 * ROWS : 3 * ROWS, lanes]
-            splits_ref[part, at] = image_ref[block, 3 * ROWS : 4 * ROWS, lanes]
+            for half in range(2):
+                row = block * ROWS + half * 8
+                at = slice(row, row + 8)
+                maps, frames, splits = (
+                    slice(half * 32 + which * 8, half * 32 + (which + 1) * 8) for which in (part, 2, 3)
+                )
+                maps_ref[part, at] = image_ref[block, maps]
+                frames_ref[part, at] = image_ref[block, frames, lanes]
+                splits_ref[part, at] = image_ref[block, splits, lanes]
         first_ref[part] = fold_phase(frames_ref[part], 0)
         last_ref[part] = fold_phase(frames_ref[part] + splits_ref[part], PHASES - 1)
 
@@ -349,6 +337,7 @@
         in_specs=[IMAGE_SPEC],
         out_specs=[MAPS_SPEC, VECTOR_SPEC, VECTOR_SPEC, FOLDED_SPEC, FOLDED_SPEC],
         out_shape=[jax.ShapeDtypeStruct((2, SIZE, SIZE), F32), VECTOR, VECTOR, FOLDED, FOLDED],
+        compiler_params=params(),
         name="receive",
     )(image)
 
@@ -379,6 +368,7 @@
         ],
         out_specs=pl.BlockSpec((1, 4, SIZE, SIZE), lambda t: (t, 0, 0, 0)),
         out_shape=jax.ShapeDtypeStruct((PHASES, 4, SIZE, SIZE), BF16),
+        compiler_params=params(),
         name="gram_tables",
     )(weight, tables)
 
@@ -396,39 +386,18 @@
 
 
 def params():
-    return pltpu.CompilerParams(vmem_limit_bytes=48 << 20)
-
-
-def start_kernel(
-    gram_ref, maps_ref, frames_ref, splits_ref, before_ref, after_ref, in_ref, out_ref, *scratch
-):
+    return pltpu.CompilerParams(vmem_limit_bytes=16 << 20)
+
+
+def start_kernel(gram_ref, maps_ref, frames_ref, out_ref, *scratch):
     pieces, backs = scratch[:4], scratch[4:]
 
     @pl.when(pl.program_id(0) == 0)
     def _():
-        group = lane_group(FOLD)
-        for i in range(8):
-            at = slice(i * FOLD, (i + 1) * FOLD)
-            for part in range(2):
-                frames, splits = frames_ref[part, at], splits_ref[part, at]
-                ahead = jnp.where(
-                    group == PHASES - 1,
-                    unfold_phase(after_ref[part], PHASES - 1, i),
-                    pltpu.roll(frames, LANES - GROUP, 1),
-                )
-                behind = jnp.where(
-                    group == 0,
-                    unfold_phase(before_ref[part], 0, i),
-                    pltpu.roll(frames + splits, GROUP, 1),
-                )
-                gap = splits - (ahead - frames)
-                gap_behind = behind - frames
-                out_ref[part, at] = (
-                    in_ref[part, at] + PENALTY * (gap_behind - gap) - DAMPING * frames
-                )
+        out_ref[...] = jnp.zeros_like(out_ref)
 
     expand(frames_ref, maps_ref, pieces)
-    gram_products(gram_ref, pieces, backs)
+    products(gram_ref, pieces, backs)
 
     def finish(at, real, imag):
         keep = in_step(at.stop - at.start)
@@ -438,43 +407,65 @@
     reduce(maps_ref, backs, finish)
 
 
-def start(grams, maps, frames, splits, before, after, so_far):
+def start(grams, maps, frames):
     return pl.pallas_call(
         start_kernel,
         grid=(2,),
-        in_specs=[GRAM_SPEC, MAPS_SPEC] + [VECTOR_SPEC] * 2 + [FOLDED_SPEC] * 2 + [VECTOR_SPEC],
+        in_specs=[GRAM_SPEC] + [IN_VMEM] * 2,
         out_specs=VECTOR_SPEC,
         out_shape=VECTOR,
         scratch_shapes=PIECES + BACKS,
         compiler_params=params(),
         name="start",
-    )(grams, maps, frames, splits, before, after, so_far)
-
-
-def adjoint_kernel(
-    part, base, window_ref, tables_ref, maps_ref, lines_ref, in_ref, out_ref, first_ref, last_ref, *scratch
-):
-    pieces, backs = scratch[:4], scratch[4:]
+    )(grams, maps, frames)
+
+
+def add_local(frames_ref, splits_ref, before_ref, after_ref, in_ref, out_ref):
+    group = lane_group(FOLD)
+    for i in range(8):
+        at = slice(i * FOLD, (i + 1) * FOLD)
+        for part in range(2):
+            frames, splits = frames_ref[part, at], splits_ref[part, at]
+            ahead = jnp.where(
+                group == PHASES - 1,
+                unfold_phase(after_ref[part], PHASES - 1, i),
+                pltpu.roll(frames, LANES - GROUP, 1),
+            )
+            behind = jnp.where(
+                group == 0,
+                unfold_phase(before_ref[part], 0, i),
+                pltpu.roll(frames + splits, GROUP, 1),
+            )
+            gap = splits - (ahead - frames)
+            gap_behind = behind - frames
+            out_ref[part, at] = in_ref[part, at] + PENALTY * (gap_behind - gap) - DAMPING * frames
+
+
+def adjoint_kernel(local_terms, window_ref, tables_ref, maps_ref, lines_ref, in_ref, *refs):
+    locals_in, refs = refs[:local_terms], refs[local_terms:]
+    out_ref, first_ref, last_ref = refs[:3]
+    pieces, backs = refs[3:7], refs[7:]
     half = pl.program_id(0)
-    count = lines_ref.shape[1] - base
+    count = lines_ref.shape[1] // 2
 
     @pl.when(half == 0)
     def _():
-        out_ref[...] = in_ref[...]
+        if local_terms:
+            add_local(*locals_in, in_ref, out_ref)
+        else:
+            out_ref[...] = in_ref[...]
 
     for t in range(4):
         for block in range(ROW_SHARDS):
             at = slice(block * ROWS, (block + 1) * ROWS)
             start = window_ref[(half * 4 + t) * ROW_SHARDS + block]
             aligned = jnp.minimum(start // 8, (count - ROWS) // 8 - 1) * 8
-            rows = lines_ref[block, pl.ds(pl.multiple_of(base + aligned, 8), ROWS + 8)]
-            rows = pltpu.roll(rows, lax.rem(ROWS + 8 - (start - aligned), ROWS + 8), 0)
-            store_split(pieces[t], 0, at, rows[:ROWS])
-        high, low = pieces[t][0], pieces[t][1]
-        cos, cos_low, sin, sin_low = (tables_ref[t, i] for i in range(4))
-        by_cos = dot(cos, high) + dot(cos, low) + dot(cos_low, high)
-        by_sin = dot(sin, high) + dot(sin, low) + dot(sin_low, high)
-        backs[t][0], backs[t][1] = (by_cos, by_sin) if part == 0 else (-by_sin, by_cos)
+            turn = lax.rem(ROWS + 8 - (start - aligned), ROWS + 8)
+            for part in range(2):
+                rows = pl.ds(pl.multiple_of(part * count + aligned, 8), ROWS + 8)
+                rows = pltpu.roll(lines_ref[block, rows], turn, 0)
+                store_split(pieces[t], 2 * part, at, rows[:ROWS])
+    products(tables_ref, pieces, backs)
 
     def finish(at, real, imag):
         keep = in_step(at.stop - at.start)
@@ -491,26 +482,26 @@
             last_ref[which] = fold_phase(value, PHASES - 1)
 
 
-def adjoint(part, base, window, tables, maps, lines, so_far):
-    return pl.pallas_call(
-        functools.partial(adjoint_kernel, part, base),
+def adjoint(window, tables, maps, lines, so_far, *local_terms):
+    return pl.pallas_call(
+        functools.partial(adjoint_kernel, len(local_terms)),
         grid_spec=pltpu.PrefetchScalarGridSpec(
             num_scalar_prefetch=1,
             grid=(2,),
-            in_specs=[GRAM_SPEC, MAPS_SPEC, whole_spec(lines), VECTOR_SPEC],
-            out_specs=[VECTOR_SPEC, FOLDED_SPEC, FOLDED_SPEC],
+            in_specs=[GRAM_SPEC] + [IN_VMEM] * (3 + len(local_terms)),
+            out_specs=[IN_VMEM] * 3,
             scratch_shapes=PIECES + BACKS,
         ),
         out_shape=[VECTOR, FOLDED, FOLDED],
         compiler_params=params(),
-        name=f"adjoint_{part}_{base}",
-    )(window, tables, maps, lines, so_far)
+        name="adjoint",
+    )(window, tables, maps, lines, so_far, *local_terms)
 
 
 def gram_kernel(gram_ref, maps_ref, in_ref, out_ref, *scratch):
     pieces, backs = scratch[:4], scratch[4:]
     expand(in_ref, maps_ref, pieces)
-    gram_products(gram_ref, pieces, backs)
+    products(gram_ref, pieces, backs)
 
     @pl.when(pl.program_id(0) == 0)
     def _():
@@ -528,8 +519,8 @@
     return pl.pallas_call(
         gram_kernel,
         grid=(2,),
-        in_specs=[GRAM_SPEC, MAPS_SPEC, VECTOR_SPEC],
-        out_specs=VECTOR_SPEC,
+        in_specs=[GRAM_SPEC, IN_VMEM, IN_VMEM],
+        out_specs=IN_VMEM,
         out_shape=VECTOR,
         scratch_shapes=PIECES + BACKS,
         compiler_params=params(),
@@ -579,41 +570,34 @@
 def normal(first, grams_first, before, after):
     return pl.pallas_call(
         normal_kernel,
+        grid=(1,),
+        in_specs=[IN_VMEM] * 4,
+        out_specs=[IN_VMEM] * 4,
         out_shape=[
             VECTOR,
             FOLDED,
             FOLDED,
             jax.ShapeDtypeStruct((4, 8, LANES), F32),
         ],
+        compiler_params=params(),
         name="normal",
     )(first, grams_first, before, after)
 
 
 def curvature_kernel(gram_ref, maps_ref, in_ref, out_ref, *scratch):
     pieces, backs = scratch[:4], scratch[4:]
-    half = pl.program_id(0)
-
-    @pl.when(half == 0)
+
+    @pl.when(pl.program_id(0) == 0)
     def _():
         out_ref[...] = jnp.zeros_like(out_ref)
 
-    for at in chunks(32):
-        real = spread_half(in_ref[0, at], half)
-        imag = spread_half(in_ref[1, at], half)
-        for t in range(4):
-            for which, value in enumerate(images_of(maps_ref, at, real[t], imag[t])):
-                pieces[t][which, at] = value.astype(BF16)
-    for t in range(4):
-        table_real, table_imag = gram_ref[t, 0], gram_ref[t, 1]
-        real, imag = pieces[t][0], pieces[t][1]
-        backs[t][0] = dot(table_real, real) - dot(table_imag, imag)
-        backs[t][1] = dot(table_real, imag) + dot(table_imag, real)
+    expand(in_ref, maps_ref, pieces)
+    products(gram_ref, pieces, backs)
     total = 0.0
     for at in chunks(32):
         for t in range(4):
-            both = pieces[t][0, at].astype(F32) * backs[t][0, at] + pieces[t][1, at].astype(
-                F32
-            ) * backs[t][1, at]
+            real_high, real_low, imag_high, imag_low = (pieces[t][i, at].astype(F32) for i in range(4))
+            both = (real_high + real_low) * backs[t][0, at] + (imag_high + imag_low) * backs[t][1, at]
             total += fold(both[:, :LANES] + both[:, LANES:])
     out_ref[...] += total
 
@@ -622,10 +606,10 @@
     return pl.pallas_call(
         curvature_kernel,
         grid=(2,),
-        in_specs=[pl.BlockSpec((4, 2, SIZE, SIZE), lambda i: (i, 0, 0, 0)), MAPS_SPEC, VECTOR_SPEC],
-        out_specs=pl.BlockSpec((8, LANES), lambda i: (0, 0)),
+        in_specs=[GRAM_SPEC, IN_VMEM, IN_VMEM],
+        out_specs=IN_VMEM,
         out_shape=jax.ShapeDtypeStruct((8, LANES), F32),
-        scratch_shapes=[pltpu.VMEM((2, SIZE, SIZE), BF16)] * 4 + BACKS,
+        scratch_shapes=PIECES + BACKS,
         compiler_params=params(),
         name="curvature",
     )(grams, maps, vector)
@@ -656,7 +640,13 @@
 
 def share(sums, curve, last, after):
     return pl.pallas_call(
-        share_kernel, out_shape=jax.ShapeDtypeStruct((ALL, 1, LANES), F32), name="share"
+        share_kernel,
+        grid=(1,),
+        in_specs=[IN_VMEM] * 4,
+        out_specs=pl.BlockSpec((ALL, 1, LANES), lambda i: (0, 0, 0)),
+        out_shape=jax.ShapeDtypeStruct((ALL, 1, LANES), F32),
+        compiler_params=params(),
+        name="share",
     )(sums, curve, last, after)
 
 
@@ -696,7 +686,11 @@
 def solve(shared, frames, residual, product, frames_after, residual_after, product_after):
     return pl.pallas_call(
         solve_kernel,
+        grid=(1,),
+        in_specs=[IN_VMEM] * 7,
+        out_specs=pl.BlockSpec((ROW_SHARDS, 3, ROWS, LANES), lambda i: (0, 0, 0, 0)),
         out_shape=jax.ShapeDtypeStruct((ROW_SHARDS, 3, ROWS, LANES), F32),
+        compiler_params=params(),
         name="solve",
     )(shared, frames, residual, product, frames_after, residual_after, product_after)
 
@@ -738,10 +732,14 @@
 
 
 def finish(back, auxiliary, scaled_dual):
-    image = jax.ShapeDtypeStruct((2, PHASES, ROWS, SIZE), F32)
+    image = jax.ShapeDtypeStruct(auxiliary.shape, F32)
     return pl.pallas_call(
         finish_kernel,
+        grid=(1,),
+        in_specs=[whole_spec(value) for value in (back, auxiliary, scaled_dual)],
+        out_specs=[whole_spec(image)] * 3 + [pl.BlockSpec((ALL, 1, LANES), lambda i: (0, 0, 0))],
         out_shape=[image, image, image, jax.ShapeDtypeStruct((ALL, 1, LANES), F32)],
+        compiler_params=params(),
         name="finish",
     )(back, auxiliary, scaled_dual)
 
@@ -788,12 +786,17 @@
     own = lax.dynamic_slice_in_dim(sampling, lax.axis_index("row") * ROWS, ROWS, 1)
     own = own.astype(F32).reshape(1, LINES)
 
-    packed = pack_first(own, lines, *(in_hbm(v) for v in (coil_maps, frames, auxiliary, scaled_dual)))
+    packed = pack_image(*(in_hbm(v) for v in (coil_maps, frames, auxiliary, scaled_dual)))
     image = exchange(packed, "row")
-    lines, own, late_sampling, packed = lax.optimization_barrier((lines, own, sampling, packed))
-    packed = pack_more(own, lines, 1, 0, MAIN)
-    late_sampling, packed = lax.optimization_barrier((late_sampling, packed))
+    lines, own, packed = lax.optimization_barrier((lines, own, packed))
+    packed = pack_measured(own, lines, 0, MAIN)
+    packed, late_sampling = lax.optimization_barrier((packed, sampling))
+    received = exchange(packed, "row")
+
     grams = in_hbm(gram_tables(late_sampling.astype(F32)[:, None, :], table))
+    maps, frames_cols, splits, first, last = receive(image)
+    frames_before, frames_after = shift(last, 1), shift(first, -1)
+    residual = start(grams, maps, frames_cols)
 
     acquired = late_sampling.reshape(PHASES, ROW_SHARDS, ROWS)
     by_phase = jnp.sum(acquired, 2, keepdims=True)
@@ -801,27 +804,14 @@
     overflow = jnp.max(number) > MAIN
     window, index = windows(number, acquired, 0, MAIN)
     line_table = in_hbm(line_tables(index, table))
-    image, packed, grams, line_table, window, overflow = lax.optimization_barrier(
-        (image, packed, grams, line_table, window, overflow)
+    residual, first, last = adjoint(
+        window, line_table, maps, received, residual, frames_cols, splits, frames_before, frames_after
     )
-    lines_imag = in_hbm(exchange(packed, "row"))
-    image = in_hbm(image)
-
-    maps, frames_cols, splits, first, last = receive(image)
-    frames_before, frames_after = shift(last, 1), shift(first, -1)
-    residual, _, _ = adjoint(0, IMAGE, window, line_table, maps, image, jnp.zeros((2, SIZE, LANES), F32))
-    residual = start(grams, maps, frames_cols, splits, frames_before, frames_after, residual)
-
-    residual, first, last = adjoint(1, 0, window, line_table, maps, lines_imag, residual)
 
     def more(carry):
-        residual = carry[1]
         window, index = windows(number, acquired, MAIN, EXTRA)
-        line_table = line_tables(index, table)
-        for part in range(2):
-            extra = exchange(pack_more(own, lines, part, MAIN, EXTRA), "row")
-            residual, first, last = adjoint(part, 0, window, line_table, maps, extra, residual)
-        return jnp.array(False), residual, first, last
+        extra = exchange(pack_measured(own, lines, MAIN, EXTRA), "row")
+        return jnp.array(False), *adjoint(window, line_tables(index, table), maps, extra, carry[1])
 
     _, residual, first, last = lax.while_loop(
         lambda carry: carry[0], more, (overflow, residual, first, last)

time: 168 us -> 146 us (0.87)
  Pallas kernels: 68.3 us -> 51.9 us
  blocking collectives: 52.8 us -> 43 us
  local copies, waits for them, and re-layouts: 7.31 us -> 10.6 us
    all_to_all x3, blocking collectives: 52.8 us -> 43 us  [exchange(): return lax.all_to_all(value, axes, 0, 0, tiled=True)]
    pallas_call x11 -> x10, Pallas kernels: 52.5 us -> 43.6 us  [the longest x1 8.91 us: pack_measured(): pl.pallas_call(functools.partial(pack_measured_kernel, base), grid=(2, PA...]
    unnamed x26 -> x32, local copies, waits for them, and re-layouts: 5.75 us -> 10.3 us
    pallas_call x1, Pallas kernels: 6.26 us -> 2.48 us  [line_tables(): pl.pallas_call(line_table_kernel, grid=(PHASES,), in_specs=[pl.BlockSpec(...]
    pallas_call x1, Pallas kernels: 7.37 us -> 4.82 us  [gram_tables(): pl.pallas_call(gram_table_kernel, grid=(PHASES,), in_specs=[pl.BlockSpec(...]
    ppermute x5, starting transfers between devices: 11.5 us -> 13.8 us  [shift(): return lax.ppermute(value, 'phase', pairs)]
    all_to_all x2, starting transfers between devices: 13 us -> 11.2 us  [exchange(): return lax.all_to_all(value, axes, 0, 0, tiled=True)]
  transfers between devices with their start and end apart: 7 -> 7, of which waited for: 1 -> 2; matrix products, arithmetic and copies ran while one was open for 4% -> 4% of each run, Pallas kernels for 27% -> 26%
where the time goes in v3:
time: 146 us; the launch traced here: 145 us
  Pallas kernels  51.9 us (36%)
  blocking collectives  43 us (29%)
  starting transfers between devices  25 us (17%)
  local copies, waits for them, and re-layouts  10.6 us (7%)
  waiting for transfers between devices  8.41 us (6%)
  other arithmetic  4.89 us (3%)
  between operations  1.55 us (1%)
    all_to_all x3, blocking collectives, exchange(): return lax.all_to_all(value, axes, 0, 0, tiled=True)  43 us
    ppermute x5, starting transfers between devices, shift(): return lax.ppermute(value, 'phase', pairs)  13.8 us
    all_to_all x2, starting transfers between devices, exchange(): return lax.all_to_all(value, axes, 0, 0, tiled=True)  11.2 us
    unnamed x32, local copies, waits for them, and re-layouts  10.3 us
    pallas_call x1, Pallas kernels, pack_measured(): pl.pallas_call(functools.partial(pack_measured_kernel, base), grid=(2, PA...  8.91 us
    all_to_all x2, waiting for transfers between devices, exchange(): return lax.all_to_all(value, axes, 0, 0, tiled=True)  8.4 us
    pallas_call x1, Pallas kernels, adjoint(): pl.pallas_call(functools.partial(adjoint_kernel, len(local_terms)), grid_...  8.2 us
    pallas_call x1, Pallas kernels, gram_apply(): pl.pallas_call(gram_kernel, grid=(2,), in_specs=[GRAM_SPEC, IN_VMEM, IN_V...  7.86 us
  transfers between devices with their start and end apart: 7, of which 2 were waited for; matrix products, arithmetic and copies ran while one was open for 4% of the time, Pallas kernels for 26%

profile of v3, /device:TPU:1, one launch (start us, length us, event | category | flops | bytes accessed | tf_op | source)
XLA Modules:
  0.0 145.3 jit_solution(13532116427859757751)
XLA Ops:
  0.6 0.0 copy-start.19
  0.6 2.8 %pack_image.1 = f32[16,64,256]{2,1,0:T(8,128)} custom-call(f32[16,2,16,256]{3,2,1,0:T(8,128)} %maps_ref.1, f32[2,8,16,256]{3,2,1,0:T(8,128)} %frames_ref.1, f32[2,8,16,256]{3,2,1,0:T(8,128)} %aux_ref.3, f32[2,8,16,256]{3,2,1,0:T(8,128)} %dual_ref.3), custom_call_target="tpu_custom_call" | custom-call | tf_op jit(solution)/shard_map/pack_image/pallas_call | solution.py:258
  3.4 6.8 %all-to-all-start.1 = ((f32[16,64,256]{2,1,0:T(8,128)}), f32[16,64,256]{2,1,0:T(8,128)S(1)}, u32[]{:S(2)}, u32[]{:S(2)}) async-start(f32[16,64,256]{2,1,0:T(8,128)} %pack_image.1), calls=%async_computation.1 | async-start | bytes 2097152 | tf_op jit(solution)/shard_map/all_to_all | solution.py:764
  10.3 0.0 copy-done.19
  10.3 0.1 dynamic-slice_convert_fusion
  10.3 0.1 reshape.141.weight_ref
  10.4 8.9 %pack_measured_0.1 = f32[16,176,256]{2,1,0:T(8,128)} custom-call(f32[1,128]{1,0:T(1,128)S(1)} %reshape.141.weight_ref, f32[16,2,128,256]{3,2,1,0:T(8,128)} %bitcast.in_ref), custom_call_target="tpu_custom_call" | custom-call | tf_op jit(solution)/shard_map/pack_measured_0/pallas_call | solution.py:282
  19.3 6.6 %all-to-all-done.1.image_ref = f32[16,64,256]{2,1,0:T(8,128)S(1)} async-done(((f32[16,64,256]{2,1,0:T(8,128)}), f32[16,64,256]{2,1,0:T(8,128)S(1)}, u32[]{:S(2)}, u32[]{:S(2)}) %all-to-all-start.1) | async-done | bytes 1048608 | tf_op jit(solution)/shard_map/all_to_all | solution.py:764
  26.0 1.0 copy-done.5
  26.9 4.4 %all-to-all-start.2 = ((f32[16,176,256]{2,1,0:T(8,128)}), f32[16,176,256]{2,1,0:T(8,128)S(1)}, u32[]{:S(2)}, u32[]{:S(2)}) async-start(f32[16,176,256]{2,1,0:T(8,128)} %pack_measured_0.1), calls=%async_computation.2 | async-start | bytes 5767168 | tf_op jit(solution)/shard_map/all_to_all | solution.py:764
  31.3 0.1 reshape.142
  31.4 0.2 reduce_sum.36
  31.6 1.4 reduce_window_sum.22
  33.0 0.1 broadcast_compare_fusion.4
  33.1 0.2 fusion.1
  33.4 0.1 add_add_fusion.1
  33.5 0.7 broadcast_add_fusion.3
  34.1 1.5 %select_reduce_fusion.1 = s32[8,16,16]{2,1,0:T(8,128)S(1)} fusion(s32[16,16]{1,0:T(8,128)S(1)} %add_add_fusion.1, s32[8,16,16]{2,1,0:T(8,128)S(1)} %get-tuple-element.183, s32[8,16,16]{2,1,0:T(8,128)S(1)} %get-tuple-element.181, pred[8,16,16]{2,1,0:T(8,128)(4,1)S(1)} %get-tuple-element.184, pred[8,16,16]{2,1,0:T(8,128)(4,1)S(1)} %get-tuple-element.176, ...), kind=kLoop, calls=%fused_computation.10 | loop fusion | flops 194560 | bytes 31744 | tf_op jit(solution)/shard_map/reduce_sum | solution.py:775
  35.6 0.0 copy-start.6
  35.6 1.2 copy-done.6
  36.8 0.9 receive.1
  37.8 0.7 copy-done.11
  38.5 1.6 %collective-permute-start = (f32[2,32,128]{2,1,0:T(8,128)S(1)}, f32[2,32,128]{2,1,0:T(8,128)S(1)}, u32[]{:S(2)}, u32[]{:S(2)}) collective-permute-start(f32[2,32,128]{2,1,0:T(8,128)S(1)} %get-tuple-element.85), channel_id=1, source_target_pairs={{0,16},{16,32},{32,48},{48,64},{64,80},{80,96},{96,112},{112,0},{1... | collective-permute-start | bytes 98312 | tf_op jit(solution)/shard_map/ppermute | solution.py:760
  40.1 4.5 %collective-permute-start.1 = (f32[2,32,128]{2,1,0:T(8,128)S(1)}, f32[2,32,128]{2,1,0:T(8,128)S(1)}, u32[]{:S(2)}, u32[]{:S(2)}) collective-permute-start(f32[2,32,128]{2,1,0:T(8,128)S(1)} %get-tuple-element.86), channel_id=1, source_target_pairs={{0,112},{16,0},{32,16},{48,32},{64,48},{80,64},{96,80},{112,96},{1... | collective-permute-start | bytes 98312 | tf_op jit(solution)/shard_map/ppermute | solution.py:760
  44.6 0.7 copy.29
  45.3 0.1 reshape.143.window_ref
  45.4 0.7 copy.28
  46.1 0.1 sub.49.index_ref
  46.2 0.0 copy-start.7
  46.2 1.0 copy-done.7
  47.2 4.8 %gram_tables.1.gram_ref = bf16[8,4,256,256]{3,2,1,0:T(8,128)(2,1)S(1)} custom-call(f32[8,1,256]{2,1,0:T(1,128)S(1)} %broadcast_in_dim.40.weight_ref, bf16[4,256,256]{2,1,0:T(8,128)(2,1)S(1)} %copy-done.7), custom_call_target="tpu_custom_call" | custom-call | tf_op jit(solution)/shard_map/gram_tables/pallas_call | solution.py:362
  52.1 0.0 copy-start.2
  52.1 1.9 %copy-done.2 = bf16[8,4,256,256]{3,2,1,0:T(8,128)(2,1)} copy-done((bf16[8,4,256,256]{3,2,1,0:T(8,128)(2,1)}, bf16[8,4,256,256]{3,2,1,0:T(8,128)(2,1)S(1)}, u32[]{:S(2)}) %copy-start.2) | copy-done | bytes 4194328
  54.0 0.0 copy-done.8
  54.0 2.5 %line_tables.2.tables_ref = bf16[8,4,256,256]{3,2,1,0:T(8,128)(2,1)S(1)} custom-call(s32[8,1,256]{2,1,0:T(1,128)S(1)} %sub.49.index_ref, bf16[4,256,256]{2,1,0:T(8,128)(2,1)S(1)} %copy-done.8), custom_call_target="tpu_custom_call" | custom-call | tf_op jit(solution)/shard_map/line_tables/pallas_call | solution.py:305
  56.5 0.0 copy-start.3
  56.5 2.0 %copy-done.3 = bf16[8,4,256,256]{3,2,1,0:T(8,128)(2,1)} copy-done((bf16[8,4,256,256]{3,2,1,0:T(8,128)(2,1)}, bf16[8,4,256,256]{3,2,1,0:T(8,128)(2,1)S(1)}, u32[]{:S(2)}) %copy-start.3) | copy-done | bytes 4194328
  59.2 6.7 %start.1.in_ref = f32[2,256,128]{2,1,0:T(8,128)S(1)} custom-call(bf16[8,4,256,256]{3,2,1,0:T(8,128)(2,1)} %copy-done.2, f32[2,256,256]{2,1,0:T(8,128)} %get-tuple-element.203.maps_ref, f32[2,256,128]{2,1,0:T(8,128)S(1)} %get-tuple-element.83.frames_ref.refs_0_), custom_call_target="tpu_custom_call" | custom-call | tf_op jit(solution)/shard_map/start/pallas_call | solution.py:411
  65.9 0.0 collective-permute-done.refs_2_
  65.9 0.0 collective-permute-done.1.refs_3_.frames_after_ref
  65.9 1.8 %all-to-all-done.2.lines_ref = f32[16,176,256]{2,1,0:T(8,128)S(1)} async-done(((f32[16,176,256]{2,1,0:T(8,128)}), f32[16,176,256]{2,1,0:T(8,128)S(1)}, u32[]{:S(2)}, u32[]{:S(2)}) %all-to-all-start.2) | async-done | bytes 2883616 | tf_op jit(solution)/shard_map/all_to_all | solution.py:764
  67.7 0.9 copy-done.12
  68.6 8.2 %adjoint.2 = (f32[2,256,128]{2,1,0:T(8,128)}, f32[2,32,128]{2,1,0:T(8,128)}, f32[2,32,128]{2,1,0:T(8,128)}) custom-call(s32[128]{0:T(128)S(1)} %reshape.143.window_ref, bf16[8,4,256,256]{3,2,1,0:T(8,128)(2,1)} %copy-done.3, f32[2,256,256]{2,1,0:T(8,128)} %get-tuple-element.203.maps_ref, f32[16,176,256]{2,1,0:T(8,128)S(1)} %all-to-all-done.2.lines_ref, ...), custom_call_target="tpu_custom_call" | custom-call | tf_op jit(solution)/shard_map/adjoint/pallas_call | solution.py:486
  76.8 0.0 copy-start.16
  76.9 1.7 %collective-permute-start.2 = (f32[2,32,128]{2,1,0:T(8,128)}, f32[2,32,128]{2,1,0:T(8,128)S(1)}, u32[]{:S(2)}, u32[]{:S(2)}) collective-permute-start(f32[2,32,128]{2,1,0:T(8,128)} %get-tuple-element.91), channel_id=1, source_target_pairs={{0,16},{16,32},{32,48},{48,64},{64,80},{80,96},{96,112},{112,0},{1... | collective-permute-start | bytes 98312 | tf_op jit(solution)/shard_map/ppermute | solution.py:760
  78.5 4.5 %collective-permute-start.3 = (f32[2,32,128]{2,1,0:T(8,128)}, f32[2,32,128]{2,1,0:T(8,128)S(1)}, u32[]{:S(2)}, u32[]{:S(2)}) collective-permute-start(f32[2,32,128]{2,1,0:T(8,128)} %get-tuple-element.92), channel_id=1, source_target_pairs={{0,112},{16,0},{32,16},{48,32},{64,48},{80,64},{96,80},{112,96},{1... | collective-permute-start | bytes 98312 | tf_op jit(solution)/shard_map/ppermute | solution.py:760
  83.1 7.9 %gram_apply.1.gram_ref = f32[2,256,128]{2,1,0:T(8,128)S(1)} custom-call(bf16[8,4,256,256]{3,2,1,0:T(8,128)(2,1)} %copy-done.2, f32[2,256,256]{2,1,0:T(8,128)} %get-tuple-element.233, f32[2,256,128]{2,1,0:T(8,128)} %get-tuple-element.90.in_ref.first_ref.residual_ref), custom_call_target="tpu_custom_call" | custom-call | tf_op jit(solution)/shard_map/gram_apply/pallas_call | solution.py:519
  90.9 0.0 copy-start.9
  90.9 0.0 copy-start.10
  91.0 0.0 collective-permute-done.2.before_ref
  91.0 0.0 collective-permute-done.3.after_ref.residual_after_ref
  91.0 1.3 normal.1
  92.3 1.5 %collective-permute-start.4 = (f32[2,32,128]{2,1,0:T(8,128)S(1)}, f32[2,32,128]{2,1,0:T(8,128)S(1)}, u32[]{:S(2)}, u32[]{:S(2)}) collective-permute-start(f32[2,32,128]{2,1,0:T(8,128)S(1)} %get-tuple-element.96), channel_id=1, source_target_pairs={{0,112},{16,0},{32,16},{48,32},{64,48},{80,64},{96,80},{112,96},{1... | collective-permute-start | bytes 98312 | tf_op jit(solution)/shard_map/ppermute | solution.py:760
  93.8 6.2 %curvature.1.curve_ref = f32[8,128]{1,0:T(8,128)S(1)} custom-call(bf16[8,4,256,256]{3,2,1,0:T(8,128)(2,1)} %copy-done.2, f32[2,256,256]{2,1,0:T(8,128)S(1)} %copy-done.14, f32[2,256,128]{2,1,0:T(8,128)S(1)} %get-tuple-element.94.in_ref.product_ref), custom_call_target="tpu_custom_call" | custom-call | tf_op jit(solution)/shard_map/curvature/pallas_call | solution.py:606
  99.9 0.0 collective-permute-done.4.after_ref.product_after_ref
  99.9 0.1 share.1
  100.1 17.4 %all_to_all.31.shared_ref = f32[128,1,128]{2,1,0:T(1,128)S(1)} all-to-all(f32[128,1,128]{2,1,0:T(1,128)S(1)} %share.1), channel_id=1, replica_groups=mesh['phase'=8,'row'=16] {'phase','row'}, dimensions={0} | all-to-all | bytes 131072 | tf_op jit(solution)/shard_map/all_to_all | solution.py:764
  117.4 0.4 solve.1
  117.8 11.8 %all_to_all.32.in_ref = f32[16,3,16,128]{3,2,1,0:T(8,128)S(1)} all-to-all(f32[16,3,16,128]{3,2,1,0:T(8,128)S(1)} %solve.1), channel_id=1, replica_groups=mesh['phase'=8,'row'=16] {'row'}, dimensions={0} | all-to-all | bytes 786432 | tf_op jit(solution)/shard_map/all_to_all | solution.py:764
  129.7 0.0 copy-done.10
  129.7 1.2 finish.1
  130.8 13.8 %all_to_all.33 = f32[128,1,128]{2,1,0:T(1,128)S(1)} all-to-all(f32[128,1,128]{2,1,0:T(1,128)S(1)} %get-tuple-element.100), channel_id=1, replica_groups=mesh['phase'=8,'row'=16] {'phase','row'}, dimensions={0} | all-to-all | bytes 131072 | tf_op jit(solution)/shard_map/all_to_all | solution.py:764
  144.7 0.2 slice_reduce_fusion
  144.8 0.5 sqrt_multiply_fusion
  (19 shorter events, 0.1 us)
Async XLA Ops:
  0.6 9.6 %copy-start.19 = (s32[8,256]{1,0:T(8,128)S(1)}, s32[8,256]{1,0:T(8,128)}, u32[]{:S(2)}) copy-start(s32[8,256]{1,0:T(8,128)} %param.15) | copy-start | bytes 24580
  3.4 22.5 %all-to-all-start.1 = ((f32[16,64,256]{2,1,0:T(8,128)}), f32[16,64,256]{2,1,0:T(8,128)S(1)}, u32[]{:S(2)}, u32[]{:S(2)}) async-start(f32[16,64,256]{2,1,0:T(8,128)} %pack_image.1), calls=%async_computation.1 | async-start | bytes 2097152 | tf_op jit(solution)/shard_map/all_to_all | solution.py:764
  26.0 1.0 copy-start.5
  26.9 40.7 %all-to-all-start.2 = ((f32[16,176,256]{2,1,0:T(8,128)}), f32[16,176,256]{2,1,0:T(8,128)S(1)}, u32[]{:S(2)}, u32[]{:S(2)}) async-start(f32[16,176,256]{2,1,0:T(8,128)} %pack_measured_0.1), calls=%async_computation.2 | async-start | bytes 5767168 | tf_op jit(solution)/shard_map/all_to_all | solution.py:764
  35.6 1.2 copy-start.6
  37.8 0.7 copy-start.11
  38.5 27.4 %collective-permute-start = (f32[2,32,128]{2,1,0:T(8,128)S(1)}, f32[2,32,128]{2,1,0:T(8,128)S(1)}, u32[]{:S(2)}, u32[]{:S(2)}) collective-permute-start(f32[2,32,128]{2,1,0:T(8,128)S(1)} %get-tuple-element.85), channel_id=1, source_target_pairs={{0,16},{16,32},{32,48},{48,64},{64,80},{80,96},{96,112},{112,0},{1... | collective-permute-start | bytes 98312 | tf_op jit(solution)/shard_map/ppermute | solution.py:760
  40.1 25.8 %collective-permute-start.1 = (f32[2,32,128]{2,1,0:T(8,128)S(1)}, f32[2,32,128]{2,1,0:T(8,128)S(1)}, u32[]{:S(2)}, u32[]{:S(2)}) collective-permute-start(f32[2,32,128]{2,1,0:T(8,128)S(1)} %get-tuple-element.86), channel_id=1, source_target_pairs={{0,112},{16,0},{32,16},{48,32},{64,48},{80,64},{96,80},{112,96},{1... | collective-permute-start | bytes 98312 | tf_op jit(solution)/shard_map/ppermute | solution.py:760
  46.2 1.0 copy-start.7
  47.2 6.8 %copy-start.8 = (bf16[4,256,256]{2,1,0:T(8,128)(2,1)S(1)}, bf16[4,256,256]{2,1,0:T(8,128)(2,1)}, u32[]{:S(2)}) copy-start(bf16[4,256,256]{2,1,0:T(8,128)(2,1)} %constant.63.clone.tables_ref) | copy-start | bytes 1572868
  52.1 2.0 %copy-start.2 = (bf16[8,4,256,256]{3,2,1,0:T(8,128)(2,1)}, bf16[8,4,256,256]{3,2,1,0:T(8,128)(2,1)S(1)}, u32[]{:S(2)}) copy-start(bf16[8,4,256,256]{3,2,1,0:T(8,128)(2,1)S(1)} %gram_tables.1.gram_ref) | copy-start | bytes 12582916
  56.5 2.0 %copy-start.3 = (bf16[8,4,256,256]{3,2,1,0:T(8,128)(2,1)}, bf16[8,4,256,256]{3,2,1,0:T(8,128)(2,1)S(1)}, u32[]{:S(2)}) copy-start(bf16[8,4,256,256]{3,2,1,0:T(8,128)(2,1)S(1)} %line_tables.2.tables_ref) | copy-start | bytes 12582916
  67.7 1.0 copy-start.12
  68.6 8.2 %copy-start.17 = (s32[8,16,16]{1,0,2:T(8,128)S(1)}, s32[8,16,16]{1,0,2:T(8,128)}, u32[]{:S(2)}) copy-start(s32[8,16,16]{1,0,2:T(8,128)} %copy.28) | copy-start | bytes 24580
  76.8 14.2 %copy-start.16 = (f32[2,256,128]{2,1,0:T(8,128)S(1)}, f32[2,256,128]{2,1,0:T(8,128)}, u32[]{:S(2)}) copy-start(f32[2,256,128]{2,1,0:T(8,128)} %get-tuple-element.90.in_ref.first_ref.residual_ref) | copy-start | bytes 786436
  76.8 16.9 %copy-start.14 = (f32[2,256,256]{2,1,0:T(8,128)S(1)}, f32[2,256,256]{2,1,0:T(8,128)}, u32[]{:S(2)}) copy-start(f32[2,256,256]{2,1,0:T(8,128)} %get-tuple-element.233) | copy-start | bytes 1572868
  76.9 14.1 %collective-permute-start.2 = (f32[2,32,128]{2,1,0:T(8,128)}, f32[2,32,128]{2,1,0:T(8,128)S(1)}, u32[]{:S(2)}, u32[]{:S(2)}) collective-permute-start(f32[2,32,128]{2,1,0:T(8,128)} %get-tuple-element.91), channel_id=1, source_target_pairs={{0,16},{16,32},{32,48},{48,64},{64,80},{80,96},{96,112},{112,0},{1... | collective-permute-start | bytes 98312 | tf_op jit(solution)/shard_map/ppermute | solution.py:760
  78.5 12.4 %collective-permute-start.3 = (f32[2,32,128]{2,1,0:T(8,128)}, f32[2,32,128]{2,1,0:T(8,128)S(1)}, u32[]{:S(2)}, u32[]{:S(2)}) collective-permute-start(f32[2,32,128]{2,1,0:T(8,128)} %get-tuple-element.92), channel_id=1, source_target_pairs={{0,112},{16,0},{32,16},{48,32},{64,48},{80,64},{96,80},{112,96},{1... | collective-permute-start | bytes 98312 | tf_op jit(solution)/shard_map/ppermute | solution.py:760
  90.9 38.7 %copy-start.9 = (f32[2,8,16,256]{3,2,1,0:T(8,128)S(1)}, f32[2,8,16,256]{3,2,1,0:T(8,128)}, u32[]{:S(2)}) copy-start(f32[2,8,16,256]{3,2,1,0:T(8,128)} %aux_ref.3) | copy-start | bytes 786436
  90.9 38.7 %copy-start.10 = (f32[2,8,16,256]{3,2,1,0:T(8,128)S(1)}, f32[2,8,16,256]{3,2,1,0:T(8,128)}, u32[]{:S(2)}) copy-start(f32[2,8,16,256]{3,2,1,0:T(8,128)} %dual_ref.3) | copy-start | bytes 786436
  92.3 7.6 %collective-permute-start.4 = (f32[2,32,128]{2,1,0:T(8,128)S(1)}, f32[2,32,128]{2,1,0:T(8,128)S(1)}, u32[]{:S(2)}, u32[]{:S(2)}) collective-permute-start(f32[2,32,128]{2,1,0:T(8,128)S(1)} %get-tuple-element.96), channel_id=1, source_target_pairs={{0,112},{16,0},{32,16},{48,32},{64,48},{80,64},{96,80},{112,96},{1... | collective-permute-start | bytes 98312 | tf_op jit(solution)/shard_map/ppermute | solution.py:760
  93.8 51.0 %copy-start.20 = (f32[2]{0:T(128)S(1)}, f32[2]{0:T(128)}, u32[]{:S(2)}) copy-start(f32[2]{0:T(128)} %constant.64.clone) | copy-start | bytes 28

commit v4 on v3

--- a/solution.py
+++ b/solution.py
@@ -154,8 +154,11 @@
     return out_real[:, :LANES] + out_real[:, LANES:], out_imag[:, :LANES] + out_imag[:, LANES:]
 
 
-def chunks(step):
-    return [slice(row, row + step) for row in range(0, SIZE, step)]
+def row_pairs(step):
+    half = SIZE // 2
+    return [
+        (slice(row, row + step), slice(half + row, half + row + step)) for row in range(0, half, step)
+    ]
 
 
 def store_split(ref, which, at, value):
@@ -164,32 +167,39 @@
 
 def expand(vector_ref, maps_ref, pieces):
     half = pl.program_id(0)
-    for at in chunks(32):
-        real = spread_half(vector_ref[0, at], half)
-        imag = spread_half(vector_ref[1, at], half)
+    for near, far in row_pairs(16):
+        values = [
+            [spread_half(vector_ref[part, at], half) for part in range(2)] for at in (near, far)
+        ]
         for t in range(4):
-            image_real, image_imag = images_of(maps_ref, at, real[t], imag[t])
-            store_split(pieces[t], 0, at, image_real)
-            store_split(pieces[t], 2, at, image_imag)
+            real, imag = images_of(maps_ref, near, values[0][0][t], values[0][1][t])
+            far_real, far_imag = images_of(maps_ref, far, values[1][0][t], values[1][1][t])
+            store_split(pieces[t], 0, near, real + far_real)
+            store_split(pieces[t], 0, far, imag - far_imag)
+            store_split(pieces[t], 2, near, imag + far_imag)
+            store_split(pieces[t], 2, far, far_real - real)
 
 
 def reduce(maps_ref, backs, finish):
-    for at in chunks(32):
-        maps = maps_at(maps_ref, at)
-        terms = [combine(*maps, backs[t][0, at], backs[t][1, at]) for t in range(4)]
-        finish(at, sum_four([term[0] for term in terms]), sum_four([term[1] for term in terms]))
+    for near, far in row_pairs(32):
+        near_maps, far_maps = maps_at(maps_ref, near), maps_at(maps_ref, far)
+        near_terms, far_terms = [], []
+        for t in range(4):
+            p_even, p_odd, q_even, q_odd = (
+                backs[t][which, at] for which in range(2) for at in (near, far)
+            )
+            near_terms.append(combine(*near_maps, p_even - q_odd, q_even + p_odd))
+            far_terms.append(combine(*far_maps, p_even + q_odd, q_even - p_odd))
+        for at, terms in ((near, near_terms), (far, far_terms)):
+            finish(at, *(sum_four([term[part] for term in terms]) for part in range(2)))
 
 
 def products(tables_ref, pieces, backs):
     for t in range(4):
-        real_high, real_low, imag_high, imag_low = (pieces[t][i] for i in range(4))
-        table_real, table_imag, low_real, low_imag = (tables_ref[t, i] for i in range(4))
-        backs[t][0] = (
-            dot(table_real, real_high) + dot(table_real, real_low) + dot(low_real, real_high)
-        ) - (dot(table_imag, imag_high) + dot(table_imag, imag_low) + dot(low_imag, imag_high))
-        backs[t][1] = (
-            dot(table_real, imag_high) + dot(table_real, imag_low) + dot(low_real, imag_high)
-        ) + (dot(table_imag, real_high) + dot(table_imag, real_low) + dot(low_imag, real_high))
+        high, low = tables_ref[t, 0], tables_ref[t, 1]
+        for which in range(2):
+            value_high, value_low = pieces[t][2 * which], pieces[t][2 * which + 1]
+            backs[t][which] = dot(high, value_high) + dot(high, value_low) + dot(low, value_high)
 
 
 def in_step(rows):
@@ -203,8 +213,8 @@
     return high, middle, (value - middle.astype(F32)).astype(BF16)
 
 
-def compact(weight_ref, in_ref, lines_ref, base, at_step):
-    count = lines_ref.shape[1]
+def compact(weight_ref, turn_ref, in_ref, lines_ref, base, at_step):
+    count = lines_ref.shape[2]
     weight = jnp.broadcast_to(weight_ref[...], (8, LINES))
     row = lax.broadcasted_iota(jnp.int32, (LINES, LINES), 0)
     col = lax.broadcasted_iota(jnp.int32, (LINES, LINES), 1)
@@ -215,20 +225,28 @@
     line = lax.broadcasted_iota(jnp.int32, (count, LINES), 0) + (base + 1)
     select = jnp.where((number == line) & acquired, 1.0, 0.0).astype(BF16)
     step = in_ref.shape[0]
+    cos, sin = (jnp.concatenate([turn_ref[i]] * 2, 1) for i in range(2))
     for c in range(step):
-        high, middle, low = split_three(in_ref[c, 0])
-        lines_ref[at_step * step + c] = (
-            dot(select, high) + dot(select, middle) + dot(select, low)
-        )
+        real, imag = in_ref[c, 0], in_ref[c, 1]
+        for part, value in enumerate((real * cos - imag * sin, real * sin + imag * cos)):
+            high, middle, low = split_three(value)
+            lines_ref[part, at_step * step + c] = (
+                dot(select, high) + dot(select, middle) + dot(select, low)
+            )
 
 
 def pack_lines(lines_ref, out_ref):
-    for row in range(0, lines_ref.shape[1], 8):
-        at = slice(row, row + 8)
-        halves = [(lines_ref[c, at, :LANES], lines_ref[c, at, LANES:]) for c in range(COILS)]
-        for j, (low, high) in enumerate(gather_coils(halves)):
-            out_ref[j, at, :LANES] = low
-            out_ref[j, at, LANES:] = high
+    count = lines_ref.shape[2]
+    for part in range(2):
+        for row in range(0, count, 8):
+            at = slice(row, row + 8)
+            to = slice(part * count + row, part * count + row + 8)
+            halves = [
+                (lines_ref[part, c, at, :LANES], lines_ref[part, c, at, LANES:]) for c in range(COILS)
+            ]
+            for j, (low, high) in enumerate(gather_coils(halves)):
+                out_ref[j, to, :LANES] = low
+                out_ref[j, to, LANES:] = high
 
 
 def pack_image_kernel(maps_ref, frames_ref, aux_ref, dual_ref, out_ref):
@@ -269,36 +287,37 @@
 PACK_STEPS = 4
 
 
-def pack_measured_kernel(base, weight_ref, in_ref, out_ref, lines_ref):
-    step = pl.program_id(1)
-    compact(weight_ref, in_ref, lines_ref, base, step)
+def pack_measured_kernel(base, weight_ref, turn_ref, in_ref, out_ref, lines_ref):
+    step = pl.program_id(0)
+    compact(weight_ref, turn_ref, in_ref, lines_ref, base, step)
 
     @pl.when(step == PACK_STEPS - 1)
     def _():
         pack_lines(lines_ref, out_ref)
 
 
-def pack_measured(weight, measured, base, count):
+def pack_measured(weight, turn, measured, base, count):
     return pl.pallas_call(
         functools.partial(pack_measured_kernel, base),
-        grid=(2, PACK_STEPS),
+        grid=(PACK_STEPS,),
         in_specs=[
             whole_spec(weight),
-            pl.BlockSpec((COILS // PACK_STEPS, 1, LINES, SIZE), lambda part, i: (i, part, 0, 0)),
+            whole_spec(turn),
+            pl.BlockSpec((COILS // PACK_STEPS, 2, LINES, SIZE), lambda i: (i, 0, 0, 0)),
         ],
-        out_specs=pl.BlockSpec((ROW_SHARDS, count, SIZE), lambda part, i: (0, part, 0)),
+        out_specs=pl.BlockSpec((ROW_SHARDS, 2 * count, SIZE), lambda i: (0, 0, 0)),
         out_shape=jax.ShapeDtypeStruct((ROW_SHARDS, 2 * count, SIZE), F32),
-        scratch_shapes=[pltpu.VMEM((COILS, count, SIZE), F32)],
+        scratch_shapes=[pltpu.VMEM((2, COILS, count, SIZE), F32)],
         compiler_params=params(),
         name=f"pack_measured_{base}",
-    )(weight, measured)
+    )(weight, turn, measured)
 
 
 def line_table_kernel(index_ref, tables_ref, out_ref):
     row = lax.broadcasted_iota(jnp.int32, (SIZE, SIZE), 0)
     select = jnp.where(row == index_ref[0], 1.0, 0.0).astype(BF16)
-    for i, table in enumerate((0, 2, 1, 3)):
-        out_ref[0, i] = dot(tables_ref[table], select).astype(BF16)
+    for i in range(2):
+        out_ref[0, i] = dot(tables_ref[i], select).astype(BF16)
 
 
 def line_tables(index, tables):
@@ -306,26 +325,40 @@
         line_table_kernel,
         grid=(PHASES,),
         in_specs=[pl.BlockSpec((1, 1, SIZE), lambda t: (t, 0, 0)), whole_spec(tables)],
-        out_specs=pl.BlockSpec((1, 4, SIZE, SIZE), lambda t: (t, 0, 0, 0)),
-        out_shape=jax.ShapeDtypeStruct((PHASES, 4, SIZE, SIZE), BF16),
+        out_specs=pl.BlockSpec((1, 2, SIZE, SIZE), lambda t: (t, 0, 0, 0)),
+        out_shape=jax.ShapeDtypeStruct((PHASES, 2, SIZE, SIZE), BF16),
         compiler_params=params(),
         name="line_tables",
     )(index, tables)
+
+
+def reverse_eight(value):
+    row = lax.broadcasted_iota(jnp.int32, value.shape, 0)
+    value = pltpu.roll(value, 4, 0)
+    for bit in (2, 1):
+        value = jnp.where((row & bit) != 0, pltpu.roll(value, bit, 0), pltpu.roll(value, 8 - bit, 0))
+    return value
 
 
 def receive_kernel(image_ref, maps_ref, frames_ref, splits_ref, first_ref, last_ref):
     for part in range(2):
         lanes = slice(part * LANES, (part + 1) * LANES)
         for block in range(ROW_SHARDS):
+            turned = block >= ROW_SHARDS // 2
+            source = ROW_SHARDS + ROW_SHARDS // 2 - 1 - block if turned else block
             for half in range(2):
                 row = block * ROWS + half * 8
                 at = slice(row, row + 8)
+                start = 32 * (1 - half if turned else half)
                 maps, frames, splits = (
-                    slice(half * 32 + which * 8, half * 32 + (which + 1) * 8) for which in (part, 2, 3)
+                    image_ref[source, start + which * 8 : start + (which + 1) * 8, columns]
+                    for which, columns in ((part, slice(0, SIZE)), (2, lanes), (3, lanes))
                 )
-                maps_ref[part, at] = image_ref[block, maps]
-                frames_ref[part, at] = image_ref[block, frames, lanes]
-                splits_ref[part, at] = image_ref[block, splits, lanes]
+                if turned:
+                    maps, frames, splits = (reverse_eight(v) for v in (maps, frames, splits))
+                maps_ref[part, at] = maps
+                frames_ref[part, at] = frames
+                splits_ref[part, at] = splits
         first_ref[part] = fold_phase(frames_ref[part], 0)
         last_ref[part] = fold_phase(frames_ref[part] + splits_ref[part], PHASES - 1)
 
@@ -344,18 +377,9 @@
 
 def gram_table_kernel(weight_ref, tables_ref, out_ref):
     weight = weight_ref[0]
-    cos_high, cos_low, sin_high, sin_low = (tables_ref[i] for i in range(4))
-
-    def scaled(table):
-        return (table.astype(F32) * weight).astype(BF16)
-
-    cos_w = scaled(cos_high), scaled(cos_low)
-    sin_w = scaled(sin_high), scaled(sin_low)
-    cos, sin = (cos_high, cos_low), (sin_high, sin_low)
-    real = dot3(cos_w, cos) + dot3(sin_w, sin)
-    imag = dot3(sin_w, cos) - dot3(cos_w, sin)
-    out_ref[0, 0], out_ref[0, 2] = split(real)
-    out_ref[0, 1], out_ref[0, 3] = split(imag)
+    left = tuple((tables_ref[i].astype(F32) * weight).astype(BF16) for i in range(2))
+    right = tables_ref[2], tables_ref[3]
+    out_ref[0, 0], out_ref[0, 1] = split(dot3(left, right))
 
 
 def gram_tables(weight, tables):
@@ -366,14 +390,14 @@
             pl.BlockSpec((1, 1, SIZE), lambda t: (t, 0, 0)),
             pl.BlockSpec((4, SIZE, SIZE), lambda t: (0, 0, 0)),
         ],
-        out_specs=pl.BlockSpec((1, 4, SIZE, SIZE), lambda t: (t, 0, 0, 0)),
-        out_shape=jax.ShapeDtypeStruct((PHASES, 4, SIZE, SIZE), BF16),
+        out_specs=pl.BlockSpec((1, 2, SIZE, SIZE), lambda t: (t, 0, 0, 0)),
+        out_shape=jax.ShapeDtypeStruct((PHASES, 2, SIZE, SIZE), BF16),
         compiler_params=params(),
         name="gram_tables",
     )(weight, tables)
 
 
-GRAM_SPEC = pl.BlockSpec((4, 4, SIZE, SIZE), lambda i, *_: (i, 0, 0, 0))
+GRAM_SPEC = pl.BlockSpec((4, 2, SIZE, SIZE), lambda i, *_: (i, 0, 0, 0))
 IMAGE_SPEC = pl.BlockSpec((ROW_SHARDS, IMAGE, SIZE), lambda *_: (0, 0, 0))
 MAPS_SPEC = pl.BlockSpec((2, SIZE, SIZE), lambda *_: (0, 0, 0))
 VECTOR_SPEC = pl.BlockSpec((2, SIZE, LANES), lambda *_: (0, 0, 0))
@@ -389,12 +413,21 @@
     return pltpu.CompilerParams(vmem_limit_bytes=16 << 20)
 
 
-def start_kernel(gram_ref, maps_ref, frames_ref, out_ref, *scratch):
+def start_kernel(gram_ref, maps_ref, frames_ref, splits_ref, in_ref, out_ref, *scratch):
     pieces, backs = scratch[:4], scratch[4:]
 
     @pl.when(pl.program_id(0) == 0)
     def _():
-        out_ref[...] = jnp.zeros_like(out_ref)
+        group = lane_group(FOLD)
+        for row in range(0, SIZE, FOLD):
+            at = slice(row, row + FOLD)
+            for part in range(2):
+                frames, splits = frames_ref[part, at], splits_ref[part, at]
+                ahead = pltpu.roll(frames, LANES - GROUP, 1)
+                behind = pltpu.roll(frames + splits, GROUP, 1)
+                gap = splits - (jnp.where(group == PHASES - 1, 0.0, ahead) - frames)
+                gap_behind = jnp.where(group == 0, 0.0, behind) - frames
+                out_ref[part, at] = in_ref[part, at] + PENALTY * (gap_behind - gap) - DAMPING * frames
 
     expand(frames_ref, maps_ref, pieces)
     products(gram_ref, pieces, backs)
@@ -407,42 +440,32 @@
     reduce(maps_ref, backs, finish)
 
 
-def start(grams, maps, frames):
+def start(grams, maps, frames, splits, so_far):
     return pl.pallas_call(
         start_kernel,
         grid=(2,),
-        in_specs=[GRAM_SPEC] + [IN_VMEM] * 2,
+        in_specs=[GRAM_SPEC] + [IN_VMEM] * 4,
         out_specs=VECTOR_SPEC,
         out_shape=VECTOR,
         scratch_shapes=PIECES + BACKS,
         compiler_params=params(),
         name="start",
-    )(grams, maps, frames)
-
-
-def add_local(frames_ref, splits_ref, before_ref, after_ref, in_ref, out_ref):
+    )(grams, maps, frames, splits, so_far)
+
+
+def add_edges(before_ref, after_ref, in_ref, out_ref):
     group = lane_group(FOLD)
     for i in range(8):
         at = slice(i * FOLD, (i + 1) * FOLD)
         for part in range(2):
-            frames, splits = frames_ref[part, at], splits_ref[part, at]
-            ahead = jnp.where(
-                group == PHASES - 1,
-                unfold_phase(after_ref[part], PHASES - 1, i),
-                pltpu.roll(frames, LANES - GROUP, 1),
-            )
-            behind = jnp.where(
-                group == 0,
-                unfold_phase(before_ref[part], 0, i),
-                pltpu.roll(frames + splits, GROUP, 1),
-            )
-            gap = splits - (ahead - frames)
-            gap_behind = behind - frames
-            out_ref[part, at] = in_ref[part, at] + PENALTY * (gap_behind - gap) - DAMPING * frames
-
-
-def adjoint_kernel(local_terms, window_ref, tables_ref, maps_ref, lines_ref, in_ref, *refs):
-    locals_in, refs = refs[:local_terms], refs[local_terms:]
+            before = unfold_phase(before_ref[part], 0, i)
+            after = unfold_phase(after_ref[part], PHASES - 1, i)
+            edge = jnp.where(group == 0, before, jnp.where(group == PHASES - 1, after, 0.0))
+            out_ref[part, at] = in_ref[part, at] + PENALTY * edge
+
+
+def adjoint_kernel(edges, window_ref, tables_ref, maps_ref, lines_ref, in_ref, *refs):
+    edges_in, refs = refs[:edges], refs[edges:]
     out_ref, first_ref, last_ref = refs[:3]
     pieces, backs = refs[3:7], refs[7:]
     half = pl.program_id(0)
@@ -450,8 +473,8 @@
 
     @pl.when(half == 0)
     def _():
-        if local_terms:
-            add_local(*locals_in, in_ref, out_ref)
+        if edges:
+            add_edges(*edges_in, in_ref, out_ref)
         else:
             out_ref[...] = in_ref[...]
 
@@ -482,20 +505,20 @@
             last_ref[which] = fold_phase(value, PHASES - 1)
 
 
-def adjoint(window, tables, maps, lines, so_far, *local_terms):
-    return pl.pallas_call(
-        functools.partial(adjoint_kernel, len(local_terms)),
+def adjoint(window, tables, maps, lines, so_far, *edges):
+    return pl.pallas_call(
+        functools.partial(adjoint_kernel, len(edges)),
         grid_spec=pltpu.PrefetchScalarGridSpec(
             num_scalar_prefetch=1,
             grid=(2,),
-            in_specs=[GRAM_SPEC] + [IN_VMEM] * (3 + len(local_terms)),
+            in_specs=[GRAM_SPEC] + [IN_VMEM] * (3 + len(edges)),
             out_specs=[IN_VMEM] * 3,
             scratch_shapes=PIECES + BACKS,
         ),
         out_shape=[VECTOR, FOLDED, FOLDED],
         compiler_params=params(),
         name="adjoint",
-    )(window, tables, maps, lines, so_far, *local_terms)
+    )(window, tables, maps, lines, so_far, *edges)
 
 
 def gram_kernel(gram_ref, maps_ref, in_ref, out_ref, *scratch):
@@ -503,14 +526,10 @@
     expand(in_ref, maps_ref, pieces)
     products(gram_ref, pieces, backs)
 
-    @pl.when(pl.program_id(0) == 0)
-    def _():
-        out_ref[...] = jnp.zeros_like(out_ref)
-
     def finish(at, real, imag):
         keep = in_step(at.stop - at.start)
         for part, value in enumerate((real, imag)):
-            out_ref[part, at] += jnp.where(keep, value, 0.0)
+            out_ref[part, at] = jnp.where(keep, value, out_ref[part, at])
 
     reduce(maps_ref, backs, finish)
 
@@ -594,10 +613,11 @@
     expand(in_ref, maps_ref, pieces)
     products(gram_ref, pieces, backs)
     total = 0.0
-    for at in chunks(32):
+    for row in range(0, SIZE, 32):
+        at = slice(row, row + 32)
         for t in range(4):
-            real_high, real_low, imag_high, imag_low = (pieces[t][i, at].astype(F32) for i in range(4))
-            both = (real_high + real_low) * backs[t][0, at] + (imag_high + imag_low) * backs[t][1, at]
+            p_high, p_low, q_high, q_low = (pieces[t][i, at].astype(F32) for i in range(4))
+            both = (p_high + p_low) * backs[t][0, at] + (q_high + q_low) * backs[t][1, at]
             total += fold(both[:, :LANES] + both[:, LANES:])
     out_ref[...] += total
 
@@ -663,24 +683,33 @@
     second = fresh / bend
     by_first = alpha + second * gamma
     by_image = -second * alpha
-    group = lane_group(ROWS)
+    group = lane_group(8)
     for j in range(ROW_SHARDS):
-        at = slice(j * ROWS, (j + 1) * ROWS)
-        piece, half = j // 2, slice(j % 2 * ROWS, (j % 2 + 1) * ROWS)
-        edge = []
-        for part in range(2):
-            out_ref[j, part] = (
+        turned = j >= ROW_SHARDS // 2
+        block = ROW_SHARDS + ROW_SHARDS // 2 - 1 - j if turned else j
+        for row in range(0, ROWS, 8):
+            at = slice(block * ROWS + row, block * ROWS + row + 8)
+            piece, start = divmod(at.start, FOLD)
+            folded = slice(start, start + 8)
+            values = [
                 frames_ref[part, at]
                 + by_first * residual_ref[part, at]
                 + by_image * product_ref[part, at]
-            )
-            after = (
-                frames_after_ref[part, half]
-                + by_first * residual_after_ref[part, half]
-                + by_image * product_after_ref[part, half]
-            )
-            edge.append(roll(after, part - piece))
-        out_ref[j, 2] = jnp.where(group == 0, edge[0], edge[1])
+                for part in range(2)
+            ]
+            edge = [
+                roll(
+                    frames_after_ref[part, folded]
+                    + by_first * residual_after_ref[part, folded]
+                    + by_image * product_after_ref[part, folded],
+                    part - piece,
+                )
+                for part in range(2)
+            ]
+            values.append(jnp.where(group == 0, edge[0], edge[1]))
+            to = slice(ROWS - 8 - row, ROWS - row) if turned else slice(row, row + 8)
+            for which, value in enumerate(values):
+                out_ref[j, which, to] = reverse_eight(value) if turned else value
 
 
 def solve(shared, frames, residual, product, frames_after, residual_after, product_after):
@@ -745,14 +774,16 @@
 
 
 def tables():
-    index = np.arange(SIZE)
-    angle = (index[:, None] * index[None, :] % SIZE) * (2.0 * math.pi / SIZE)
-    out = []
-    for table in (np.cos(angle), np.sin(angle)):
-        table = (table / math.sqrt(SIZE)).astype(np.float32)
-        high = table.astype(BF16)
-        out += [high, (table - high.astype(np.float32)).astype(BF16)]
-    return np.stack(out)
+    k = np.arange(SIZE)
+    x = np.arange(SIZE // 2)
+    unit = 2.0 * math.pi / (2 * SIZE)
+    angle = (k[None, :] * (2 * x[:, None] - (SIZE - 1)) % (2 * SIZE)) * unit
+    table = (np.concatenate([np.cos(angle), np.sin(angle)]) / math.sqrt(SIZE)).astype(np.float32)
+    high = table.astype(BF16)
+    low = (table - high.astype(np.float32)).astype(BF16)
+    turn = (k * (SIZE - 1) % (2 * SIZE)) * unit
+    turn = np.stack([np.cos(turn), np.sin(turn)]).astype(np.float32)
+    return np.stack([high, low, high.T, low.T]), turn
 
 
 def shift(value, steps):
@@ -781,40 +812,45 @@
 
 
 def local(frames, auxiliary, scaled_dual, coil_maps, measured, sampling):
-    table = jnp.asarray(tables())
+    table, turn = (jnp.asarray(value) for value in tables())
     lines = measured.reshape(COILS, 2, LINES, SIZE)
     own = lax.dynamic_slice_in_dim(sampling, lax.axis_index("row") * ROWS, ROWS, 1)
     own = own.astype(F32).reshape(1, LINES)
 
     packed = pack_image(*(in_hbm(v) for v in (coil_maps, frames, auxiliary, scaled_dual)))
     image = exchange(packed, "row")
-    lines, own, packed = lax.optimization_barrier((lines, own, packed))
-    packed = pack_measured(own, lines, 0, MAIN)
+    lines, own, turn, packed = lax.optimization_barrier((lines, own, turn, packed))
+    turn = lax.dynamic_slice_in_dim(turn, lax.axis_index("row") * ROWS, ROWS, 1)
+    turn = jnp.broadcast_to(turn[:, None, :, None], (2, PHASES, ROWS, LANES)).reshape(2, LINES, LANES)
+    packed = pack_measured(own, turn, lines, 0, MAIN)
     packed, late_sampling = lax.optimization_barrier((packed, sampling))
-    received = exchange(packed, "row")
-
-    grams = in_hbm(gram_tables(late_sampling.astype(F32)[:, None, :], table))
-    maps, frames_cols, splits, first, last = receive(image)
-    frames_before, frames_after = shift(last, 1), shift(first, -1)
-    residual = start(grams, maps, frames_cols)
-
     acquired = late_sampling.reshape(PHASES, ROW_SHARDS, ROWS)
     by_phase = jnp.sum(acquired, 2, keepdims=True)
     number = jnp.cumsum(acquired, 2) + jnp.cumsum(by_phase, 0) - by_phase
     overflow = jnp.max(number) > MAIN
+
+    def more(carry):
+        window, index = windows(number, acquired, MAIN, EXTRA)
+        maps = receive(image)[0]
+        extra = exchange(pack_measured(own, turn, lines, MAIN, EXTRA), "row")
+        residual, _, _ = adjoint(window, line_tables(index, table), maps, extra, carry[1])
+        return jnp.array(False), residual
+
+    _, residual = lax.while_loop(
+        lambda carry: carry[0], more, (overflow, jnp.zeros((2, SIZE, LANES), F32))
+    )
+    packed, residual = lax.optimization_barrier((packed, residual))
+    received = exchange(packed, "row")
+
+    grams = in_hbm(gram_tables(late_sampling.astype(F32)[:, None, :], table))
+    maps, frames_cols, splits, first, last = receive(image)
+    frames_before, frames_after = shift(last, 1), shift(first, -1)
+    residual = start(grams, maps, frames_cols, splits, residual)
+
     window, index = windows(number, acquired, 0, MAIN)
     line_table = in_hbm(line_tables(index, table))
     residual, first, last = adjoint(
-        window, line_table, maps, received, residual, frames_cols, splits, frames_before, frames_after
-    )
-
-    def more(carry):
-        window, index = windows(number, acquired, MAIN, EXTRA)
-        extra = exchange(pack_measured(own, lines, MAIN, EXTRA), "row")
-        return jnp.array(False), *adjoint(window, line_tables(index, table), maps, extra, carry[1])
-
-    _, residual, first, last = lax.while_loop(
-        lambda carry: carry[0], more, (overflow, residual, first, last)
+        window, line_table, maps, received, residual, frames_before, frames_after
     )
 
     residual_before = shift(last, 1)

time: 146 us -> 141 us (0.966)
  Pallas kernels: 51.9 us -> 37.4 us
  waiting for transfers between devices: 8.41 us -> 14.2 us
  blocking collectives: 43 us -> 45.6 us
    pallas_call x2, Pallas kernels: 17.1 us -> 10.9 us  [the longest x1 5.76 us: adjoint(): pl.pallas_call(functools.partial(adjoint_kernel, len(edges)), grid_spec=p...]
    all_to_all x2, waiting for transfers between devices: 8.4 us -> 14.1 us  [exchange(): return lax.all_to_all(value, axes, 0, 0, tiled=True)]
    pallas_call x1, Pallas kernels: 7.86 us -> 4.97 us  [gram_apply(): pl.pallas_call(gram_kernel, grid=(2,), in_specs=[GRAM_SPEC, IN_VMEM, IN_V...]
    pallas_call x1, Pallas kernels: 4.82 us -> 2.25 us  [gram_tables(): pl.pallas_call(gram_table_kernel, grid=(PHASES,), in_specs=[pl.BlockSpec(...]
    all_to_all x3, blocking collectives: 43 us -> 45.6 us  [exchange(): return lax.all_to_all(value, axes, 0, 0, tiled=True)]
    pallas_call x1, Pallas kernels: 6.15 us -> 4.34 us  [curvature(): pl.pallas_call(curvature_kernel, grid=(2,), in_specs=[GRAM_SPEC, IN_VMEM,...]
    unnamed x32 -> x44, local copies, waits for them, and re-layouts: 10.3 us -> 8.58 us
    pallas_call x1, Pallas kernels: 6.72 us -> 5.21 us  [start(): pl.pallas_call(start_kernel, grid=(2,), in_specs=[GRAM_SPEC] + [IN_VMEM]...]
  transfers between devices with their start and end apart: 7 -> 7, of which waited for: 2 -> 2; matrix products, arithmetic and copies ran while one was open for 4% -> 5% of each run, Pallas kernels for 26% -> 18%
where the time goes in v4:
time: 141 us
  blocking collectives  45.6 us (32%)
  Pallas kernels  37.4 us (27%)
  starting transfers between devices  25.2 us (18%)
  waiting for transfers between devices  14.2 us (10%)
  local copies, waits for them, and re-layouts  11.2 us (8%)
  other arithmetic  5.6 us (4%)
  between operations  1.6 us (1%)
    all_to_all x3, blocking collectives, exchange(): return lax.all_to_all(value, axes, 0, 0, tiled=True)  45.6 us
    all_to_all x2, waiting for transfers between devices, exchange(): return lax.all_to_all(value, axes, 0, 0, tiled=True)  14.1 us
    ppermute x5, starting transfers between devices, shift(): return lax.ppermute(value, 'phase', pairs)  13.8 us
    all_to_all x2, starting transfers between devices, exchange(): return lax.all_to_all(value, axes, 0, 0, tiled=True)  11.4 us
    unnamed x44, local copies, waits for them, and re-layouts  8.58 us
    pallas_call x1, Pallas kernels, adjoint(): pl.pallas_call(functools.partial(adjoint_kernel, len(edges)), grid_spec=p...  5.76 us
    pallas_call x1, Pallas kernels, start(): pl.pallas_call(start_kernel, grid=(2,), in_specs=[GRAM_SPEC] + [IN_VMEM]...  5.21 us
    pallas_call x1, Pallas kernels, pack_measured(): pl.pallas_call(functools.partial(pack_measured_kernel, base), grid=(PACK_...  5.13 us
  transfers between devices with their start and end apart: 7, of which 2 were waited for; matrix products, arithmetic and copies ran while one was open for 5% of the time, Pallas kernels for 18%

profile of v4, /device:TPU:1, one launch (start us, length us, event | category | flops | bytes accessed | tf_op | source)
XLA Modules:
  0.0 140.7 jit_solution(3743611932092387084)
XLA Ops:
  0.6 0.0 copy-start.23
  0.6 0.0 copy-start.21
  0.7 2.8 %pack_image.1 = f32[16,64,256]{2,1,0:T(8,128)} custom-call(f32[16,2,16,256]{3,2,1,0:T(8,128)} %maps_ref.1, f32[2,8,16,256]{3,2,1,0:T(8,128)} %frames_ref.1, f32[2,8,16,256]{3,2,1,0:T(8,128)} %aux_ref.3, f32[2,8,16,256]{3,2,1,0:T(8,128)} %dual_ref.3), custom_call_target="tpu_custom_call" | custom-call | tf_op jit(solution)/shard_map/pack_image/pallas_call | solution.py:276
  3.4 6.8 %all-to-all-start.1 = ((f32[16,64,256]{2,1,0:T(8,128)}), f32[16,64,256]{2,1,0:T(8,128)}, u32[]{:S(2)}, u32[]{:S(2)}) async-start(f32[16,64,256]{2,1,0:T(8,128)} %pack_image.1), calls=%async_computation.1 | async-start | bytes 2097152 | tf_op jit(solution)/shard_map/all_to_all | solution.py:795
  10.3 0.1 dynamic-slice_convert_fusion
  10.4 0.6 reshape.144.weight_ref
  11.0 0.1 constant_dynamic-slice_fusion
  11.0 0.1 broadcast_in_dim.52
  11.1 0.1 broadcast_in_dim.53.turn_ref
  11.2 5.1 %pack_measured_0.1 = f32[16,176,256]{2,1,0:T(8,128)S(1)} custom-call(f32[1,128]{1,0:T(1,128)} %reshape.144.weight_ref, f32[2,128,128]{2,1,0:T(8,128)S(1)} %broadcast_in_dim.53.turn_ref, f32[16,2,128,256]{3,2,1,0:T(8,128)} %bitcast.4), custom_call_target="tpu_custom_call" | custom-call | tf_op jit(solution)/shard_map/pack_measured_0/pallas_call | solution.py:300
  16.4 1.6 %copy-done.5 = f32[16,176,256]{2,1,0:T(8,128)} copy-done((f32[16,176,256]{2,1,0:T(8,128)}, f32[16,176,256]{2,1,0:T(8,128)S(1)}, u32[]{:S(2)}) %copy-start.5) | copy-done | bytes 2883608
  17.9 0.1 reshape.145
  18.0 0.2 reduce_sum.36
  18.2 1.4 reduce_window_sum.22
  19.6 0.1 copy.30
  19.7 0.7 fusion.4
  20.5 0.1 copy.29
  21.2 4.9 %all-to-all-done.1.image_ref = f32[16,64,256]{2,1,0:T(8,128)} async-done(((f32[16,64,256]{2,1,0:T(8,128)}), f32[16,64,256]{2,1,0:T(8,128)}, u32[]{:S(2)}, u32[]{:S(2)}) %all-to-all-start.1) | async-done | bytes 1048608 | tf_op jit(solution)/shard_map/all_to_all | solution.py:795
  26.1 0.7 broadcast_in_dim.56
  26.8 0.0 copy-start.22
  26.8 4.5 %all-to-all-start.2 = ((f32[16,176,256]{2,1,0:T(8,128)}), f32[16,176,256]{2,1,0:T(8,128)S(1)}, u32[]{:S(2)}, u32[]{:S(2)}) async-start(f32[16,176,256]{2,1,0:T(8,128)} %copy-done.5), calls=%async_computation.2 | async-start | bytes 5767168 | tf_op jit(solution)/shard_map/all_to_all | solution.py:795
  31.4 0.2 fusion.3
  31.6 0.1 add_add_fusion.1
  31.7 0.1 iota_add_fusion.1
  31.8 1.5 %select_reduce_fusion.1 = s32[8,16,16]{2,1,0:T(8,128)S(1)} fusion(s32[16,16]{1,0:T(8,128)S(1)} %add_add_fusion.1, s32[8,16,16]{2,1,0:T(8,128)S(1)} %get-tuple-element.195, s32[8,16,16]{2,1,0:T(8,128)S(1)} %get-tuple-element.196, pred[8,16,16]{2,1,0:T(8,128)(4,1)S(1)} %get-tuple-element.194, pred[8,16,16]{2,1,0:T(8,128)(4,1)S(1)} %get-tuple-element.193, ...), kind=kLoop, calls=%fused_computation.11 | loop fusion | flops 194560 | bytes 31744 | tf_op jit(solution)/shard_map/reduce_sum | solution.py:806
  33.3 2.1 %receive.2 = (f32[2,256,256]{2,1,0:T(8,128)S(1)}, f32[2,256,128]{2,1,0:T(8,128)S(1)}, f32[2,256,128]{2,1,0:T(8,128)S(1)}, f32[2,32,128]{2,1,0:T(8,128)}, f32[2,32,128]{2,1,0:T(8,128)S(1)}) custom-call(f32[16,64,256]{2,1,0:T(8,128)} %all-to-all-done.1.image_ref), custom_call_target="tpu_custom_call" | custom-call | tf_op jit(solution)/shard_map/receive/pallas_call | solution.py:367
  35.4 0.7 copy-done.10
  36.1 0.7 copy-done.15
  36.8 6.1 %collective-permute-start.1 = (f32[2,32,128]{2,1,0:T(8,128)}, f32[2,32,128]{2,1,0:T(8,128)S(1)}, u32[]{:S(2)}, u32[]{:S(2)}) collective-permute-start(f32[2,32,128]{2,1,0:T(8,128)} %get-tuple-element.87), channel_id=1, source_target_pairs={{0,112},{16,0},{32,16},{48,32},{64,48},{80,64},{96,80},{112,96},{1... | collective-permute-start | bytes 98312 | tf_op jit(solution)/shard_map/ppermute | solution.py:791
  42.9 0.0 collective-permute-start
  42.9 0.6 broadcast_add_fusion.2
  43.5 0.1 reshape.146.window_ref
  43.6 0.9 sub.49.index_ref
  44.5 0.0 copy-start.7
  44.5 1.0 copy-done.7
  45.6 2.2 %gram_tables.1.gram_ref = bf16[8,2,256,256]{3,2,1,0:T(8,128)(2,1)S(1)} custom-call(f32[8,1,256]{2,1,0:T(1,128)S(1)} %broadcast_in_dim.57.weight_ref, bf16[4,256,256]{2,1,0:T(8,128)(2,1)S(1)} %copy-done.7), custom_call_target="tpu_custom_call" | custom-call | tf_op jit(solution)/shard_map/gram_tables/pallas_call | solution.py:386
  47.9 1.3 copy-done
  49.2 1.9 %line_tables.2.tables_ref = bf16[8,2,256,256]{3,2,1,0:T(8,128)(2,1)S(1)} custom-call(s32[8,1,256]{2,1,0:T(1,128)S(1)} %sub.49.index_ref, bf16[4,256,256]{2,1,0:T(8,128)(2,1)S(1)} %copy-done.7), custom_call_target="tpu_custom_call" | custom-call | tf_op jit(solution)/shard_map/line_tables/pallas_call | solution.py:324
  51.1 1.3 copy-done.6
  52.5 5.2 %start.1.in_ref = f32[2,256,128]{2,1,0:T(8,128)S(1)} custom-call(bf16[8,2,256,256]{3,2,1,0:T(8,128)(2,1)} %copy-done, f32[2,256,256]{2,1,0:T(8,128)S(1)} %get-tuple-element.79.maps_ref, f32[2,256,128]{2,1,0:T(8,128)S(1)} %copy-done.11, f32[2,256,128]{2,1,0:T(8,128)S(1)} %copy-done.16, f32[2,256,128]{2,1,0:T(8,128)} %get-tuple-element.85.in_ref), custom_call_target="tpu_custom_call" | custom-call | tf_op jit(solution)/shard_map/start/pallas_call | solution.py:444
  57.7 0.0 copy-start.8
  57.7 0.7 copy-done.8
  58.4 0.0 collective-permute-done.1.refs_1_.frames_after_ref
  58.4 0.0 collective-permute-done.refs_0_
  58.4 9.3 %all-to-all-done.2.lines_ref = f32[16,176,256]{2,1,0:T(8,128)S(1)} async-done(((f32[16,176,256]{2,1,0:T(8,128)}), f32[16,176,256]{2,1,0:T(8,128)S(1)}, u32[]{:S(2)}, u32[]{:S(2)}) %all-to-all-start.2) | async-done | bytes 2883616 | tf_op jit(solution)/shard_map/all_to_all | solution.py:795
  67.7 0.9 copy-done.9
  68.6 5.8 %adjoint.2 = (f32[2,256,128]{2,1,0:T(8,128)S(1)}, f32[2,32,128]{2,1,0:T(8,128)S(1)}, f32[2,32,128]{2,1,0:T(8,128)S(1)}) custom-call(s32[128]{0:T(128)S(1)} %reshape.146.window_ref, bf16[8,2,256,256]{3,2,1,0:T(8,128)(2,1)} %copy-done.6, f32[2,256,256]{2,1,0:T(8,128)S(1)} %get-tuple-element.79.maps_ref, f32[16,176,256]{2,1,0:T(8,128)S(1)} %all-to-all-done.2.lines_ref, ...), custom_call_target="tpu_custom_call" | custom-call | tf_op jit(solution)/shard_map/adjoint/pallas_call | solution.py:509
  74.4 1.7 %collective-permute-start.2 = (f32[2,32,128]{2,1,0:T(8,128)S(1)}, f32[2,32,128]{2,1,0:T(8,128)S(1)}, u32[]{:S(2)}, u32[]{:S(2)}) collective-permute-start(f32[2,32,128]{2,1,0:T(8,128)S(1)} %get-tuple-element.89), channel_id=1, source_target_pairs={{0,16},{16,32},{32,48},{48,64},{64,80},{80,96},{96,112},{112,0},{1... | collective-permute-start | bytes 98312 | tf_op jit(solution)/shard_map/ppermute | solution.py:791
  76.1 4.5 %collective-permute-start.3 = (f32[2,32,128]{2,1,0:T(8,128)S(1)}, f32[2,32,128]{2,1,0:T(8,128)S(1)}, u32[]{:S(2)}, u32[]{:S(2)}) collective-permute-start(f32[2,32,128]{2,1,0:T(8,128)S(1)} %get-tuple-element.90), channel_id=1, source_target_pairs={{0,112},{16,0},{32,16},{48,32},{64,48},{80,64},{96,80},{112,96},{1... | collective-permute-start | bytes 98312 | tf_op jit(solution)/shard_map/ppermute | solution.py:791
  80.6 5.0 %gram_apply.1.gram_ref = f32[2,256,128]{2,1,0:T(8,128)S(1)} custom-call(bf16[8,2,256,256]{3,2,1,0:T(8,128)(2,1)} %copy-done, f32[2,256,256]{2,1,0:T(8,128)S(1)} %get-tuple-element.79.maps_ref, f32[2,256,128]{2,1,0:T(8,128)S(1)} %get-tuple-element.88.in_ref.first_ref.residual_ref), custom_call_target="tpu_custom_call" | custom-call | tf_op jit(solution)/shard_map/gram_apply/pallas_call | solution.py:538
  85.6 0.0 copy-start.12
  85.6 0.0 collective-permute-done.2.before_ref
  85.6 1.3 normal.1
  87.0 1.5 %collective-permute-start.4 = (f32[2,32,128]{2,1,0:T(8,128)S(1)}, f32[2,32,128]{2,1,0:T(8,128)S(1)}, u32[]{:S(2)}, u32[]{:S(2)}) collective-permute-start(f32[2,32,128]{2,1,0:T(8,128)S(1)} %get-tuple-element.94), channel_id=1, source_target_pairs={{0,112},{16,0},{32,16},{48,32},{64,48},{80,64},{96,80},{112,96},{1... | collective-permute-start | bytes 98312 | tf_op jit(solution)/shard_map/ppermute | solution.py:791
  88.4 4.3 %curvature.1.curve_ref = f32[8,128]{1,0:T(8,128)S(1)} custom-call(bf16[8,2,256,256]{3,2,1,0:T(8,128)(2,1)} %copy-done, f32[2,256,256]{2,1,0:T(8,128)S(1)} %get-tuple-element.79.maps_ref, f32[2,256,128]{2,1,0:T(8,128)S(1)} %get-tuple-element.92.in_ref.product_ref), custom_call_target="tpu_custom_call" | custom-call | tf_op jit(solution)/shard_map/curvature/pallas_call | solution.py:626
  92.8 0.0 copy-start.24
  92.8 0.1 share.1
  92.9 19.9 %all_to_all.32.shared_ref = f32[128,1,128]{2,1,0:T(1,128)S(1)} all-to-all(f32[128,1,128]{2,1,0:T(1,128)S(1)} %share.1), channel_id=1, replica_groups=mesh['phase'=8,'row'=16] {'phase','row'}, dimensions={0} | all-to-all | bytes 131072 | tf_op jit(solution)/shard_map/all_to_all | solution.py:795
  112.8 0.4 solve.1
  113.2 11.8 %all_to_all.33.in_ref = f32[16,3,16,128]{3,2,1,0:T(8,128)S(1)} all-to-all(f32[16,3,16,128]{3,2,1,0:T(8,128)S(1)} %solve.1), channel_id=1, replica_groups=mesh['phase'=8,'row'=16] {'row'}, dimensions={0} | all-to-all | bytes 786432 | tf_op jit(solution)/shard_map/all_to_all | solution.py:795
  125.1 1.2 finish.1
  126.2 13.8 %all_to_all.34 = f32[128,1,128]{2,1,0:T(1,128)S(1)} all-to-all(f32[128,1,128]{2,1,0:T(1,128)S(1)} %get-tuple-element.98), channel_id=1, replica_groups=mesh['phase'=8,'row'=16] {'phase','row'}, dimensions={0} | all-to-all | bytes 131072 | tf_op jit(solution)/shard_map/all_to_all | solution.py:795
  140.1 0.2 slice_reduce_fusion
  140.2 0.5 sqrt_multiply_fusion
  (36 shorter events, 0.1 us)
Async XLA Ops:
  0.6 10.3 %copy-start.23 = (f32[2,256]{1,0:T(2,128)S(1)}, f32[2,256]{1,0:T(2,128)}, u32[]{:S(2)}) copy-start(f32[2,256]{1,0:T(2,128)} %constant.67.clone) | copy-start | bytes 6148
  0.6 9.6 %copy-start.21 = (s32[8,256]{1,0:T(8,128)S(1)}, s32[8,256]{1,0:T(8,128)}, u32[]{:S(2)}) copy-start(s32[8,256]{1,0:T(8,128)} %param.16) | copy-start | bytes 24580
  3.4 22.6 %all-to-all-start.1 = ((f32[16,64,256]{2,1,0:T(8,128)}), f32[16,64,256]{2,1,0:T(8,128)}, u32[]{:S(2)}, u32[]{:S(2)}) async-start(f32[16,64,256]{2,1,0:T(8,128)} %pack_image.1), calls=%async_computation.1 | async-start | bytes 2097152 | tf_op jit(solution)/shard_map/all_to_all | solution.py:795
  16.4 1.6 %copy-start.5 = (f32[16,176,256]{2,1,0:T(8,128)}, f32[16,176,256]{2,1,0:T(8,128)S(1)}, u32[]{:S(2)}) copy-start(f32[16,176,256]{2,1,0:T(8,128)S(1)} %pack_measured_0.1) | copy-start | bytes 8650756
  18.0 8.8 %copy-start.17 = (s32[8,16,16]{2,1,0:T(8,128)}, s32[8,16,16]{2,1,0:T(8,128)S(1)}, u32[]{:S(2)}) copy-start(s32[8,16,16]{2,1,0:T(8,128)S(1)} %reshape.145) | copy-start | bytes 24580
  20.5 6.4 %copy-start.19 = (s32[8,16,16]{2,1,0:T(8,128)}, s32[8,16,16]{2,1,0:T(8,128)S(1)}, u32[]{:S(2)}) copy-start(s32[8,16,16]{2,1,0:T(8,128)S(1)} %get-tuple-element.189) | copy-start | bytes 24580
  26.8 4.6 %copy-start.18 = (s32[8,16,16]{2,1,0:T(8,128)S(1)}, s32[8,16,16]{2,1,0:T(8,128)}, u32[]{:S(2)}) copy-start(s32[8,16,16]{2,1,0:T(8,128)} %copy-done.17) | copy-start | bytes 24580
  26.8 4.6 %copy-start.20 = (s32[8,16,16]{2,1,0:T(8,128)S(1)}, s32[8,16,16]{2,1,0:T(8,128)}, u32[]{:S(2)}) copy-start(s32[8,16,16]{2,1,0:T(8,128)} %copy-done.19) | copy-start | bytes 24580
  26.8 16.7 %copy-start.22 = (s32[8,256]{1,0:T(8,128)S(1)}, s32[8,256]{1,0:T(8,128)}, u32[]{:S(2)}) copy-start(s32[8,256]{1,0:T(8,128)} %param.16) | copy-start | bytes 24580
  26.8 40.8 %all-to-all-start.2 = ((f32[16,176,256]{2,1,0:T(8,128)}), f32[16,176,256]{2,1,0:T(8,128)S(1)}, u32[]{:S(2)}, u32[]{:S(2)}) async-start(f32[16,176,256]{2,1,0:T(8,128)} %copy-done.5), calls=%async_computation.2 | async-start | bytes 5767168 | tf_op jit(solution)/shard_map/all_to_all | solution.py:795
  35.4 0.7 copy-start.10
  36.1 0.7 copy-start.15
  36.8 21.6 %collective-permute-start.1 = (f32[2,32,128]{2,1,0:T(8,128)}, f32[2,32,128]{2,1,0:T(8,128)S(1)}, u32[]{:S(2)}, u32[]{:S(2)}) collective-permute-start(f32[2,32,128]{2,1,0:T(8,128)} %get-tuple-element.87), channel_id=1, source_target_pairs={{0,112},{16,0},{32,16},{48,32},{64,48},{80,64},{96,80},{112,96},{1... | collective-permute-start | bytes 98312 | tf_op jit(solution)/shard_map/ppermute | solution.py:791
  42.9 15.5 %collective-permute-start = (f32[2,32,128]{2,1,0:T(8,128)S(1)}, f32[2,32,128]{2,1,0:T(8,128)S(1)}, u32[]{:S(2)}, u32[]{:S(2)}) collective-permute-start(f32[2,32,128]{2,1,0:T(8,128)S(1)} %get-tuple-element.86), channel_id=1, source_target_pairs={{0,16},{16,32},{32,48},{48,64},{64,80},{80,96},{96,112},{112,0},{1... | collective-permute-start | bytes 98312 | tf_op jit(solution)/shard_map/ppermute | solution.py:791
  44.5 1.0 copy-start.7
  45.6 6.9 %copy-start.11 = (f32[2,256,128]{2,1,0:T(8,128)S(1)}, f32[2,256,128]{2,1,0:T(8,128)}, u32[]{:S(2)}) copy-start(f32[2,256,128]{2,1,0:T(8,128)} %copy-done.10) | copy-start | bytes 786436
  45.6 6.9 %copy-start.16 = (f32[2,256,128]{2,1,0:T(8,128)S(1)}, f32[2,256,128]{2,1,0:T(8,128)}, u32[]{:S(2)}) copy-start(f32[2,256,128]{2,1,0:T(8,128)} %copy-done.15) | copy-start | bytes 786436
  47.8 1.4 copy-start
  51.1 1.4 copy-start.6
  57.7 0.7 copy-start.8
  67.7 1.0 copy-start.9
  74.4 11.2 %collective-permute-start.2 = (f32[2,32,128]{2,1,0:T(8,128)S(1)}, f32[2,32,128]{2,1,0:T(8,128)S(1)}, u32[]{:S(2)}, u32[]{:S(2)}) collective-permute-start(f32[2,32,128]{2,1,0:T(8,128)S(1)} %get-tuple-element.89), channel_id=1, source_target_pairs={{0,16},{16,32},{32,48},{48,64},{64,80},{80,96},{96,112},{112,0},{1... | collective-permute-start | bytes 98312 | tf_op jit(solution)/shard_map/ppermute | solution.py:791
  76.1 9.5 %collective-permute-start.3 = (f32[2,32,128]{2,1,0:T(8,128)S(1)}, f32[2,32,128]{2,1,0:T(8,128)S(1)}, u32[]{:S(2)}, u32[]{:S(2)}) collective-permute-start(f32[2,32,128]{2,1,0:T(8,128)S(1)} %get-tuple-element.90), channel_id=1, source_target_pairs={{0,112},{16,0},{32,16},{48,32},{64,48},{80,64},{96,80},{112,96},{1... | collective-permute-start | bytes 98312 | tf_op jit(solution)/shard_map/ppermute | solution.py:791
  85.6 27.2 %copy-start.12 = (f32[2,256,128]{2,1,0:T(8,128)S(1)}, f32[2,256,128]{2,1,0:T(8,128)}, u32[]{:S(2)}) copy-start(f32[2,256,128]{2,1,0:T(8,128)} %copy-done.10) | copy-start | bytes 786436
  87.0 5.8 %collective-permute-start.4 = (f32[2,32,128]{2,1,0:T(8,128)S(1)}, f32[2,32,128]{2,1,0:T(8,128)S(1)}, u32[]{:S(2)}, u32[]{:S(2)}) collective-permute-start(f32[2,32,128]{2,1,0:T(8,128)S(1)} %get-tuple-element.94), channel_id=1, source_target_pairs={{0,112},{16,0},{32,16},{48,32},{64,48},{80,64},{96,80},{112,96},{1... | collective-permute-start | bytes 98312 | tf_op jit(solution)/shard_map/ppermute | solution.py:791
  88.4 36.7 %copy-start.13 = (f32[2,8,16,256]{3,2,1,0:T(8,128)S(1)}, f32[2,8,16,256]{3,2,1,0:T(8,128)}, u32[]{:S(2)}) copy-start(f32[2,8,16,256]{3,2,1,0:T(8,128)} %aux_ref.3) | copy-start | bytes 786436
  88.4 36.7 %copy-start.14 = (f32[2,8,16,256]{3,2,1,0:T(8,128)S(1)}, f32[2,8,16,256]{3,2,1,0:T(8,128)}, u32[]{:S(2)}) copy-start(f32[2,8,16,256]{3,2,1,0:T(8,128)} %dual_ref.3) | copy-start | bytes 786436
  92.8 47.4 %copy-start.24 = (f32[2]{0:T(128)S(1)}, f32[2]{0:T(128)}, u32[]{:S(2)}) copy-start(f32[2]{0:T(128)} %constant.68.clone) | copy-start | bytes 28

commit v5 on v4

--- a/solution.py
+++ b/solution.py
@@ -287,13 +287,14 @@
 PACK_STEPS = 4
 
 
-def pack_measured_kernel(base, weight_ref, turn_ref, in_ref, out_ref, lines_ref):
+def pack_measured_kernel(base, weight_ref, turn_ref, in_ref, out_ref, zero_ref, lines_ref):
     step = pl.program_id(0)
     compact(weight_ref, turn_ref, in_ref, lines_ref, base, step)
 
     @pl.when(step == PACK_STEPS - 1)
     def _():
         pack_lines(lines_ref, out_ref)
+        zero_ref[...] = jnp.zeros_like(zero_ref)
 
 
 def pack_measured(weight, turn, measured, base, count):
@@ -305,8 +306,8 @@
             whole_spec(turn),
             pl.BlockSpec((COILS // PACK_STEPS, 2, LINES, SIZE), lambda i: (i, 0, 0, 0)),
         ],
-        out_specs=pl.BlockSpec((ROW_SHARDS, 2 * count, SIZE), lambda i: (0, 0, 0)),
-        out_shape=jax.ShapeDtypeStruct((ROW_SHARDS, 2 * count, SIZE), F32),
+        out_specs=[pl.BlockSpec((ROW_SHARDS, 2 * count, SIZE), lambda i: (0, 0, 0)), VECTOR_SPEC],
+        out_shape=[jax.ShapeDtypeStruct((ROW_SHARDS, 2 * count, SIZE), F32), VECTOR],
         scratch_shapes=[pltpu.VMEM((2, COILS, count, SIZE), F32)],
         compiler_params=params(),
         name=f"pack_measured_{base}",
@@ -822,7 +823,7 @@
     lines, own, turn, packed = lax.optimization_barrier((lines, own, turn, packed))
     turn = lax.dynamic_slice_in_dim(turn, lax.axis_index("row") * ROWS, ROWS, 1)
     turn = jnp.broadcast_to(turn[:, None, :, None], (2, PHASES, ROWS, LANES)).reshape(2, LINES, LANES)
-    packed = pack_measured(own, turn, lines, 0, MAIN)
+    packed, residual = pack_measured(own, turn, lines, 0, MAIN)
     packed, late_sampling = lax.optimization_barrier((packed, sampling))
     acquired = late_sampling.reshape(PHASES, ROW_SHARDS, ROWS)
     by_phase = jnp.sum(acquired, 2, keepdims=True)
@@ -832,20 +833,18 @@
     def more(carry):
         window, index = windows(number, acquired, MAIN, EXTRA)
         maps = receive(image)[0]
-        extra = exchange(pack_measured(own, turn, lines, MAIN, EXTRA), "row")
+        extra = exchange(pack_measured(own, turn, lines, MAIN, EXTRA)[0], "row")
         residual, _, _ = adjoint(window, line_tables(index, table), maps, extra, carry[1])
         return jnp.array(False), residual
 
-    _, residual = lax.while_loop(
-        lambda carry: carry[0], more, (overflow, jnp.zeros((2, SIZE, LANES), F32))
-    )
+    _, residual = lax.while_loop(lambda carry: carry[0], more, (overflow, residual))
     packed, residual = lax.optimization_barrier((packed, residual))
     received = exchange(packed, "row")
 
     grams = in_hbm(gram_tables(late_sampling.astype(F32)[:, None, :], table))
     maps, frames_cols, splits, first, last = receive(image)
     frames_before, frames_after = shift(last, 1), shift(first, -1)
-    residual = start(grams, maps, frames_cols, splits, residual)
+    residual = in_hbm(start(grams, maps, frames_cols, splits, residual))
 
     window, index = windows(number, acquired, 0, MAIN)
     line_table = in_hbm(line_tables(index, table))

time: 141 us -> 140 us (level)
  local copies, waits for them, and re-layouts: 11.2 us -> 9.59 us
    unnamed x44 -> x42, local copies, waits for them, and re-layouts: 8.58 us -> 7.63 us
  transfers between devices with their start and end apart: 7 -> 7, of which waited for: 2 -> 2; matrix products, arithmetic and copies ran while one was open for 5% -> 5% of each run, Pallas kernels for 18% -> 19%
where the time goes in v5:
time: 140 us; the launch traced here: 139 us
  blocking collectives  45.6 us (33%)
  Pallas kernels  38.2 us (27%)
  starting transfers between devices  25.2 us (18%)
  waiting for transfers between devices  13.4 us (10%)
  local copies, waits for them, and re-layouts  9.59 us (7%)
  other arithmetic  5.61 us (4%)
  between operations  1.58 us (1%)
    all_to_all x3, blocking collectives, exchange(): return lax.all_to_all(value, axes, 0, 0, tiled=True)  45.6 us
    ppermute x5, starting transfers between devices, shift(): return lax.ppermute(value, 'phase', pairs)  13.8 us
    all_to_all x2, waiting for transfers between devices, exchange(): return lax.all_to_all(value, axes, 0, 0, tiled=True)  13.4 us
    all_to_all x2, starting transfers between devices, exchange(): return lax.all_to_all(value, axes, 0, 0, tiled=True)  11.4 us
    unnamed x42, local copies, waits for them, and re-layouts  7.63 us
    pallas_call x1, Pallas kernels, pack_measured(): pl.pallas_call(functools.partial(pack_measured_kernel, base), grid=(PACK_...  5.82 us
    pallas_call x1, Pallas kernels, adjoint(): pl.pallas_call(functools.partial(adjoint_kernel, len(edges)), grid_spec=p...  5.81 us
    pallas_call x1, Pallas kernels, start(): pl.pallas_call(start_kernel, grid=(2,), in_specs=[GRAM_SPEC] + [IN_VMEM]...  5.22 us
  transfers between devices with their start and end apart: 7, of which 2 were waited for; matrix products, arithmetic and copies ran while one was open for 5% of the time, Pallas kernels for 19%

profile of v5, /device:TPU:1, one launch (start us, length us, event | category | flops | bytes accessed | tf_op | source)
XLA Modules:
  0.0 139.1 jit_solution(2549484485029819417)
XLA Ops:
  0.6 0.0 copy-start.22
  0.6 0.0 copy-start.20
  0.7 2.8 %pack_image.1 = f32[16,64,256]{2,1,0:T(8,128)} custom-call(f32[16,2,16,256]{3,2,1,0:T(8,128)} %maps_ref.1, f32[2,8,16,256]{3,2,1,0:T(8,128)} %frames_ref.1, f32[2,8,16,256]{3,2,1,0:T(8,128)} %aux_ref.3, f32[2,8,16,256]{3,2,1,0:T(8,128)} %dual_ref.3), custom_call_target="tpu_custom_call" | custom-call | tf_op jit(solution)/shard_map/pack_image/pallas_call | solution.py:276
  3.5 6.8 %all-to-all-start.1 = ((f32[16,64,256]{2,1,0:T(8,128)}), f32[16,64,256]{2,1,0:T(8,128)}, u32[]{:S(2)}, u32[]{:S(2)}) async-start(f32[16,64,256]{2,1,0:T(8,128)} %pack_image.1), calls=%async_computation.1 | async-start | bytes 2097152 | tf_op jit(solution)/shard_map/all_to_all | solution.py:796
  10.3 0.1 dynamic-slice_convert_fusion
  10.4 0.6 reshape.144.weight_ref
  11.0 0.1 constant_dynamic-slice_fusion
  11.1 0.1 broadcast_in_dim.49
  11.2 0.1 broadcast_in_dim.50.turn_ref
  11.3 5.8 %pack_measured_0.1 = (f32[16,176,256]{2,1,0:T(8,128)S(1)}, f32[2,256,128]{2,1,0:T(8,128)}) custom-call(f32[1,128]{1,0:T(1,128)} %reshape.144.weight_ref, f32[2,128,128]{2,1,0:T(8,128)S(1)} %broadcast_in_dim.50.turn_ref, f32[16,2,128,256]{3,2,1,0:T(8,128)} %bitcast.4), custom_call_target="tpu_custom_call" | custom-call | tf_op jit(solution)/shard_map/pack_measured_0/pallas_call | solution.py:301
  17.1 1.6 %copy-done.6 = f32[16,176,256]{2,1,0:T(8,128)} copy-done((f32[16,176,256]{2,1,0:T(8,128)}, f32[16,176,256]{2,1,0:T(8,128)S(1)}, u32[]{:S(2)}) %copy-start.6) | copy-done | bytes 2883608
  18.6 0.1 reshape.145
  18.7 0.2 reduce_sum.36
  18.9 1.4 reduce_window_sum.22
  20.3 0.1 copy.30
  20.4 0.7 fusion.4
  21.2 0.1 copy.29
  21.9 4.2 %all-to-all-done.1.image_ref = f32[16,64,256]{2,1,0:T(8,128)} async-done(((f32[16,64,256]{2,1,0:T(8,128)}), f32[16,64,256]{2,1,0:T(8,128)}, u32[]{:S(2)}, u32[]{:S(2)}) %all-to-all-start.1) | async-done | bytes 1048608 | tf_op jit(solution)/shard_map/all_to_all | solution.py:796
  26.1 0.0 copy-start.21
  26.1 4.5 %all-to-all-start.2 = ((f32[16,176,256]{2,1,0:T(8,128)}), f32[16,176,256]{2,1,0:T(8,128)S(1)}, u32[]{:S(2)}, u32[]{:S(2)}) async-start(f32[16,176,256]{2,1,0:T(8,128)} %copy-done.6), calls=%async_computation.2 | async-start | bytes 5767168 | tf_op jit(solution)/shard_map/all_to_all | solution.py:796
  30.7 0.2 fusion.3
  30.9 0.1 add_add_fusion.1
  31.0 0.1 iota_add_fusion.1
  31.1 1.5 %select_reduce_fusion.1 = s32[8,16,16]{2,1,0:T(8,128)S(1)} fusion(s32[16,16]{1,0:T(8,128)S(1)} %add_add_fusion.1, s32[8,16,16]{2,1,0:T(8,128)S(1)} %get-tuple-element.203, s32[8,16,16]{2,1,0:T(8,128)S(1)} %get-tuple-element.204, pred[8,16,16]{2,1,0:T(8,128)(4,1)S(1)} %get-tuple-element.202, pred[8,16,16]{2,1,0:T(8,128)(4,1)S(1)} %get-tuple-element.201, ...), kind=kLoop, calls=%fused_computation.11 | loop fusion | flops 194560 | bytes 31744 | tf_op jit(solution)/shard_map/reduce_sum | solution.py:807
  32.6 2.1 %receive.2 = (f32[2,256,256]{2,1,0:T(8,128)S(1)}, f32[2,256,128]{2,1,0:T(8,128)S(1)}, f32[2,256,128]{2,1,0:T(8,128)S(1)}, f32[2,32,128]{2,1,0:T(8,128)}, f32[2,32,128]{2,1,0:T(8,128)S(1)}) custom-call(f32[16,64,256]{2,1,0:T(8,128)} %all-to-all-done.1.image_ref), custom_call_target="tpu_custom_call" | custom-call | tf_op jit(solution)/shard_map/receive/pallas_call | solution.py:368
  34.7 0.7 copy-done.9
  35.4 0.7 copy-done.14
  36.1 6.1 %collective-permute-start.1 = (f32[2,32,128]{2,1,0:T(8,128)}, f32[2,32,128]{2,1,0:T(8,128)S(1)}, u32[]{:S(2)}, u32[]{:S(2)}) collective-permute-start(f32[2,32,128]{2,1,0:T(8,128)} %get-tuple-element.92), channel_id=1, source_target_pairs={{0,112},{16,0},{32,16},{48,32},{64,48},{80,64},{96,80},{112,96},{1... | collective-permute-start | bytes 98312 | tf_op jit(solution)/shard_map/ppermute | solution.py:792
  42.2 0.0 collective-permute-start
  42.2 0.6 broadcast_add_fusion.2
  42.8 0.1 reshape.146.window_ref
  42.9 0.9 sub.49.index_ref
  43.9 0.0 copy-start.7
  43.9 1.0 copy-done.7
  44.9 2.2 %gram_tables.1.gram_ref = bf16[8,2,256,256]{3,2,1,0:T(8,128)(2,1)S(1)} custom-call(f32[8,1,256]{2,1,0:T(1,128)S(1)} %broadcast_in_dim.53.weight_ref, bf16[4,256,256]{2,1,0:T(8,128)(2,1)S(1)} %copy-done.7), custom_call_target="tpu_custom_call" | custom-call | tf_op jit(solution)/shard_map/gram_tables/pallas_call | solution.py:387
  47.2 1.3 copy-done
  48.5 1.9 %line_tables.2.tables_ref = bf16[8,2,256,256]{3,2,1,0:T(8,128)(2,1)S(1)} custom-call(s32[8,1,256]{2,1,0:T(1,128)S(1)} %sub.49.index_ref, bf16[4,256,256]{2,1,0:T(8,128)(2,1)S(1)} %copy-done.7), custom_call_target="tpu_custom_call" | custom-call | tf_op jit(solution)/shard_map/line_tables/pallas_call | solution.py:325
  50.4 1.3 copy-done.5
  51.8 5.2 %start.1.in_ref = f32[2,256,128]{2,1,0:T(8,128)S(1)} custom-call(bf16[8,2,256,256]{3,2,1,0:T(8,128)(2,1)} %copy-done, f32[2,256,256]{2,1,0:T(8,128)S(1)} %get-tuple-element.83.maps_ref, f32[2,256,128]{2,1,0:T(8,128)S(1)} %copy-done.10, f32[2,256,128]{2,1,0:T(8,128)S(1)} %copy-done.15, f32[2,256,128]{2,1,0:T(8,128)} %get-tuple-element.90.in_ref), custom_call_target="tpu_custom_call" | custom-call | tf_op jit(solution)/shard_map/start/pallas_call | solution.py:445
  57.0 0.0 copy-start.8
  57.0 0.7 copy-done.8
  57.7 0.0 collective-permute-done.1.refs_1_.frames_after_ref
  57.7 0.0 collective-permute-done.refs_0_
  57.7 9.2 %all-to-all-done.2.lines_ref = f32[16,176,256]{2,1,0:T(8,128)S(1)} async-done(((f32[16,176,256]{2,1,0:T(8,128)}), f32[16,176,256]{2,1,0:T(8,128)S(1)}, u32[]{:S(2)}, u32[]{:S(2)}) %all-to-all-start.2) | async-done | bytes 2883616 | tf_op jit(solution)/shard_map/all_to_all | solution.py:796
  67.0 5.8 %adjoint.2 = (f32[2,256,128]{2,1,0:T(8,128)S(1)}, f32[2,32,128]{2,1,0:T(8,128)S(1)}, f32[2,32,128]{2,1,0:T(8,128)S(1)}) custom-call(s32[128]{0:T(128)S(1)} %reshape.146.window_ref, bf16[8,2,256,256]{3,2,1,0:T(8,128)(2,1)} %copy-done.5, f32[2,256,256]{2,1,0:T(8,128)S(1)} %get-tuple-element.83.maps_ref, f32[16,176,256]{2,1,0:T(8,128)S(1)} %all-to-all-done.2.lines_ref, ...), custom_call_target="tpu_custom_call" | custom-call | tf_op jit(solution)/shard_map/adjoint/pallas_call | solution.py:510
  72.8 1.7 %collective-permute-start.2 = (f32[2,32,128]{2,1,0:T(8,128)S(1)}, f32[2,32,128]{2,1,0:T(8,128)S(1)}, u32[]{:S(2)}, u32[]{:S(2)}) collective-permute-start(f32[2,32,128]{2,1,0:T(8,128)S(1)} %get-tuple-element.94), channel_id=1, source_target_pairs={{0,16},{16,32},{32,48},{48,64},{64,80},{80,96},{96,112},{112,0},{1... | collective-permute-start | bytes 98312 | tf_op jit(solution)/shard_map/ppermute | solution.py:792
  74.5 4.5 %collective-permute-start.3 = (f32[2,32,128]{2,1,0:T(8,128)S(1)}, f32[2,32,128]{2,1,0:T(8,128)S(1)}, u32[]{:S(2)}, u32[]{:S(2)}) collective-permute-start(f32[2,32,128]{2,1,0:T(8,128)S(1)} %get-tuple-element.95), channel_id=1, source_target_pairs={{0,112},{16,0},{32,16},{48,32},{64,48},{80,64},{96,80},{112,96},{1... | collective-permute-start | bytes 98312 | tf_op jit(solution)/shard_map/ppermute | solution.py:792
  79.0 5.0 %gram_apply.1.gram_ref = f32[2,256,128]{2,1,0:T(8,128)S(1)} custom-call(bf16[8,2,256,256]{3,2,1,0:T(8,128)(2,1)} %copy-done, f32[2,256,256]{2,1,0:T(8,128)S(1)} %get-tuple-element.83.maps_ref, f32[2,256,128]{2,1,0:T(8,128)S(1)} %get-tuple-element.93.in_ref.first_ref.residual_ref), custom_call_target="tpu_custom_call" | custom-call | tf_op jit(solution)/shard_map/gram_apply/pallas_call | solution.py:539
  84.0 0.0 copy-start.11
  84.0 0.0 collective-permute-done.2.before_ref
  84.0 0.0 collective-permute-done.3.after_ref.residual_after_ref
  84.0 1.3 normal.1
  85.4 1.5 %collective-permute-start.4 = (f32[2,32,128]{2,1,0:T(8,128)S(1)}, f32[2,32,128]{2,1,0:T(8,128)S(1)}, u32[]{:S(2)}, u32[]{:S(2)}) collective-permute-start(f32[2,32,128]{2,1,0:T(8,128)S(1)} %get-tuple-element.99), channel_id=1, source_target_pairs={{0,112},{16,0},{32,16},{48,32},{64,48},{80,64},{96,80},{112,96},{1... | collective-permute-start | bytes 98312 | tf_op jit(solution)/shard_map/ppermute | solution.py:792
  86.8 4.3 %curvature.1.curve_ref = f32[8,128]{1,0:T(8,128)S(1)} custom-call(bf16[8,2,256,256]{3,2,1,0:T(8,128)(2,1)} %copy-done, f32[2,256,256]{2,1,0:T(8,128)S(1)} %get-tuple-element.83.maps_ref, f32[2,256,128]{2,1,0:T(8,128)S(1)} %get-tuple-element.97.in_ref.product_ref), custom_call_target="tpu_custom_call" | custom-call | tf_op jit(solution)/shard_map/curvature/pallas_call | solution.py:627
  91.2 0.0 copy-start.23
  91.2 0.0 collective-permute-done.4.after_ref.product_after_ref
  91.2 0.1 share.1
  91.3 19.9 %all_to_all.32.shared_ref = f32[128,1,128]{2,1,0:T(1,128)S(1)} all-to-all(f32[128,1,128]{2,1,0:T(1,128)S(1)} %share.1), channel_id=1, replica_groups=mesh['phase'=8,'row'=16] {'phase','row'}, dimensions={0} | all-to-all | bytes 131072 | tf_op jit(solution)/shard_map/all_to_all | solution.py:796
  111.2 0.4 solve.1
  111.6 11.8 %all_to_all.33.in_ref = f32[16,3,16,128]{3,2,1,0:T(8,128)S(1)} all-to-all(f32[16,3,16,128]{3,2,1,0:T(8,128)S(1)} %solve.1), channel_id=1, replica_groups=mesh['phase'=8,'row'=16] {'row'}, dimensions={0} | all-to-all | bytes 786432 | tf_op jit(solution)/shard_map/all_to_all | solution.py:796
  123.5 1.2 finish.1
  124.6 13.8 %all_to_all.34 = f32[128,1,128]{2,1,0:T(1,128)S(1)} all-to-all(f32[128,1,128]{2,1,0:T(1,128)S(1)} %get-tuple-element.103), channel_id=1, replica_groups=mesh['phase'=8,'row'=16] {'phase','row'}, dimensions={0} | all-to-all | bytes 131072 | tf_op jit(solution)/shard_map/all_to_all | solution.py:796
  138.5 0.2 slice_reduce_fusion
  138.6 0.5 sqrt_multiply_fusion
  (33 shorter events, 0.1 us)
Async XLA Ops:
  0.6 10.4 %copy-start.22 = (f32[2,256]{1,0:T(2,128)S(1)}, f32[2,256]{1,0:T(2,128)}, u32[]{:S(2)}) copy-start(f32[2,256]{1,0:T(2,128)} %constant.66.clone) | copy-start | bytes 6148
  0.6 9.7 %copy-start.20 = (s32[8,256]{1,0:T(8,128)S(1)}, s32[8,256]{1,0:T(8,128)}, u32[]{:S(2)}) copy-start(s32[8,256]{1,0:T(8,128)} %param.16) | copy-start | bytes 24580
  3.5 22.6 %all-to-all-start.1 = ((f32[16,64,256]{2,1,0:T(8,128)}), f32[16,64,256]{2,1,0:T(8,128)}, u32[]{:S(2)}, u32[]{:S(2)}) async-start(f32[16,64,256]{2,1,0:T(8,128)} %pack_image.1), calls=%async_computation.1 | async-start | bytes 2097152 | tf_op jit(solution)/shard_map/all_to_all | solution.py:796
  17.1 1.6 %copy-start.6 = (f32[16,176,256]{2,1,0:T(8,128)}, f32[16,176,256]{2,1,0:T(8,128)S(1)}, u32[]{:S(2)}) copy-start(f32[16,176,256]{2,1,0:T(8,128)S(1)} %get-tuple-element.87) | copy-start | bytes 8650756
  18.7 7.4 %copy-start.16 = (s32[8,16,16]{2,1,0:T(8,128)}, s32[8,16,16]{2,1,0:T(8,128)S(1)}, u32[]{:S(2)}) copy-start(s32[8,16,16]{2,1,0:T(8,128)S(1)} %reshape.145) | copy-start | bytes 24580
  21.2 4.9 %copy-start.18 = (s32[8,16,16]{2,1,0:T(8,128)}, s32[8,16,16]{2,1,0:T(8,128)S(1)}, u32[]{:S(2)}) copy-start(s32[8,16,16]{2,1,0:T(8,128)S(1)} %get-tuple-element.197) | copy-start | bytes 24580
  26.1 4.6 %copy-start.17 = (s32[8,16,16]{2,1,0:T(8,128)S(1)}, s32[8,16,16]{2,1,0:T(8,128)}, u32[]{:S(2)}) copy-start(s32[8,16,16]{2,1,0:T(8,128)} %copy-done.16) | copy-start | bytes 24580
  26.1 4.6 %copy-start.19 = (s32[8,16,16]{2,1,0:T(8,128)S(1)}, s32[8,16,16]{2,1,0:T(8,128)}, u32[]{:S(2)}) copy-start(s32[8,16,16]{2,1,0:T(8,128)} %copy-done.18) | copy-start | bytes 24580
  26.1 16.7 %copy-start.21 = (s32[8,256]{1,0:T(8,128)S(1)}, s32[8,256]{1,0:T(8,128)}, u32[]{:S(2)}) copy-start(s32[8,256]{1,0:T(8,128)} %param.16) | copy-start | bytes 24580
  26.1 40.8 %all-to-all-start.2 = ((f32[16,176,256]{2,1,0:T(8,128)}), f32[16,176,256]{2,1,0:T(8,128)S(1)}, u32[]{:S(2)}, u32[]{:S(2)}) async-start(f32[16,176,256]{2,1,0:T(8,128)} %copy-done.6), calls=%async_computation.2 | async-start | bytes 5767168 | tf_op jit(solution)/shard_map/all_to_all | solution.py:796
  34.7 0.7 copy-start.9
  35.4 0.7 copy-start.14
  36.1 21.6 %collective-permute-start.1 = (f32[2,32,128]{2,1,0:T(8,128)}, f32[2,32,128]{2,1,0:T(8,128)S(1)}, u32[]{:S(2)}, u32[]{:S(2)}) collective-permute-start(f32[2,32,128]{2,1,0:T(8,128)} %get-tuple-element.92), channel_id=1, source_target_pairs={{0,112},{16,0},{32,16},{48,32},{64,48},{80,64},{96,80},{112,96},{1... | collective-permute-start | bytes 98312 | tf_op jit(solution)/shard_map/ppermute | solution.py:792
  42.2 15.5 %collective-permute-start = (f32[2,32,128]{2,1,0:T(8,128)S(1)}, f32[2,32,128]{2,1,0:T(8,128)S(1)}, u32[]{:S(2)}, u32[]{:S(2)}) collective-permute-start(f32[2,32,128]{2,1,0:T(8,128)S(1)} %get-tuple-element.91), channel_id=1, source_target_pairs={{0,16},{16,32},{32,48},{48,64},{64,80},{80,96},{96,112},{112,0},{1... | collective-permute-start | bytes 98312 | tf_op jit(solution)/shard_map/ppermute | solution.py:792
  43.9 1.0 copy-start.7
  44.9 6.9 %copy-start.10 = (f32[2,256,128]{2,1,0:T(8,128)S(1)}, f32[2,256,128]{2,1,0:T(8,128)}, u32[]{:S(2)}) copy-start(f32[2,256,128]{2,1,0:T(8,128)} %copy-done.9) | copy-start | bytes 786436
  44.9 6.9 %copy-start.15 = (f32[2,256,128]{2,1,0:T(8,128)S(1)}, f32[2,256,128]{2,1,0:T(8,128)}, u32[]{:S(2)}) copy-start(f32[2,256,128]{2,1,0:T(8,128)} %copy-done.14) | copy-start | bytes 786436
  47.2 1.3 copy-start
  50.4 1.4 copy-start.5
  57.0 0.7 copy-start.8
  72.8 11.2 %collective-permute-start.2 = (f32[2,32,128]{2,1,0:T(8,128)S(1)}, f32[2,32,128]{2,1,0:T(8,128)S(1)}, u32[]{:S(2)}, u32[]{:S(2)}) collective-permute-start(f32[2,32,128]{2,1,0:T(8,128)S(1)} %get-tuple-element.94), channel_id=1, source_target_pairs={{0,16},{16,32},{32,48},{48,64},{64,80},{80,96},{96,112},{112,0},{1... | collective-permute-start | bytes 98312 | tf_op jit(solution)/shard_map/ppermute | solution.py:792
  74.5 9.5 %collective-permute-start.3 = (f32[2,32,128]{2,1,0:T(8,128)S(1)}, f32[2,32,128]{2,1,0:T(8,128)S(1)}, u32[]{:S(2)}, u32[]{:S(2)}) collective-permute-start(f32[2,32,128]{2,1,0:T(8,128)S(1)} %get-tuple-element.95), channel_id=1, source_target_pairs={{0,112},{16,0},{32,16},{48,32},{64,48},{80,64},{96,80},{112,96},{1... | collective-permute-start | bytes 98312 | tf_op jit(solution)/shard_map/ppermute | solution.py:792
  84.0 27.2 %copy-start.11 = (f32[2,256,128]{2,1,0:T(8,128)S(1)}, f32[2,256,128]{2,1,0:T(8,128)}, u32[]{:S(2)}) copy-start(f32[2,256,128]{2,1,0:T(8,128)} %copy-done.9) | copy-start | bytes 786436
  85.4 5.8 %collective-permute-start.4 = (f32[2,32,128]{2,1,0:T(8,128)S(1)}, f32[2,32,128]{2,1,0:T(8,128)S(1)}, u32[]{:S(2)}, u32[]{:S(2)}) collective-permute-start(f32[2,32,128]{2,1,0:T(8,128)S(1)} %get-tuple-element.99), channel_id=1, source_target_pairs={{0,112},{16,0},{32,16},{48,32},{64,48},{80,64},{96,80},{112,96},{1... | collective-permute-start | bytes 98312 | tf_op jit(solution)/shard_map/ppermute | solution.py:792
  86.8 36.7 %copy-start.12 = (f32[2,8,16,256]{3,2,1,0:T(8,128)S(1)}, f32[2,8,16,256]{3,2,1,0:T(8,128)}, u32[]{:S(2)}) copy-start(f32[2,8,16,256]{3,2,1,0:T(8,128)} %aux_ref.3) | copy-start | bytes 786436
  86.8 36.7 %copy-start.13 = (f32[2,8,16,256]{3,2,1,0:T(8,128)S(1)}, f32[2,8,16,256]{3,2,1,0:T(8,128)}, u32[]{:S(2)}) copy-start(f32[2,8,16,256]{3,2,1,0:T(8,128)} %dual_ref.3) | copy-start | bytes 786436
  91.2 47.4 %copy-start.23 = (f32[2]{0:T(128)S(1)}, f32[2]{0:T(128)}, u32[]{:S(2)}) copy-start(f32[2]{0:T(128)} %constant.67.clone) | copy-start | bytes 28

commit v6 on v5

--- a/solution.py
+++ b/solution.py
@@ -167,7 +167,7 @@
 
 def expand(vector_ref, maps_ref, pieces):
     half = pl.program_id(0)
-    for near, far in row_pairs(16):
+    for near, far in row_pairs(32):
         values = [
             [spread_half(vector_ref[part, at], half) for part in range(2)] for at in (near, far)
         ]
@@ -688,29 +688,30 @@
     for j in range(ROW_SHARDS):
         turned = j >= ROW_SHARDS // 2
         block = ROW_SHARDS + ROW_SHARDS // 2 - 1 - j if turned else j
+        edges = jnp.zeros((8, LANES), F32)
         for row in range(0, ROWS, 8):
             at = slice(block * ROWS + row, block * ROWS + row + 8)
             piece, start = divmod(at.start, FOLD)
             folded = slice(start, start + 8)
-            values = [
-                frames_ref[part, at]
-                + by_first * residual_ref[part, at]
-                + by_image * product_ref[part, at]
-                for part in range(2)
-            ]
-            edge = [
-                roll(
+            to = ROWS - 8 - row if turned else row
+            for part in range(2):
+                value = (
+                    frames_ref[part, at]
+                    + by_first * residual_ref[part, at]
+                    + by_image * product_ref[part, at]
+                )
+                place = 2 * part + to // 8
+                edge = roll(
                     frames_after_ref[part, folded]
                     + by_first * residual_after_ref[part, folded]
                     + by_image * product_after_ref[part, folded],
-                    part - piece,
+                    place - piece,
                 )
-                for part in range(2)
-            ]
-            values.append(jnp.where(group == 0, edge[0], edge[1]))
-            to = slice(ROWS - 8 - row, ROWS - row) if turned else slice(row, row + 8)
-            for which, value in enumerate(values):
-                out_ref[j, which, to] = reverse_eight(value) if turned else value
+                if turned:
+                    value, edge = reverse_eight(value), reverse_eight(edge)
+                out_ref[j, part * ROWS + to : part * ROWS + to + 8] = value
+                edges = jnp.where(group == place, edge, edges)
+        out_ref[j, 2 * ROWS : 2 * ROWS + 8] = edges
 
 
 def solve(shared, frames, residual, product, frames_after, residual_after, product_after):
@@ -718,8 +719,8 @@
         solve_kernel,
         grid=(1,),
         in_specs=[IN_VMEM] * 7,
-        out_specs=pl.BlockSpec((ROW_SHARDS, 3, ROWS, LANES), lambda i: (0, 0, 0, 0)),
-        out_shape=jax.ShapeDtypeStruct((ROW_SHARDS, 3, ROWS, LANES), F32),
+        out_specs=pl.BlockSpec((ROW_SHARDS, 2 * ROWS + 8, LANES), lambda i: (0, 0, 0)),
+        out_shape=jax.ShapeDtypeStruct((ROW_SHARDS, 2 * ROWS + 8, LANES), F32),
         compiler_params=params(),
         name="solve",
     )(shared, frames, residual, product, frames_after, residual_after, product_after)
@@ -734,11 +735,13 @@
             cols = slice(half * LANES, (half + 1) * LANES)
             parts = []
             for part in range(2):
-                blocks = [in_ref[half * 8 + jj, part, at] for jj in range(8)]
+                rows = slice(part * ROWS + row, part * ROWS + row + 8)
+                blocks = [in_ref[half * 8 + jj, rows] for jj in range(8)]
                 values = transpose_groups(blocks)
                 after = None
                 for jj in range(8):
-                    piece = roll(in_ref[half * 8 + jj, 2, at], jj - part)
+                    place = 2 * part + row // 8
+                    piece = roll(in_ref[half * 8 + jj, 2 * ROWS : 2 * ROWS + 8], jj - place)
                     after = piece if after is None else jnp.where(group == jj, piece, after)
                 for t in range(PHASES):
                     x_ref[part, t, at, cols] = values[t]

time: 140 us -> 139 us (level)
  no operation moved by 1% of the time
where the time goes in v6:
time: 139 us; the launch traced here: 138 us
  blocking collectives  44.9 us (32%)
  Pallas kernels  38.2 us (27%)
  starting transfers between devices  25.2 us (18%)
  waiting for transfers between devices  13.4 us (10%)
  local copies, waits for them, and re-layouts  9.59 us (7%)
  other arithmetic  5.61 us (4%)
  between operations  1.58 us (1%)
    all_to_all x3, blocking collectives, exchange(): return lax.all_to_all(value, axes, 0, 0, tiled=True)  44.9 us
    ppermute x5, starting transfers between devices, shift(): return lax.ppermute(value, 'phase', pairs)  13.8 us
    all_to_all x2, waiting for transfers between devices, exchange(): return lax.all_to_all(value, axes, 0, 0, tiled=True)  13.4 us
    all_to_all x2, starting transfers between devices, exchange(): return lax.all_to_all(value, axes, 0, 0, tiled=True)  11.4 us
    unnamed x42, local copies, waits for them, and re-layouts  7.63 us
    pallas_call x1, Pallas kernels, pack_measured(): pl.pallas_call(functools.partial(pack_measured_kernel, base), grid=(PACK_...  5.82 us
    pallas_call x1, Pallas kernels, adjoint(): pl.pallas_call(functools.partial(adjoint_kernel, len(edges)), grid_spec=p...  5.81 us
    pallas_call x1, Pallas kernels, start(): pl.pallas_call(start_kernel, grid=(2,), in_specs=[GRAM_SPEC] + [IN_VMEM]...  5.22 us
  transfers between devices with their start and end apart: 7, of which 2 were waited for; matrix products, arithmetic and copies ran while one was open for 5% of the time, Pallas kernels for 19%

profile of v6, /device:TPU:1, one launch (start us, length us, event | category | flops | bytes accessed | tf_op | source)
XLA Modules:
  0.0 138.4 jit_solution(4824574137339942428)
XLA Ops:
  0.6 0.0 copy-start.22
  0.6 0.0 copy-start.20
  0.7 2.8 %pack_image.1 = f32[16,64,256]{2,1,0:T(8,128)} custom-call(f32[16,2,16,256]{3,2,1,0:T(8,128)} %maps_ref.1, f32[2,8,16,256]{3,2,1,0:T(8,128)} %frames_ref.1, f32[2,8,16,256]{3,2,1,0:T(8,128)} %aux_ref.3, f32[2,8,16,256]{3,2,1,0:T(8,128)} %dual_ref.3), custom_call_target="tpu_custom_call" | custom-call | tf_op jit(solution)/shard_map/pack_image/pallas_call | solution.py:276
  3.5 6.8 %all-to-all-start.1 = ((f32[16,64,256]{2,1,0:T(8,128)}), f32[16,64,256]{2,1,0:T(8,128)}, u32[]{:S(2)}, u32[]{:S(2)}) async-start(f32[16,64,256]{2,1,0:T(8,128)} %pack_image.1), calls=%async_computation.1 | async-start | bytes 2097152 | tf_op jit(solution)/shard_map/all_to_all | solution.py:799
  10.3 0.1 dynamic-slice_convert_fusion
  10.4 0.6 reshape.144.weight_ref
  11.0 0.1 constant_dynamic-slice_fusion
  11.1 0.1 broadcast_in_dim.49
  11.2 0.1 broadcast_in_dim.50.turn_ref
  11.3 5.8 %pack_measured_0.1 = (f32[16,176,256]{2,1,0:T(8,128)S(1)}, f32[2,256,128]{2,1,0:T(8,128)}) custom-call(f32[1,128]{1,0:T(1,128)} %reshape.144.weight_ref, f32[2,128,128]{2,1,0:T(8,128)S(1)} %broadcast_in_dim.50.turn_ref, f32[16,2,128,256]{3,2,1,0:T(8,128)} %bitcast.4), custom_call_target="tpu_custom_call" | custom-call | tf_op jit(solution)/shard_map/pack_measured_0/pallas_call | solution.py:301
  17.1 1.6 %copy-done.6 = f32[16,176,256]{2,1,0:T(8,128)} copy-done((f32[16,176,256]{2,1,0:T(8,128)}, f32[16,176,256]{2,1,0:T(8,128)S(1)}, u32[]{:S(2)}) %copy-start.6) | copy-done | bytes 2883608
  18.6 0.1 reshape.145
  18.7 0.2 reduce_sum.36
  18.9 1.4 reduce_window_sum.22
  20.3 0.1 copy.30
  20.4 0.7 fusion.4
  21.2 0.1 copy.29
  21.9 4.2 %all-to-all-done.1.image_ref = f32[16,64,256]{2,1,0:T(8,128)} async-done(((f32[16,64,256]{2,1,0:T(8,128)}), f32[16,64,256]{2,1,0:T(8,128)}, u32[]{:S(2)}, u32[]{:S(2)}) %all-to-all-start.1) | async-done | bytes 1048608 | tf_op jit(solution)/shard_map/all_to_all | solution.py:799
  26.1 0.0 copy-start.21
  26.1 4.5 %all-to-all-start.2 = ((f32[16,176,256]{2,1,0:T(8,128)}), f32[16,176,256]{2,1,0:T(8,128)S(1)}, u32[]{:S(2)}, u32[]{:S(2)}) async-start(f32[16,176,256]{2,1,0:T(8,128)} %copy-done.6), calls=%async_computation.2 | async-start | bytes 5767168 | tf_op jit(solution)/shard_map/all_to_all | solution.py:799
  30.7 0.2 fusion.3
  30.9 0.1 add_add_fusion.1
  31.0 0.1 iota_add_fusion.1
  31.1 1.5 %select_reduce_fusion.1 = s32[8,16,16]{2,1,0:T(8,128)S(1)} fusion(s32[16,16]{1,0:T(8,128)S(1)} %add_add_fusion.1, s32[8,16,16]{2,1,0:T(8,128)S(1)} %get-tuple-element.203, s32[8,16,16]{2,1,0:T(8,128)S(1)} %get-tuple-element.204, pred[8,16,16]{2,1,0:T(8,128)(4,1)S(1)} %get-tuple-element.202, pred[8,16,16]{2,1,0:T(8,128)(4,1)S(1)} %get-tuple-element.201, ...), kind=kLoop, calls=%fused_computation.11 | loop fusion | flops 194560 | bytes 31744 | tf_op jit(solution)/shard_map/reduce_sum | solution.py:810
  32.6 2.1 %receive.2 = (f32[2,256,256]{2,1,0:T(8,128)S(1)}, f32[2,256,128]{2,1,0:T(8,128)S(1)}, f32[2,256,128]{2,1,0:T(8,128)S(1)}, f32[2,32,128]{2,1,0:T(8,128)}, f32[2,32,128]{2,1,0:T(8,128)S(1)}) custom-call(f32[16,64,256]{2,1,0:T(8,128)} %all-to-all-done.1.image_ref), custom_call_target="tpu_custom_call" | custom-call | tf_op jit(solution)/shard_map/receive/pallas_call | solution.py:368
  34.7 0.7 copy-done.8
  35.4 0.7 copy-done.14
  36.1 6.1 %collective-permute-start.1 = (f32[2,32,128]{2,1,0:T(8,128)}, f32[2,32,128]{2,1,0:T(8,128)S(1)}, u32[]{:S(2)}, u32[]{:S(2)}) collective-permute-start(f32[2,32,128]{2,1,0:T(8,128)} %get-tuple-element.92), channel_id=1, source_target_pairs={{0,112},{16,0},{32,16},{48,32},{64,48},{80,64},{96,80},{112,96},{1... | collective-permute-start | bytes 98312 | tf_op jit(solution)/shard_map/ppermute | solution.py:795
  42.2 0.0 collective-permute-start
  42.2 0.6 broadcast_add_fusion.2
  42.8 0.1 reshape.146.window_ref
  42.9 0.9 sub.49.index_ref
  43.9 0.0 copy-start.7
  43.9 1.0 copy-done.7
  44.9 2.2 %gram_tables.1.gram_ref = bf16[8,2,256,256]{3,2,1,0:T(8,128)(2,1)S(1)} custom-call(f32[8,1,256]{2,1,0:T(1,128)S(1)} %broadcast_in_dim.53.weight_ref, bf16[4,256,256]{2,1,0:T(8,128)(2,1)S(1)} %copy-done.7), custom_call_target="tpu_custom_call" | custom-call | tf_op jit(solution)/shard_map/gram_tables/pallas_call | solution.py:387
  47.2 1.3 copy-done
  48.5 1.9 %line_tables.2.tables_ref = bf16[8,2,256,256]{3,2,1,0:T(8,128)(2,1)S(1)} custom-call(s32[8,1,256]{2,1,0:T(1,128)S(1)} %sub.49.index_ref, bf16[4,256,256]{2,1,0:T(8,128)(2,1)S(1)} %copy-done.7), custom_call_target="tpu_custom_call" | custom-call | tf_op jit(solution)/shard_map/line_tables/pallas_call | solution.py:325
  50.4 1.3 copy-done.5
  51.8 5.2 %start.1.in_ref = f32[2,256,128]{2,1,0:T(8,128)S(1)} custom-call(bf16[8,2,256,256]{3,2,1,0:T(8,128)(2,1)} %copy-done, f32[2,256,256]{2,1,0:T(8,128)S(1)} %get-tuple-element.83.maps_ref, f32[2,256,128]{2,1,0:T(8,128)S(1)} %copy-done.9, f32[2,256,128]{2,1,0:T(8,128)S(1)} %copy-done.15, f32[2,256,128]{2,1,0:T(8,128)} %get-tuple-element.90.in_ref), custom_call_target="tpu_custom_call" | custom-call | tf_op jit(solution)/shard_map/start/pallas_call | solution.py:445
  57.0 0.0 copy-start.11
  57.0 0.7 copy-done.11
  57.7 0.0 collective-permute-done.1.refs_1_.frames_after_ref
  57.7 0.0 collective-permute-done.refs_0_
  57.7 9.2 %all-to-all-done.2.lines_ref = f32[16,176,256]{2,1,0:T(8,128)S(1)} async-done(((f32[16,176,256]{2,1,0:T(8,128)}), f32[16,176,256]{2,1,0:T(8,128)S(1)}, u32[]{:S(2)}, u32[]{:S(2)}) %all-to-all-start.2) | async-done | bytes 2883616 | tf_op jit(solution)/shard_map/all_to_all | solution.py:799
  67.0 5.8 %adjoint.2 = (f32[2,256,128]{2,1,0:T(8,128)S(1)}, f32[2,32,128]{2,1,0:T(8,128)S(1)}, f32[2,32,128]{2,1,0:T(8,128)S(1)}) custom-call(s32[128]{0:T(128)S(1)} %reshape.146.window_ref, bf16[8,2,256,256]{3,2,1,0:T(8,128)(2,1)} %copy-done.5, f32[2,256,256]{2,1,0:T(8,128)S(1)} %get-tuple-element.83.maps_ref, f32[16,176,256]{2,1,0:T(8,128)S(1)} %all-to-all-done.2.lines_ref, ...), custom_call_target="tpu_custom_call" | custom-call | tf_op jit(solution)/shard_map/adjoint/pallas_call | solution.py:510
  72.8 1.7 %collective-permute-start.2 = (f32[2,32,128]{2,1,0:T(8,128)S(1)}, f32[2,32,128]{2,1,0:T(8,128)S(1)}, u32[]{:S(2)}, u32[]{:S(2)}) collective-permute-start(f32[2,32,128]{2,1,0:T(8,128)S(1)} %get-tuple-element.94), channel_id=1, source_target_pairs={{0,16},{16,32},{32,48},{48,64},{64,80},{80,96},{96,112},{112,0},{1... | collective-permute-start | bytes 98312 | tf_op jit(solution)/shard_map/ppermute | solution.py:795
  74.5 4.5 %collective-permute-start.3 = (f32[2,32,128]{2,1,0:T(8,128)S(1)}, f32[2,32,128]{2,1,0:T(8,128)S(1)}, u32[]{:S(2)}, u32[]{:S(2)}) collective-permute-start(f32[2,32,128]{2,1,0:T(8,128)S(1)} %get-tuple-element.95), channel_id=1, source_target_pairs={{0,112},{16,0},{32,16},{48,32},{64,48},{80,64},{96,80},{112,96},{1... | collective-permute-start | bytes 98312 | tf_op jit(solution)/shard_map/ppermute | solution.py:795
  79.0 5.0 %gram_apply.1.gram_ref = f32[2,256,128]{2,1,0:T(8,128)S(1)} custom-call(bf16[8,2,256,256]{3,2,1,0:T(8,128)(2,1)} %copy-done, f32[2,256,256]{2,1,0:T(8,128)S(1)} %get-tuple-element.83.maps_ref, f32[2,256,128]{2,1,0:T(8,128)S(1)} %get-tuple-element.93.in_ref.first_ref.residual_ref), custom_call_target="tpu_custom_call" | custom-call | tf_op jit(solution)/shard_map/gram_apply/pallas_call | solution.py:539
  84.0 0.0 copy-start.10
  84.0 0.0 collective-permute-done.2.before_ref
  84.0 0.0 collective-permute-done.3.after_ref.residual_after_ref
  84.0 1.3 normal.1
  85.4 1.5 %collective-permute-start.4 = (f32[2,32,128]{2,1,0:T(8,128)S(1)}, f32[2,32,128]{2,1,0:T(8,128)S(1)}, u32[]{:S(2)}, u32[]{:S(2)}) collective-permute-start(f32[2,32,128]{2,1,0:T(8,128)S(1)} %get-tuple-element.99), channel_id=1, source_target_pairs={{0,112},{16,0},{32,16},{48,32},{64,48},{80,64},{96,80},{112,96},{1... | collective-permute-start | bytes 98312 | tf_op jit(solution)/shard_map/ppermute | solution.py:795
  86.8 4.3 %curvature.1.curve_ref = f32[8,128]{1,0:T(8,128)S(1)} custom-call(bf16[8,2,256,256]{3,2,1,0:T(8,128)(2,1)} %copy-done, f32[2,256,256]{2,1,0:T(8,128)S(1)} %get-tuple-element.83.maps_ref, f32[2,256,128]{2,1,0:T(8,128)S(1)} %get-tuple-element.97.in_ref.product_ref), custom_call_target="tpu_custom_call" | custom-call | tf_op jit(solution)/shard_map/curvature/pallas_call | solution.py:627
  91.2 0.0 copy-start.23
  91.2 0.0 collective-permute-done.4.after_ref.product_after_ref
  91.2 0.1 share.1
  91.3 19.9 %all_to_all.32.shared_ref = f32[128,1,128]{2,1,0:T(1,128)S(1)} all-to-all(f32[128,1,128]{2,1,0:T(1,128)S(1)} %share.1), channel_id=1, replica_groups=mesh['phase'=8,'row'=16] {'phase','row'}, dimensions={0} | all-to-all | bytes 131072 | tf_op jit(solution)/shard_map/all_to_all | solution.py:799
  111.2 0.4 solve.1
  111.6 11.3 %all_to_all.33.in_ref = f32[16,40,128]{2,1,0:T(8,128)S(1)} all-to-all(f32[16,40,128]{2,1,0:T(8,128)S(1)} %solve.1), channel_id=1, replica_groups=mesh['phase'=8,'row'=16] {'row'}, dimensions={0} | all-to-all | bytes 655360 | tf_op jit(solution)/shard_map/all_to_all | solution.py:799
  122.9 1.2 finish.1
  124.1 13.7 %all_to_all.34 = f32[128,1,128]{2,1,0:T(1,128)S(1)} all-to-all(f32[128,1,128]{2,1,0:T(1,128)S(1)} %get-tuple-element.103), channel_id=1, replica_groups=mesh['phase'=8,'row'=16] {'phase','row'}, dimensions={0} | all-to-all | bytes 131072 | tf_op jit(solution)/shard_map/all_to_all | solution.py:799
  137.8 0.2 slice_reduce_fusion
  137.9 0.5 sqrt_multiply_fusion
  (33 shorter events, 0.1 us)
Async XLA Ops:
  0.6 10.4 %copy-start.22 = (f32[2,256]{1,0:T(2,128)S(1)}, f32[2,256]{1,0:T(2,128)}, u32[]{:S(2)}) copy-start(f32[2,256]{1,0:T(2,128)} %constant.66.clone) | copy-start | bytes 6148
  0.6 9.7 %copy-start.20 = (s32[8,256]{1,0:T(8,128)S(1)}, s32[8,256]{1,0:T(8,128)}, u32[]{:S(2)}) copy-start(s32[8,256]{1,0:T(8,128)} %param.16) | copy-start | bytes 24580
  3.5 22.6 %all-to-all-start.1 = ((f32[16,64,256]{2,1,0:T(8,128)}), f32[16,64,256]{2,1,0:T(8,128)}, u32[]{:S(2)}, u32[]{:S(2)}) async-start(f32[16,64,256]{2,1,0:T(8,128)} %pack_image.1), calls=%async_computation.1 | async-start | bytes 2097152 | tf_op jit(solution)/shard_map/all_to_all | solution.py:799
  17.1 1.6 %copy-start.6 = (f32[16,176,256]{2,1,0:T(8,128)}, f32[16,176,256]{2,1,0:T(8,128)S(1)}, u32[]{:S(2)}) copy-start(f32[16,176,256]{2,1,0:T(8,128)S(1)} %get-tuple-element.87) | copy-start | bytes 8650756
  18.7 7.4 %copy-start.16 = (s32[8,16,16]{2,1,0:T(8,128)}, s32[8,16,16]{2,1,0:T(8,128)S(1)}, u32[]{:S(2)}) copy-start(s32[8,16,16]{2,1,0:T(8,128)S(1)} %reshape.145) | copy-start | bytes 24580
  21.2 4.9 %copy-start.18 = (s32[8,16,16]{2,1,0:T(8,128)}, s32[8,16,16]{2,1,0:T(8,128)S(1)}, u32[]{:S(2)}) copy-start(s32[8,16,16]{2,1,0:T(8,128)S(1)} %get-tuple-element.197) | copy-start | bytes 24580
  26.1 4.6 %copy-start.17 = (s32[8,16,16]{2,1,0:T(8,128)S(1)}, s32[8,16,16]{2,1,0:T(8,128)}, u32[]{:S(2)}) copy-start(s32[8,16,16]{2,1,0:T(8,128)} %copy-done.16) | copy-start | bytes 24580
  26.1 4.6 %copy-start.19 = (s32[8,16,16]{2,1,0:T(8,128)S(1)}, s32[8,16,16]{2,1,0:T(8,128)}, u32[]{:S(2)}) copy-start(s32[8,16,16]{2,1,0:T(8,128)} %copy-done.18) | copy-start | bytes 24580
  26.1 16.7 %copy-start.21 = (s32[8,256]{1,0:T(8,128)S(1)}, s32[8,256]{1,0:T(8,128)}, u32[]{:S(2)}) copy-start(s32[8,256]{1,0:T(8,128)} %param.16) | copy-start | bytes 24580
  26.1 40.8 %all-to-all-start.2 = ((f32[16,176,256]{2,1,0:T(8,128)}), f32[16,176,256]{2,1,0:T(8,128)S(1)}, u32[]{:S(2)}, u32[]{:S(2)}) async-start(f32[16,176,256]{2,1,0:T(8,128)} %copy-done.6), calls=%async_computation.2 | async-start | bytes 5767168 | tf_op jit(solution)/shard_map/all_to_all | solution.py:799
  34.7 0.7 copy-start.8
  35.4 0.7 copy-start.14
  36.1 21.6 %collective-permute-start.1 = (f32[2,32,128]{2,1,0:T(8,128)}, f32[2,32,128]{2,1,0:T(8,128)S(1)}, u32[]{:S(2)}, u32[]{:S(2)}) collective-permute-start(f32[2,32,128]{2,1,0:T(8,128)} %get-tuple-element.92), channel_id=1, source_target_pairs={{0,112},{16,0},{32,16},{48,32},{64,48},{80,64},{96,80},{112,96},{1... | collective-permute-start | bytes 98312 | tf_op jit(solution)/shard_map/ppermute | solution.py:795
  42.2 15.5 %collective-permute-start = (f32[2,32,128]{2,1,0:T(8,128)S(1)}, f32[2,32,128]{2,1,0:T(8,128)S(1)}, u32[]{:S(2)}, u32[]{:S(2)}) collective-permute-start(f32[2,32,128]{2,1,0:T(8,128)S(1)} %get-tuple-element.91), channel_id=1, source_target_pairs={{0,16},{16,32},{32,48},{48,64},{64,80},{80,96},{96,112},{112,0},{1... | collective-permute-start | bytes 98312 | tf_op jit(solution)/shard_map/ppermute | solution.py:795
  43.9 1.0 copy-start.7
  44.9 6.9 %copy-start.9 = (f32[2,256,128]{2,1,0:T(8,128)S(1)}, f32[2,256,128]{2,1,0:T(8,128)}, u32[]{:S(2)}) copy-start(f32[2,256,128]{2,1,0:T(8,128)} %copy-done.8) | copy-start | bytes 786436
  44.9 6.9 %copy-start.15 = (f32[2,256,128]{2,1,0:T(8,128)S(1)}, f32[2,256,128]{2,1,0:T(8,128)}, u32[]{:S(2)}) copy-start(f32[2,256,128]{2,1,0:T(8,128)} %copy-done.14) | copy-start | bytes 786436
  47.2 1.3 copy-start
  50.4 1.4 copy-start.5
  57.0 0.7 copy-start.11
  72.8 11.2 %collective-permute-start.2 = (f32[2,32,128]{2,1,0:T(8,128)S(1)}, f32[2,32,128]{2,1,0:T(8,128)S(1)}, u32[]{:S(2)}, u32[]{:S(2)}) collective-permute-start(f32[2,32,128]{2,1,0:T(8,128)S(1)} %get-tuple-element.94), channel_id=1, source_target_pairs={{0,16},{16,32},{32,48},{48,64},{64,80},{80,96},{96,112},{112,0},{1... | collective-permute-start | bytes 98312 | tf_op jit(solution)/shard_map/ppermute | solution.py:795
  74.5 9.5 %collective-permute-start.3 = (f32[2,32,128]{2,1,0:T(8,128)S(1)}, f32[2,32,128]{2,1,0:T(8,128)S(1)}, u32[]{:S(2)}, u32[]{:S(2)}) collective-permute-start(f32[2,32,128]{2,1,0:T(8,128)S(1)} %get-tuple-element.95), channel_id=1, source_target_pairs={{0,112},{16,0},{32,16},{48,32},{64,48},{80,64},{96,80},{112,96},{1... | collective-permute-start | bytes 98312 | tf_op jit(solution)/shard_map/ppermute | solution.py:795
  84.0 27.2 %copy-start.10 = (f32[2,256,128]{2,1,0:T(8,128)S(1)}, f32[2,256,128]{2,1,0:T(8,128)}, u32[]{:S(2)}) copy-start(f32[2,256,128]{2,1,0:T(8,128)} %copy-done.8) | copy-start | bytes 786436
  85.4 5.8 %collective-permute-start.4 = (f32[2,32,128]{2,1,0:T(8,128)S(1)}, f32[2,32,128]{2,1,0:T(8,128)S(1)}, u32[]{:S(2)}, u32[]{:S(2)}) collective-permute-start(f32[2,32,128]{2,1,0:T(8,128)S(1)} %get-tuple-element.99), channel_id=1, source_target_pairs={{0,112},{16,0},{32,16},{48,32},{64,48},{80,64},{96,80},{112,96},{1... | collective-permute-start | bytes 98312 | tf_op jit(solution)/shard_map/ppermute | solution.py:795
  86.8 36.1 %copy-start.12 = (f32[2,8,16,256]{3,2,1,0:T(8,128)S(1)}, f32[2,8,16,256]{3,2,1,0:T(8,128)}, u32[]{:S(2)}) copy-start(f32[2,8,16,256]{3,2,1,0:T(8,128)} %aux_ref.3) | copy-start | bytes 786436
  86.8 36.1 %copy-start.13 = (f32[2,8,16,256]{3,2,1,0:T(8,128)S(1)}, f32[2,8,16,256]{3,2,1,0:T(8,128)}, u32[]{:S(2)}) copy-start(f32[2,8,16,256]{3,2,1,0:T(8,128)} %dual_ref.3) | copy-start | bytes 786436
  91.2 46.7 %copy-start.23 = (f32[2]{0:T(128)S(1)}, f32[2]{0:T(128)}, u32[]{:S(2)}) copy-start(f32[2]{0:T(128)} %constant.67.clone) | copy-start | bytes 28

commit v7 on v6

--- a/solution.py
+++ b/solution.py
@@ -844,7 +844,7 @@
     packed, residual = lax.optimization_barrier((packed, residual))
     received = exchange(packed, "row")
 
-    grams = in_hbm(gram_tables(late_sampling.astype(F32)[:, None, :], table))
+    grams = gram_tables(late_sampling.astype(F32)[:, None, :], table)
     maps, frames_cols, splits, first, last = receive(image)
     frames_before, frames_after = shift(last, 1), shift(first, -1)
     residual = in_hbm(start(grams, maps, frames_cols, splits, residual))

time: 139 us -> 141 us (1.014)
  waiting for transfers between devices: 13.4 us -> 18.5 us
  local copies, waits for them, and re-layouts: 9.59 us -> 5.57 us
  Pallas kernels: 38.2 us -> 36.2 us
  starting transfers between devices: 25.2 us -> 27.1 us
    all_to_all x2, waiting for transfers between devices: 13.4 us -> 18.5 us  [exchange(): return lax.all_to_all(value, axes, 0, 0, tiled=True)]
    unnamed x42 -> x34, local copies, waits for them, and re-layouts: 7.63 us -> 4.5 us
  transfers between devices with their start and end apart: 7 -> 7, of which waited for: 2 -> 2; matrix products, arithmetic and copies ran while one was open for 5% -> 4% of each run, Pallas kernels for 19% -> 17%
where the time goes in v7:
time: 141 us; the launch traced here: 140 us
  blocking collectives  46.1 us (33%)
  Pallas kernels  36.2 us (26%)
  starting transfers between devices  27.1 us (19%)
  waiting for transfers between devices  18.5 us (13%)
  local copies, waits for them, and re-layouts  5.57 us (4%)
  other arithmetic  4.99 us (4%)
  between operations  1.6 us (1%)
    all_to_all x3, blocking collectives, exchange(): return lax.all_to_all(value, axes, 0, 0, tiled=True)  46.1 us
    all_to_all x2, waiting for transfers between devices, exchange(): return lax.all_to_all(value, axes, 0, 0, tiled=True)  18.5 us
    ppermute x5, starting transfers between devices, shift(): return lax.ppermute(value, 'phase', pairs)  15 us
    all_to_all x2, starting transfers between devices, exchange(): return lax.all_to_all(value, axes, 0, 0, tiled=True)  12.1 us
    pallas_call x1, Pallas kernels, adjoint(): pl.pallas_call(functools.partial(adjoint_kernel, len(edges)), grid_spec=p...  6.7 us
    pallas_call x1, Pallas kernels, pack_measured(): pl.pallas_call(functools.partial(pack_measured_kernel, base), grid=(PACK_...  5.82 us
    pallas_call x1, Pallas kernels, start(): pl.pallas_call(start_kernel, grid=(2,), in_specs=[GRAM_SPEC] + [IN_VMEM]...  4.88 us
    unnamed x34, local copies, waits for them, and re-layouts  4.5 us
  transfers between devices with their start and end apart: 7, of which 2 were waited for; matrix products, arithmetic and copies ran while one was open for 4% of the time, Pallas kernels for 17%

profile of v7, /device:TPU:1, one launch (start us, length us, event | category | flops | bytes accessed | tf_op | source)
XLA Modules:
  0.0 140.0 jit_solution(3770190002558599829)
XLA Ops:
  0.6 0.0 copy-start.18
  0.6 0.0 copy-start.16
  0.7 2.8 %pack_image.1 = f32[16,64,256]{2,1,0:T(8,128)} custom-call(f32[16,2,16,256]{3,2,1,0:T(8,128)} %maps_ref.1, f32[2,8,16,256]{3,2,1,0:T(8,128)} %frames_ref.1, f32[2,8,16,256]{3,2,1,0:T(8,128)} %aux_ref.3, f32[2,8,16,256]{3,2,1,0:T(8,128)} %dual_ref.3), custom_call_target="tpu_custom_call" | custom-call | tf_op jit(solution)/shard_map/pack_image/pallas_call | solution.py:276
  3.5 6.8 %all-to-all-start.1 = ((f32[16,64,256]{2,1,0:T(8,128)}), f32[16,64,256]{2,1,0:T(8,128)}, u32[]{:S(2)}, u32[]{:S(2)}) async-start(f32[16,64,256]{2,1,0:T(8,128)} %pack_image.1), calls=%async_computation.1 | async-start | bytes 2097152 | tf_op jit(solution)/shard_map/all_to_all | solution.py:799
  10.3 0.0 copy-done.16
  10.3 0.1 dynamic-slice_convert_fusion
  10.4 0.6 reshape.144.weight_ref
  10.9 0.1 constant_dynamic-slice_fusion
  11.0 0.1 broadcast_in_dim.49
  11.1 0.1 broadcast_in_dim.50.turn_ref
  11.2 5.8 %pack_measured_0.1 = (f32[16,176,256]{2,1,0:T(8,128)S(1)}, f32[2,256,128]{2,1,0:T(8,128)}) custom-call(f32[1,128]{1,0:T(1,128)} %reshape.144.weight_ref, f32[2,128,128]{2,1,0:T(8,128)S(1)} %broadcast_in_dim.50.turn_ref, f32[16,2,128,256]{3,2,1,0:T(8,128)} %bitcast.4), custom_call_target="tpu_custom_call" | custom-call | tf_op jit(solution)/shard_map/pack_measured_0/pallas_call | solution.py:301
  17.0 1.6 %copy-done.5 = f32[16,176,256]{2,1,0:T(8,128)} copy-done((f32[16,176,256]{2,1,0:T(8,128)}, f32[16,176,256]{2,1,0:T(8,128)S(1)}, u32[]{:S(2)}) %copy-start.5) | copy-done | bytes 2883608
  18.6 0.1 reshape.145
  18.7 0.2 reduce_sum.36
  18.9 1.4 reduce_window_sum.22
  20.3 0.1 copy.30
  20.4 0.7 fusion.4
  21.1 0.1 copy.29
  21.9 4.2 %all-to-all-done.1.image_ref = f32[16,64,256]{2,1,0:T(8,128)} async-done(((f32[16,64,256]{2,1,0:T(8,128)}), f32[16,64,256]{2,1,0:T(8,128)}, u32[]{:S(2)}, u32[]{:S(2)}) %all-to-all-start.1) | async-done | bytes 1048608 | tf_op jit(solution)/shard_map/all_to_all | solution.py:799
  26.1 0.0 copy-done.12
  26.1 0.0 copy-start.17
  26.1 5.2 %all-to-all-start.2 = ((f32[16,176,256]{2,1,0:T(8,128)}), f32[16,176,256]{2,1,0:T(8,128)}, u32[]{:S(2)}, u32[]{:S(2)}) async-start(f32[16,176,256]{2,1,0:T(8,128)} %copy-done.5), calls=%async_computation.2 | async-start | bytes 5767168 | tf_op jit(solution)/shard_map/all_to_all | solution.py:799
  31.4 0.2 fusion.3
  31.6 0.1 add_add_fusion.1
  31.7 0.1 iota_add_fusion.1
  31.8 1.5 %select_reduce_fusion.1 = s32[8,16,16]{2,1,0:T(8,128)S(1)} fusion(s32[16,16]{1,0:T(8,128)S(1)} %add_add_fusion.1, s32[8,16,16]{2,1,0:T(8,128)S(1)} %get-tuple-element.203, s32[8,16,16]{2,1,0:T(8,128)S(1)} %get-tuple-element.204, pred[8,16,16]{2,1,0:T(8,128)(4,1)S(1)} %get-tuple-element.202, pred[8,16,16]{2,1,0:T(8,128)(4,1)S(1)} %get-tuple-element.201, ...), kind=kLoop, calls=%fused_computation.11 | loop fusion | flops 194560 | bytes 31744 | tf_op jit(solution)/shard_map/reduce_sum | solution.py:810
  33.3 2.1 %receive.2 = (f32[2,256,256]{2,1,0:T(8,128)S(1)}, f32[2,256,128]{2,1,0:T(8,128)S(1)}, f32[2,256,128]{2,1,0:T(8,128)S(1)}, f32[2,32,128]{2,1,0:T(8,128)}, f32[2,32,128]{2,1,0:T(8,128)S(1)}) custom-call(f32[16,64,256]{2,1,0:T(8,128)} %all-to-all-done.1.image_ref), custom_call_target="tpu_custom_call" | custom-call | tf_op jit(solution)/shard_map/receive/pallas_call | solution.py:368
  35.4 0.7 copy-done.10
  36.1 6.1 %collective-permute-start.1 = (f32[2,32,128]{2,1,0:T(8,128)}, f32[2,32,128]{2,1,0:T(8,128)S(1)}, u32[]{:S(2)}, u32[]{:S(2)}) collective-permute-start(f32[2,32,128]{2,1,0:T(8,128)} %get-tuple-element.92), channel_id=1, source_target_pairs={{0,112},{16,0},{32,16},{48,32},{64,48},{80,64},{96,80},{112,96},{1... | collective-permute-start | bytes 98312 | tf_op jit(solution)/shard_map/ppermute | solution.py:795
  42.2 0.0 collective-permute-start
  42.2 0.1 reshape.146.window_ref
  42.3 0.1 sub.49.index_ref
  42.4 0.0 copy-done.6
  42.4 0.0 copy-start.11
  42.4 2.3 %gram_tables.1.gram_ref = bf16[8,2,256,256]{3,2,1,0:T(8,128)(2,1)S(1)} custom-call(f32[8,1,256]{2,1,0:T(1,128)S(1)} %broadcast_in_dim.53.weight_ref, bf16[4,256,256]{2,1,0:T(8,128)(2,1)S(1)} %copy-done.6), custom_call_target="tpu_custom_call" | custom-call | tf_op jit(solution)/shard_map/gram_tables/pallas_call | solution.py:387
  44.7 1.9 %line_tables.2.tables_ref = bf16[8,2,256,256]{3,2,1,0:T(8,128)(2,1)S(1)} custom-call(s32[8,1,256]{2,1,0:T(1,128)S(1)} %sub.49.index_ref, bf16[4,256,256]{2,1,0:T(8,128)(2,1)S(1)} %copy-done.6), custom_call_target="tpu_custom_call" | custom-call | tf_op jit(solution)/shard_map/line_tables/pallas_call | solution.py:325
  46.6 0.0 copy-start.4
  46.6 1.3 copy-done.4
  47.9 4.9 %start.1.in_ref = f32[2,256,128]{2,1,0:T(8,128)S(1)} custom-call(bf16[8,2,256,256]{3,2,1,0:T(8,128)(2,1)S(1)} %gram_tables.1.gram_ref, f32[2,256,256]{2,1,0:T(8,128)S(1)} %get-tuple-element.83.maps_ref, f32[2,256,128]{2,1,0:T(8,128)S(1)} %get-tuple-element.88.frames_ref, f32[2,256,128]{2,1,0:T(8,128)S(1)} %copy-done.11, f32[2,256,128]{2,1,0:T(8,128)} %get-tuple-element.90.in_ref), custom_call_target="tpu_custom_call" | custom-call | tf_op jit(solution)/shard_map/start/pallas_call | solution.py:445
  52.8 0.0 copy-start.7
  52.8 0.7 copy-done.7
  53.5 0.0 collective-permute-done.1.refs_1_.frames_after_ref
  53.5 0.0 collective-permute-done.refs_0_
  53.5 14.2 %all-to-all-done.2.lines_ref = f32[16,176,256]{2,1,0:T(8,128)} async-done(((f32[16,176,256]{2,1,0:T(8,128)}), f32[16,176,256]{2,1,0:T(8,128)}, u32[]{:S(2)}, u32[]{:S(2)}) %all-to-all-start.2) | async-done | bytes 2883616 | tf_op jit(solution)/shard_map/all_to_all | solution.py:799
  67.7 6.7 %adjoint.2 = (f32[2,256,128]{2,1,0:T(8,128)S(1)}, f32[2,32,128]{2,1,0:T(8,128)S(1)}, f32[2,32,128]{2,1,0:T(8,128)S(1)}) custom-call(s32[128]{0:T(128)S(1)} %reshape.146.window_ref, bf16[8,2,256,256]{3,2,1,0:T(8,128)(2,1)} %copy-done.4, f32[2,256,256]{2,1,0:T(8,128)S(1)} %get-tuple-element.83.maps_ref, f32[16,176,256]{2,1,0:T(8,128)} %all-to-all-done.2.lines_ref, ...), custom_call_target="tpu_custom_call" | custom-call | tf_op jit(solution)/shard_map/adjoint/pallas_call | solution.py:510
  74.4 1.7 %collective-permute-start.2 = (f32[2,32,128]{2,1,0:T(8,128)S(1)}, f32[2,32,128]{2,1,0:T(8,128)S(1)}, u32[]{:S(2)}, u32[]{:S(2)}) collective-permute-start(f32[2,32,128]{2,1,0:T(8,128)S(1)} %get-tuple-element.94), channel_id=1, source_target_pairs={{0,16},{16,32},{32,48},{48,64},{64,80},{80,96},{96,112},{112,0},{1... | collective-permute-start | bytes 98312 | tf_op jit(solution)/shard_map/ppermute | solution.py:795
  76.2 4.5 %collective-permute-start.3 = (f32[2,32,128]{2,1,0:T(8,128)S(1)}, f32[2,32,128]{2,1,0:T(8,128)S(1)}, u32[]{:S(2)}, u32[]{:S(2)}) collective-permute-start(f32[2,32,128]{2,1,0:T(8,128)S(1)} %get-tuple-element.95), channel_id=1, source_target_pairs={{0,112},{16,0},{32,16},{48,32},{64,48},{80,64},{96,80},{112,96},{1... | collective-permute-start | bytes 98312 | tf_op jit(solution)/shard_map/ppermute | solution.py:795
  80.7 3.7 %gram_apply.1.gram_ref = f32[2,256,128]{2,1,0:T(8,128)S(1)} custom-call(bf16[8,2,256,256]{3,2,1,0:T(8,128)(2,1)S(1)} %gram_tables.1.gram_ref, f32[2,256,256]{2,1,0:T(8,128)S(1)} %get-tuple-element.83.maps_ref, f32[2,256,128]{2,1,0:T(8,128)S(1)} %get-tuple-element.93.in_ref.first_ref.residual_ref), custom_call_target="tpu_custom_call" | custom-call | tf_op jit(solution)/shard_map/gram_apply/pallas_call | solution.py:539
  84.4 0.0 collective-permute-done.2.before_ref
  84.4 0.0 collective-permute-done.3.after_ref.residual_after_ref
  84.4 1.3 normal.1
  85.8 2.7 %collective-permute-start.4 = (f32[2,32,128]{2,1,0:T(8,128)S(1)}, f32[2,32,128]{2,1,0:T(8,128)S(1)}, u32[]{:S(2)}, u32[]{:S(2)}) collective-permute-start(f32[2,32,128]{2,1,0:T(8,128)S(1)} %get-tuple-element.99), channel_id=1, source_target_pairs={{0,112},{16,0},{32,16},{48,32},{64,48},{80,64},{96,80},{112,96},{1... | collective-permute-start | bytes 98312 | tf_op jit(solution)/shard_map/ppermute | solution.py:795
  88.5 3.1 %curvature.1.curve_ref = f32[8,128]{1,0:T(8,128)S(1)} custom-call(bf16[8,2,256,256]{3,2,1,0:T(8,128)(2,1)S(1)} %gram_tables.1.gram_ref, f32[2,256,256]{2,1,0:T(8,128)S(1)} %get-tuple-element.83.maps_ref, f32[2,256,128]{2,1,0:T(8,128)S(1)} %get-tuple-element.97.in_ref.product_ref), custom_call_target="tpu_custom_call" | custom-call | tf_op jit(solution)/shard_map/curvature/pallas_call | solution.py:627
  91.5 0.0 copy-start.19
  91.5 0.0 collective-permute-done.4.after_ref.product_after_ref
  91.5 0.1 share.1
  91.7 21.1 %all_to_all.32.shared_ref = f32[128,1,128]{2,1,0:T(1,128)S(1)} all-to-all(f32[128,1,128]{2,1,0:T(1,128)S(1)} %share.1), channel_id=1, replica_groups=mesh['phase'=8,'row'=16] {'phase','row'}, dimensions={0} | all-to-all | bytes 131072 | tf_op jit(solution)/shard_map/all_to_all | solution.py:799
  112.8 0.4 solve.1
  113.2 11.3 %all_to_all.33.in_ref = f32[16,40,128]{2,1,0:T(8,128)S(1)} all-to-all(f32[16,40,128]{2,1,0:T(8,128)S(1)} %solve.1), channel_id=1, replica_groups=mesh['phase'=8,'row'=16] {'row'}, dimensions={0} | all-to-all | bytes 655360 | tf_op jit(solution)/shard_map/all_to_all | solution.py:799
  124.5 1.2 finish.1
  125.6 13.7 %all_to_all.34 = f32[128,1,128]{2,1,0:T(1,128)S(1)} all-to-all(f32[128,1,128]{2,1,0:T(1,128)S(1)} %get-tuple-element.103), channel_id=1, replica_groups=mesh['phase'=8,'row'=16] {'phase','row'}, dimensions={0} | all-to-all | bytes 131072 | tf_op jit(solution)/shard_map/all_to_all | solution.py:799
  139.3 0.2 slice_reduce_fusion
  139.5 0.0 copy-done.19
  139.5 0.5 sqrt_multiply_fusion
  (25 shorter events, 0.1 us)
Async XLA Ops:
  0.6 10.3 %copy-start.18 = (f32[2,256]{1,0:T(2,128)S(1)}, f32[2,256]{1,0:T(2,128)}, u32[]{:S(2)}) copy-start(f32[2,256]{1,0:T(2,128)} %constant.66.clone) | copy-start | bytes 6148
  0.6 9.6 %copy-start.16 = (s32[8,256]{1,0:T(8,128)S(1)}, s32[8,256]{1,0:T(8,128)}, u32[]{:S(2)}) copy-start(s32[8,256]{1,0:T(8,128)} %param.16) | copy-start | bytes 24580
  3.5 22.6 %all-to-all-start.1 = ((f32[16,64,256]{2,1,0:T(8,128)}), f32[16,64,256]{2,1,0:T(8,128)}, u32[]{:S(2)}, u32[]{:S(2)}) async-start(f32[16,64,256]{2,1,0:T(8,128)} %pack_image.1), calls=%async_computation.1 | async-start | bytes 2097152 | tf_op jit(solution)/shard_map/all_to_all | solution.py:799
  17.0 1.6 %copy-start.5 = (f32[16,176,256]{2,1,0:T(8,128)}, f32[16,176,256]{2,1,0:T(8,128)S(1)}, u32[]{:S(2)}) copy-start(f32[16,176,256]{2,1,0:T(8,128)S(1)} %get-tuple-element.87) | copy-start | bytes 8650756
  18.7 7.4 %copy-start.12 = (s32[8,16,16]{2,1,0:T(8,128)}, s32[8,16,16]{2,1,0:T(8,128)S(1)}, u32[]{:S(2)}) copy-start(s32[8,16,16]{2,1,0:T(8,128)S(1)} %reshape.145) | copy-start | bytes 24580
  21.1 5.0 %copy-start.14 = (s32[8,16,16]{2,1,0:T(8,128)}, s32[8,16,16]{2,1,0:T(8,128)S(1)}, u32[]{:S(2)}) copy-start(s32[8,16,16]{2,1,0:T(8,128)S(1)} %get-tuple-element.197) | copy-start | bytes 24580
  26.1 5.3 %copy-start.13 = (s32[8,16,16]{2,1,0:T(8,128)S(1)}, s32[8,16,16]{2,1,0:T(8,128)}, u32[]{:S(2)}) copy-start(s32[8,16,16]{2,1,0:T(8,128)} %copy-done.12) | copy-start | bytes 24580
  26.1 5.3 %copy-start.15 = (s32[8,16,16]{2,1,0:T(8,128)S(1)}, s32[8,16,16]{2,1,0:T(8,128)}, u32[]{:S(2)}) copy-start(s32[8,16,16]{2,1,0:T(8,128)} %copy-done.14) | copy-start | bytes 24580
  26.1 16.1 %copy-start.17 = (s32[8,256]{1,0:T(8,128)S(1)}, s32[8,256]{1,0:T(8,128)}, u32[]{:S(2)}) copy-start(s32[8,256]{1,0:T(8,128)} %param.16) | copy-start | bytes 24580
  26.1 41.6 %all-to-all-start.2 = ((f32[16,176,256]{2,1,0:T(8,128)}), f32[16,176,256]{2,1,0:T(8,128)}, u32[]{:S(2)}, u32[]{:S(2)}) async-start(f32[16,176,256]{2,1,0:T(8,128)} %copy-done.5), calls=%async_computation.2 | async-start | bytes 5767168 | tf_op jit(solution)/shard_map/all_to_all | solution.py:799
  31.4 11.1 %copy-start.6 = (bf16[4,256,256]{2,1,0:T(8,128)(2,1)S(1)}, bf16[4,256,256]{2,1,0:T(8,128)(2,1)}, u32[]{:S(2)}) copy-start(bf16[4,256,256]{2,1,0:T(8,128)(2,1)} %constant.65.clone.tables_ref) | copy-start | bytes 1572868
  35.4 0.7 copy-start.10
  36.1 17.4 %collective-permute-start.1 = (f32[2,32,128]{2,1,0:T(8,128)}, f32[2,32,128]{2,1,0:T(8,128)S(1)}, u32[]{:S(2)}, u32[]{:S(2)}) collective-permute-start(f32[2,32,128]{2,1,0:T(8,128)} %get-tuple-element.92), channel_id=1, source_target_pairs={{0,112},{16,0},{32,16},{48,32},{64,48},{80,64},{96,80},{112,96},{1... | collective-permute-start | bytes 98312 | tf_op jit(solution)/shard_map/ppermute | solution.py:795
  42.2 11.3 %collective-permute-start = (f32[2,32,128]{2,1,0:T(8,128)S(1)}, f32[2,32,128]{2,1,0:T(8,128)S(1)}, u32[]{:S(2)}, u32[]{:S(2)}) collective-permute-start(f32[2,32,128]{2,1,0:T(8,128)S(1)} %get-tuple-element.91), channel_id=1, source_target_pairs={{0,16},{16,32},{32,48},{48,64},{64,80},{80,96},{96,112},{112,0},{1... | collective-permute-start | bytes 98312 | tf_op jit(solution)/shard_map/ppermute | solution.py:795
  42.4 5.5 %copy-start.11 = (f32[2,256,128]{2,1,0:T(8,128)S(1)}, f32[2,256,128]{2,1,0:T(8,128)}, u32[]{:S(2)}) copy-start(f32[2,256,128]{2,1,0:T(8,128)} %copy-done.10) | copy-start | bytes 786436
  46.6 1.3 copy-start.4
  52.8 0.7 copy-start.7
  74.4 10.0 %collective-permute-start.2 = (f32[2,32,128]{2,1,0:T(8,128)S(1)}, f32[2,32,128]{2,1,0:T(8,128)S(1)}, u32[]{:S(2)}, u32[]{:S(2)}) collective-permute-start(f32[2,32,128]{2,1,0:T(8,128)S(1)} %get-tuple-element.94), channel_id=1, source_target_pairs={{0,16},{16,32},{32,48},{48,64},{64,80},{80,96},{96,112},{112,0},{1... | collective-permute-start | bytes 98312 | tf_op jit(solution)/shard_map/ppermute | solution.py:795
  76.2 8.3 %collective-permute-start.3 = (f32[2,32,128]{2,1,0:T(8,128)S(1)}, f32[2,32,128]{2,1,0:T(8,128)S(1)}, u32[]{:S(2)}, u32[]{:S(2)}) collective-permute-start(f32[2,32,128]{2,1,0:T(8,128)S(1)} %get-tuple-element.95), channel_id=1, source_target_pairs={{0,112},{16,0},{32,16},{48,32},{64,48},{80,64},{96,80},{112,96},{1... | collective-permute-start | bytes 98312 | tf_op jit(solution)/shard_map/ppermute | solution.py:795
  85.8 5.8 %collective-permute-start.4 = (f32[2,32,128]{2,1,0:T(8,128)S(1)}, f32[2,32,128]{2,1,0:T(8,128)S(1)}, u32[]{:S(2)}, u32[]{:S(2)}) collective-permute-start(f32[2,32,128]{2,1,0:T(8,128)S(1)} %get-tuple-element.99), channel_id=1, source_target_pairs={{0,112},{16,0},{32,16},{48,32},{64,48},{80,64},{96,80},{112,96},{1... | collective-permute-start | bytes 98312 | tf_op jit(solution)/shard_map/ppermute | solution.py:795
  88.5 36.0 %copy-start.8 = (f32[2,8,16,256]{3,2,1,0:T(8,128)S(1)}, f32[2,8,16,256]{3,2,1,0:T(8,128)}, u32[]{:S(2)}) copy-start(f32[2,8,16,256]{3,2,1,0:T(8,128)} %aux_ref.3) | copy-start | bytes 786436
  88.5 36.0 %copy-start.9 = (f32[2,8,16,256]{3,2,1,0:T(8,128)S(1)}, f32[2,8,16,256]{3,2,1,0:T(8,128)}, u32[]{:S(2)}) copy-start(f32[2,8,16,256]{3,2,1,0:T(8,128)} %dual_ref.3) | copy-start | bytes 786436
  91.5 48.0 %copy-start.19 = (f32[2]{0:T(128)S(1)}, f32[2]{0:T(128)}, u32[]{:S(2)}) copy-start(f32[2]{0:T(128)} %constant.67.clone) | copy-start | bytes 28
